TPU v7x, 32 devices: a whole 2x2x4 slice. The times are simulated.
32 devices in a mesh: inv: 2 (over y), test: 2 (over core), tx: 4 (over z), ty: 2 (over x).
Axes of the slice: x: 2, y: 2, z: 4, core: 2. Of those that a mesh axis runs over, the one named last changes fastest.
Arguments:
- log_cond: float32 [2560, 512], P(('inv', 'tx'), 'ty'), parts along dimension 0, may hold values from -3.5 to -1.7
- log_shape: float32 [2560, 512], P(('inv', 'tx'), 'ty'), parts along dimension 0, may hold values from -2.8 to -1.6
- zone_ids: int32 [2560, 512], P(('inv', 'tx'), 'ty'), parts along dimension 0, may hold values from 0 to 7
- storage: float32 [4, 8], P('inv'), parts along dimension 0, may hold values from 0.9 to 1.2
- pump_x: int32 [4, 1], P(('inv', 'test')), parts along dimension 0, may hold values from 0 to 1279
- pump_y: int32 [4, 1], P(('inv', 'test')), parts along dimension 0, may hold values from 0 to 511
- pump_rates: float32 [4, 3, 1], P(('inv', 'test')), parts along dimension 0, may hold values from -4 to -1
- obs_x: int32 [128], P('inv'), parts along dimension 0, may hold values from 0 to 1279
- obs_y: int32 [128], P('inv'), parts along dimension 0, may hold values from 0 to 511
- observed: float32 [4, 3, 64], P(('inv', 'test')), parts along dimension 0, may hold values from -6 to 6
- frac_start: float32 [4, 1280, 512], P(('inv', 'test'), 'tx', 'ty'), parts along dimension 0, may hold values from -6 to 6
- matrix_start: float32 [4, 1280, 512], P(('inv', 'test'), 'tx', 'ty'), parts along dimension 0, may hold values from -6 to 6
- frac_end: float32 [4, 1280, 512], P(('inv', 'test'), 'tx', 'ty'), parts along dimension 0, may hold values from -6 to 6
- matrix_end: float32 [4, 1280, 512], P(('inv', 'test'), 'tx', 'ty'), parts along dimension 0, may hold values from -6 to 6
Outputs:
- cond_direction: float32 [2560, 512], P(('inv', 'tx'), 'ty'), parts along dimension 0
- shape_direction: float32 [2560, 512], P(('inv', 'tx'), 'ty'), parts along dimension 0
- frac_adjoint: float32 [4, 1280, 512], P(('inv', 'test'), 'tx', 'ty'), parts along dimension 0
- matrix_adjoint: float32 [4, 1280, 512], P(('inv', 'test'), 'tx', 'ty'), parts along dimension 0
There are 2 independent parts, one for each index of `inv`. A program takes and returns all parts, laid end to end along the dimension named above; each array names one. Nothing has to cross between parts.
All inputs are finite; a program needn't handle non-finite values.
Results may differ from a plain program's by a relative error of at most 0.0001.
Values sent between devices are 32-bit elements; how exact they have to be, the bound alone decides.
No kernel may reach another device: no remote copies, remote signals or barrier semaphores. Data moves between devices by JAX's collectives and lax.ppermute only.
A program may use at most 64 MiB of HBM per device.

v0:
```python
import jax
import jax.numpy as jnp
from jax import lax
from jax.sharding import PartitionSpec as P

SMOOTH = 2


blend_rate = 0.2


def padded_2(cells, sides, width):
    for axis, dim in sides:
        count = lax.axis_size(axis)
        ends = count - 1
        head = lax.slice_in_dim(cells, 0, width, axis=dim)
        tail = lax.slice_in_dim(cells, cells.shape[dim] - width, cells.shape[dim], axis=dim)
        cells = jnp.concatenate(
            [
                lax.ppermute(tail, axis, [(i, (i + 1) % count) for i in range(ends)]),
                cells,
                lax.ppermute(head, axis, [((i + 1) % count, i) for i in range(ends)]),
            ],
            axis=dim,
        )
    return cells


def neighbours(padded):
    return (
        padded[..., :-2, 1:-1],
        padded[..., 2:, 1:-1],
        padded[..., 1:-1, :-2],
        padded[..., 1:-1, 2:],
    )


def flow_sum(padded, conductances):
    centre = padded[..., 1:-1, 1:-1]
    summed = jnp.zeros_like(centre)
    for conductance, beside in zip(conductances, neighbours(padded)):
        summed = summed + conductance * (beside - centre)
    return summed


def zero_border(field):
    return jnp.pad(field, [(0, 0)] * (field.ndim - 2) + [(1, 1), (1, 1)])


def local_spots(coord_x, coord_y, tile_rows, tile_cols, margin):
    local_x = coord_x - lax.axis_index("tx") * tile_rows + margin
    local_y = coord_y - lax.axis_index("ty") * tile_cols + margin
    extent_x = tile_rows + 2 * margin
    extent_y = tile_cols + 2 * margin
    inside = (local_x >= 0) & (local_x < extent_x) & (local_y >= 0) & (local_y < extent_y)
    return (jnp.clip(local_x, 0, extent_x - 1), jnp.clip(local_y, 0, extent_y - 1), inside)


def smooth(grad_field):
    for sweep_index in range(SMOOTH):
        padded = padded_2(grad_field, (("tx", 1), ("ty", 2)), 1)
        nearby = neighbours(padded)
        grad_field = grad_field + blend_rate * (
            nearby[0] + nearby[1] + nearby[2] + nearby[3] - 4.0 * grad_field
        )
    return grad_field


def margin_window(
    cond,
    shape_factor,
    store_frac,
    store_matrix,
    pump_x,
    pump_y,
    pump_rates,
    obs_x,
    obs_y,
    observed,
    frac_start,
    matrix_start,
    frac_end,
    matrix_end,
):
    tile_rows, tile_cols = cond.shape
    test_count = frac_start.shape[0]
    step_count = pump_rates.shape[1]
    margin = 2 * step_count
    packed = jnp.concatenate(
        [
            cond[None],
            shape_factor[None],
            store_frac[None],
            store_matrix[None],
            frac_start,
            matrix_start,
            frac_end,
            matrix_end,
        ],
        0,
    )
    widened = padded_2(packed, (("tx", 1), ("ty", 2)), margin)
    place_x = lax.axis_index("tx") * tile_rows - margin + jnp.arange(tile_rows + 2 * margin)
    place_y = lax.axis_index("ty") * tile_cols - margin + jnp.arange(tile_cols + 2 * margin)
    within = ((place_x >= 0) & (place_x < tile_rows * lax.axis_size("tx")))[:, None] & (
        (place_y >= 0) & (place_y < tile_cols * lax.axis_size("ty"))
    )[None, :]
    cond_wide = widened[0]
    shape_wide = widened[1]
    sfrac_wide = jnp.where(within, widened[2], 1.0)
    smatrix_wide = jnp.where(within, widened[3], 1.0)
    fracture = widened[4 : 4 + test_count]
    matrix = widened[4 + test_count : 4 + 2 * test_count]
    end_frac = widened[4 + 2 * test_count : 4 + 3 * test_count]
    end_matrix = widened[4 + 3 * test_count : 4 + 4 * test_count]
    cond_nearby = neighbours(zero_border(cond_wide))
    conductances = []
    slopes = []
    for beside in cond_nearby:
        total = cond_wide + beside
        safe_total = jnp.where(total > 0.0, total, 1.0)
        conductances.append(2.0 * cond_wide * beside / safe_total)
        slopes.append(2.0 * beside * beside / (safe_total * safe_total))
    spot_x, spot_y, spot_in = local_spots(pump_x, pump_y, tile_rows, tile_cols, margin)
    test_rows = jnp.arange(test_count)[:, None]
    obs_lx, obs_ly, obs_in = local_spots(obs_x, obs_y, tile_rows, tile_cols, margin)
    stored = []
    mismatches = []
    for step_index in range(step_count):
        stored.append((fracture, matrix))
        transfer = shape_wide * (fracture - matrix)
        source = (
            jnp.zeros_like(fracture)
            .at[test_rows, spot_x, spot_y]
            .add(jnp.where(spot_in, pump_rates[:, step_index], 0.0))
        )
        fracture_next = (
            fracture
            + (flow_sum(zero_border(fracture), conductances) - transfer + source) / sfrac_wide
        )
        matrix = matrix + transfer / smatrix_wide
        fracture = fracture_next
        mismatches.append(
            jnp.where(obs_in[None], fracture[:, obs_lx, obs_ly] - observed[:, step_index], 0.0)
        )

    def inject(adjoint_field, mismatch):
        return adjoint_field.at[:, obs_lx, obs_ly].add(mismatch)

    def interior(field):
        return field[..., margin : margin + tile_rows, margin : margin + tile_cols]

    fracture_adj = inject(end_frac, mismatches[step_count - 1])
    matrix_adj = end_matrix
    grad_cond = jnp.zeros((tile_rows, tile_cols), jnp.float32)
    grad_shape = jnp.zeros((tile_rows, tile_cols), jnp.float32)
    for step_index in reversed(range(step_count)):
        fracture, matrix = stored[step_index]
        scaled = fracture_adj / sfrac_wide
        matrix_scaled = matrix_adj / smatrix_wide
        scaled_pad = zero_border(scaled)
        spread = flow_sum(scaled_pad, conductances)
        face_term = jnp.zeros_like(fracture)
        for slope, head_beside, adjoint_beside in zip(
            slopes, neighbours(zero_border(fracture)), neighbours(scaled_pad)
        ):
            face_term = face_term + slope * (head_beside - fracture) * (scaled - adjoint_beside)
        grad_cond = grad_cond + interior(cond_wide * jnp.sum(face_term, axis=0))
        swap_rate = shape_wide * (matrix_scaled - scaled)
        grad_shape = grad_shape + interior(jnp.sum(swap_rate * (fracture - matrix), axis=0))
        fracture_adj = fracture_adj + spread + swap_rate
        matrix_adj = matrix_adj - swap_rate
        if step_index > 0:
            fracture_adj = inject(fracture_adj, mismatches[step_index - 1])
    return (grad_cond, grad_shape, interior(fracture_adj), interior(matrix_adj))


def on_device(
    log_cond,
    log_shape,
    zone_ids,
    storage,
    pump_x,
    pump_y,
    pump_rates,
    obs_x,
    obs_y,
    observed,
    frac_start,
    matrix_start,
    frac_end,
    matrix_end,
):
    cond = jnp.exp(log_cond)
    shape_factor = jnp.exp(log_shape)
    store_frac = jnp.zeros_like(cond)
    store_matrix = jnp.zeros_like(cond)
    for zone_index in range(storage.shape[1]):
        chosen = zone_ids == zone_index
        store_frac = jnp.where(chosen, storage[0, zone_index], store_frac)
        store_matrix = jnp.where(chosen, storage[1, zone_index], store_matrix)
    grad_cond, grad_shape, fracture_adj, matrix_adj = margin_window(
        cond,
        shape_factor,
        store_frac,
        store_matrix,
        pump_x,
        pump_y,
        pump_rates,
        obs_x,
        obs_y,
        observed,
        frac_start,
        matrix_start,
        frac_end,
        matrix_end,
    )
    stacked = jnp.stack([grad_cond, grad_shape], 0)
    summed = lax.psum(stacked, "test")
    smoothed = smooth(summed)
    return (smoothed[0], smoothed[1], fracture_adj, matrix_adj)


def solution(mesh):
    placed = (
        P(("inv", "tx"), "ty"),
        P(("inv", "tx"), "ty"),
        P(("inv", "tx"), "ty"),
        P("inv", None),
        P(("inv", "test"), None),
        P(("inv", "test"), None),
        P(("inv", "test"), None, None),
        P("inv"),
        P("inv"),
        P(("inv", "test"), None, None),
        P(("inv", "test"), "tx", "ty"),
        P(("inv", "test"), "tx", "ty"),
        P(("inv", "test"), "tx", "ty"),
        P(("inv", "test"), "tx", "ty"),
    )
    return jax.shard_map(
        on_device,
        mesh=mesh,
        in_specs=placed,
        out_specs=(
            P(("inv", "tx"), "ty"),
            P(("inv", "tx"), "ty"),
            P(("inv", "test"), "tx", "ty"),
            P(("inv", "test"), "tx", "ty"),
        ),
        check_vma=False,
    )
```

profile of v0, /device:TPU:0, one launch (start us, length us, event | category | flops | bytes accessed | tf_op | source)
XLA Modules:
  0.0 218.2 jit_solution(2237124378234032437)
XLA Ops:
  7.2 2.0 fusion.52
  9.2 1.9 copy.72
  11.1 1.9 copy.73
  13.0 1.9 copy.74
  14.9 1.9 copy.82
  16.8 1.9 copy.83
  18.7 0.9 copy.84
  19.8 1.1 bitcast_dynamic-update-slice_fusion.3
  21.0 1.1 bitcast_dynamic-update-slice_fusion.2
  22.0 6.5 %bitcast_dynamic-update-slice_fusion.1 = (f32[8,320,256]{1,2,0:T(8,128)S(1)}, pred[320,256]{0,1:T(8,128)(4,1)S(1)}, pred[320,256]{0,1:T(8,128)(4,1)S(1)}, pred[3...) fusion(f32[8,320,256]{1,2,0:T(8,128)S(1)} %bitcast_dynamic-upda, ...), kind=kLoop, calls=%fused_computation.121 | loop fusion | flops 1310720 | bytes 1507360
  28.5 5.3 %bitcast_dynamic-update-slice_fusion = f32[8,320,256]{1,2,0:T(8,128)S(1)} fusion(f32[8,320,256]{1,2,0:T(8,128)S(1)} %get-tuple-element.72, pred[320,256]{0,1:T(8,128)(4,1)S(1)} %get-tuple-element.80, pred[320,256]{0,1:T(8,128)(4,1)S(1)} %get-tuple-element.79, pred[320,256]{0,1:T(8,128)(4,1)S(1)} %get-tuple-element.78, ...), kind=kLoop, calls=%fused_computation.120 | loop fusion | flops 655360 | bytes 1179680
  34.1 1.9 fusion.49
  36.0 1.5 copy.87
  37.6 1.3 collective-permute-start.1
  38.9 1.6 copy.86
  40.4 5.6 %collective-permute-start = (f32[8,6,256]{2,0,1:T(8,128)S(1)}, f32[8,6,256]{2,0,1:T(8,128)S(1)}, u32[]{:S(2)}, u32[]{:S(2)}) collective-permute-start(f32[8,6,256]{2,0,1:T(8,128)S(1)} %copy.86), channel_id=1, source_target_pairs={{0,2},{2,4},{4,6},{1,3},{3,5},{5,7},{8,10},{10,12},{12,14},{9,11},... | collective-permute-start | bytes 147464 | tf_op jit(solution)/shard_map/ppermute | solution.py:20
  52.8 1.4 copy.88
  54.1 1.3 copy.89
  55.5 1.1 pad_maximum_fusion.20
  56.6 3.8 %collective-permute-start.2 = (f32[8,332,6]{1,2,0:T(8,128)S(1)}, f32[8,332,6]{1,2,0:T(8,128)S(1)}, u32[]{:S(2)}, u32[]{:S(2)}) collective-permute-start(f32[8,332,6]{1,2,0:T(8,128)S(1)} %get-tuple-element.81), channel_id=1, source_target_pairs={{0,1},{2,3},{4,5},{6,7},{8,9},{10,11},{12,13},{14,15},{16,17},{18,... | collective-permute-start | bytes 191240 | tf_op jit(solution)/shard_map/ppermute | solution.py:20
  60.4 1.3 collective-permute-start.3
  62.6 4.3 %collective-permute-done.3 = f32[8,332,6]{1,2,0:T(8,128)S(1)} collective-permute-done((f32[8,332,6]{1,2,0:T(8,128)S(1)}, f32[8,332,6]{1,2,0:T(8,128)S(1)}, u32[]{:S(2)}, u32[]{:S(2)}) %collective-permute-start.3) | collective-permute-done | bytes 63776 | tf_op jit(solution)/shard_map/ppermute | solution.py:22
  66.9 3.2 %pad_maximum_fusion = f32[8,332,268]{1,2,0:T(8,128)S(1)} fusion(f32[8,332,6]{1,2,0:T(8,128)S(1)} %collective-permute-done.3, f32[8,6,256]{1,2,0:T(8,128)S(1)} %copy-done.17, f32[8,320,256]{1,2,0:T(8,128)} %copy-done, f32[8,6,256]{1,2,0:T(8,128)S(1)} %copy-done.16, f32[8,332,6]{1,2,0:T(8,128)S(1)} %collective-permute-done.2), kind=kLoop, calls=%fused_computation.6 | loop fusion | flops 2847232 | bytes 5694464 | tf_op jit(solution)/shard_map/concatenate | solution.py:18
  71.0 1.9 add_subtract_fusion.2
  75.0 1.4 add.283
  76.4 1.2 divide_add_fusion.2
  78.4 2.8 %add_subtract_fusion.1 = (f32[1,332,268]{1,2,0:T(8,128)S(1)}, f32[1,332,268]{1,2,0:T(8,128)}, f32[1,332,268]{1,2,0:T(8,128)}) fusion(f32[1,332,268]{1,2,0:T(8,128)} %get-tuple-element.71, f32[1,332,268]{1,2,0:T(8,128)} %get-tuple-element.70, f32[1,332,268]{1,2,0:T(8,128)} %get-tuple-element.69, f32[1,332,268]{1,2,0:T(8,128)} %get-tuple-element.68, ...), kind=kLoop, calls=%fused_computation.82 | loop fusion | flops 1779520 | bytes 4271448 | tf_op jit(solution)/shard_map/sub | solution.py:139
  82.5 2.0 add.294
  84.5 2.0 divide_add_fusion
  86.5 1.9 gather_fusion.2
  88.4 1.9 gather_fusion.1
  90.3 2.7 %multiply_subtract_fusion = f32[1,332,268]{1,2,0:T(8,128)S(1)} fusion(f32[1,332,268]{1,2,0:T(8,128)} %get-tuple-element.71, f32[1,332,268]{1,2,0:T(8,128)} %get-tuple-element.70, f32[1,332,268]{1,2,0:T(8,128)} %get-tuple-element.69, f32[1,332,268]{1,2,0:T(8,128)} %get-tuple-element.68, f32[8,332,268]{1,2,0:T(8,128)S(1)} %pad_maximum_fusion, ...), kind=kLoop, calls=%fused_computation.74 | loop fusion | flops 1690544 | bytes 3559640 | tf_op jit(solution)/shard_map/sub | solution.py:139
  94.4 2.1 add.305
  96.4 2.2 add_bitcast_fusion.3
  98.6 1.9 gather_fusion
  100.5 9.0 %scatter_fusion = f32[332,268]{0,1:T(8,128)} fusion(f32[332,268]{0,1:T(8,128)} %get-tuple-element.84, s32[64]{0:T(128)S(1)} %get-tuple-element.110, f32[64]{0:T(128)S(1)} %get-tuple-element.108), kind=kCustom, calls=%fused_computation.3 | custom fusion | flops 64 | bytes 1280 | tf_op jit(solution)/shard_map/scatter-add | solution.py:148
  109.6 2.6 %multiply_bitcast_fusion.2 = (f32[332,268]{0,1:T(8,128)}, f32[1,332,268]{1,2,0:T(8,128)S(1)}, f32[1,332,268]{1,2,0:T(8,128)S(1)}) fusion(f32[1,332,268]{1,2,0:T(8,128)} %divide_add_fusion, f32[1,332,268]{1,2,0:T(8,128)} %get-tuple-element.66, f32[8,332,268]{1,2,0:T(8,128)S(1)} %pad_maximum_fusion, pred[268]{0:T(512)(128)(4,1)S(1)} %fusion.39, ...), kind=kLoop, calls=%fused_computation.67 | loop fusion | flops 1067712 | bytes 3915544 | tf_op jit(solution)/shard_map/reduce_sum | solution.py:170
  112.2 1.2 fusion.23
  113.4 9.1 %scatter_fusion.1 = f32[332,268]{0,1:T(8,128)} fusion(f32[332,268]{0,1:T(8,128)} %fusion.23, s32[64]{0:T(128)S(1)} %get-tuple-element.110, f32[64]{0:T(128)S(1)} %get-tuple-element.107), kind=kCustom, calls=%fused_computation.4 | custom fusion | flops 64 | bytes 1280 | tf_op jit(solution)/shard_map/scatter-add | solution.py:148
  122.5 2.4 %multiply_bitcast_fusion.1 = (f32[332,268]{0,1:T(8,128)}, f32[1,332,268]{1,2,0:T(8,128)S(1)}, f32[1,332,268]{1,2,0:T(8,128)S(1)}) fusion(f32[1,332,268]{1,2,0:T(8,128)} %get-tuple-element.65, f32[8,332,268]{1,2,0:T(8,128)S(1)} %pad_maximum_fusion, pred[268]{0:T(512)(128)(4,1)S(1)} %fusion.39, pred[332]{0:T(512)(128)(4,1)S(1)} %fusion.38, ...), kind=kLoop, calls=%fused_computation.66 | loop fusion | flops 800784 | bytes 3559640 | tf_op jit(solution)/shard_map/reduce_sum | solution.py:170
  125.0 1.2 fusion.21
  126.1 9.0 %scatter_fusion.2 = f32[332,268]{0,1:T(8,128)} fusion(f32[332,268]{0,1:T(8,128)} %fusion.21, s32[64]{0:T(128)S(1)} %get-tuple-element.110, f32[64]{0:T(128)S(1)} %get-tuple-element.62), kind=kCustom, calls=%fused_computation.5 | custom fusion | flops 64 | bytes 1280 | tf_op jit(solution)/shard_map/scatter-add | solution.py:148
  135.2 2.6 %multiply_bitcast_fusion = (f32[332,268]{0,1:T(8,128)S(1)}, f32[1,332,268]{1,2,0:T(8,128)}, f32[1,332,268]{1,2,0:T(8,128)}, f32[1,332,268]{1,2,0:T(8,128)S(1)}) fusion(f32[8,332,268]{1,2,0:T(8,128)S(1)} %pad_maximum_fusion, pred[268]{0:T(512)(128)(4,1)S(1)} %fusion.39, pred[332]{0:T(512)(128)(4,1)S(1)} %fusion.38, f32[1,332,268]{1,2,0:T(8,128)} %copy-done.26, ...), kind=kLoop, calls=%fused_computation.64 | loop fusion | flops 978736 | bytes 4627352 | tf_op jit(solution)/shard_map/reduce_sum | solution.py:170
  137.8 3.3 %fusion.32 = (f32[1,332,268]{1,2,0:T(8,128)S(1)}, f32[1,332,268]{1,2,0:T(8,128)S(1)}, f32[332,268]{0,1:T(8,128)S(1)}, f32[332,268]{0,1:T(8,128)S(1)}, f32[332,268]{0,1:T(8,128)S(1)}, /*index=5*/f32[1,332,268]{1,2,0:T(8,128)S(1)}) fusion(f32[1,332,268]{1,2,0:T(8,128)S(1)} %get-tuple-element.61, f32[1,332,268]{1,2,0:T(8,128)S(1)} %copy-done.32, ...), kind=kLoop, calls=%fused_computation.139 | loop fusion | flops 12723568 | bytes 4626752 | tf_op jit(solution)/shard_map/sub | solution.py:42
  141.1 0.9 fusion.28
  142.1 0.9 pad_maximum_fusion.17
  143.0 17.1 %all-reduce.9.cloned.1.call-done = f32[2,320,256]{1,2,0:T(8,128)} async-done(((f32[2,320,256]{1,2,0:T(8,128)}), f32[2,320,256]{1,2,0:T(8,128)}) %all-reduce.9.cloned.1.call-update) | async-done | bytes 655376 | tf_op jit(solution)/shard_map/psum | solution.py:219
  160.1 1.2 fusion.51
  161.2 3.7 %collective-permute-start.4 = (f32[2,1,256]{1,2,0:T(8,128)S(1)}, f32[2,1,256]{1,2,0:T(8,128)S(1)}, u32[]{:S(2)}, u32[]{:S(2)}) collective-permute-start(f32[2,1,256]{1,2,0:T(8,128)S(1)} %get-tuple-element.97), channel_id=1, source_target_pairs={{0,2},{2,4},{4,6},{1,3},{3,5},{5,7},{8,10},{10,12},{12,14},{9,11},... | collective-permute-start | bytes 6152 | tf_op jit(solution)/shard_map/ppermute | solution.py:20
  165.0 1.6 collective-permute-start.5
  166.6 4.3 %collective-permute-done.4 = f32[2,1,256]{1,2,0:T(8,128)S(1)} collective-permute-done((f32[2,1,256]{1,2,0:T(8,128)S(1)}, f32[2,1,256]{1,2,0:T(8,128)S(1)}, u32[]{:S(2)}, u32[]{:S(2)}) %collective-permute-start.4) | collective-permute-done | bytes 2080 | tf_op jit(solution)/shard_map/ppermute | solution.py:20
  170.9 4.5 %collective-permute-done.5 = f32[2,1,256]{1,2,0:T(8,128)S(1)} collective-permute-done((f32[2,1,256]{1,2,0:T(8,128)S(1)}, f32[2,1,256]{1,2,0:T(8,128)S(1)}, u32[]{:S(2)}, u32[]{:S(2)}) %collective-permute-start.5) | collective-permute-done | bytes 2080 | tf_op jit(solution)/shard_map/ppermute | solution.py:22
  176.2 3.4 %collective-permute-start.6 = (f32[2,322,1]{1,2,0:T(1,128)S(1)}, f32[2,322,1]{1,2,0:T(1,128)S(1)}, u32[]{:S(2)}, u32[]{:S(2)}) collective-permute-start(f32[2,322,1]{1,2,0:T(1,128)S(1)} %get-tuple-element.91), channel_id=1, source_target_pairs={{0,1},{2,3},{4,5},{6,7},{8,9},{10,11},{12,13},{14,15},{16,17},{18,... | collective-permute-start | bytes 7736 | tf_op jit(solution)/shard_map/ppermute | solution.py:20
  179.6 1.3 collective-permute-start.7
  180.9 4.2 %collective-permute-done.7 = f32[2,322,1]{1,2,0:T(1,128)S(1)} collective-permute-done((f32[2,322,1]{1,2,0:T(1,128)S(1)}, f32[2,322,1]{1,2,0:T(1,128)S(1)}, u32[]{:S(2)}, u32[]{:S(2)}) %collective-permute-start.7) | collective-permute-done | bytes 2608 | tf_op jit(solution)/shard_map/ppermute | solution.py:22
  185.1 3.5 %fusion.9 = f32[2,320,256]{1,2,0:T(8,128)S(1)} fusion(f32[2,320,256]{1,2,0:T(8,128)} %all-reduce.9.cloned.1.call-done, f32[2,322,1]{1,2,0:T(1,128)S(1)} %collective-permute-done.7, f32[2,1,256]{1,2,0:T(8,128)S(1)} %collective-permute-done.5, f32[2,1,256]{1,2,0:T(8,128)S(1)} %collective-permute-done.4, f32[2,322,1]{1,2,0:T(1,128)S(1)} %collective-permute-done.6), kind=kLoop, calls=%fused_computation.29 | loop fusion | flops 2457600 | bytes 1319968 | tf_op jit(solution)/shard_map/add | solution.py:63
  188.7 3.4 %collective-permute-start.8 = (f32[2,1,256]{1,2,0:T(8,128)S(1)}, f32[2,1,256]{1,2,0:T(8,128)S(1)}, u32[]{:S(2)}, u32[]{:S(2)}) collective-permute-start(f32[2,1,256]{1,2,0:T(8,128)S(1)} %get-tuple-element.95), channel_id=1, source_target_pairs={{0,2},{2,4},{4,6},{1,3},{3,5},{5,7},{8,10},{10,12},{12,14},{9,11},... | collective-permute-start | bytes 6152 | tf_op jit(solution)/shard_map/ppermute | solution.py:20
  192.1 1.3 collective-permute-start.9
  193.5 2.5 %collective-permute-done.8 = f32[2,1,256]{1,2,0:T(8,128)S(1)} collective-permute-done((f32[2,1,256]{1,2,0:T(8,128)S(1)}, f32[2,1,256]{1,2,0:T(8,128)S(1)}, u32[]{:S(2)}, u32[]{:S(2)}) %collective-permute-start.8) | collective-permute-done | bytes 2080 | tf_op jit(solution)/shard_map/ppermute | solution.py:20
  196.0 4.4 %collective-permute-done.9 = f32[2,1,256]{1,2,0:T(8,128)S(1)} collective-permute-done((f32[2,1,256]{1,2,0:T(8,128)S(1)}, f32[2,1,256]{1,2,0:T(8,128)S(1)}, u32[]{:S(2)}, u32[]{:S(2)}) %collective-permute-start.9) | collective-permute-done | bytes 2080 | tf_op jit(solution)/shard_map/ppermute | solution.py:22
  200.5 1.7 collective-permute-start.10
  202.1 1.3 collective-permute-start.11
  203.5 1.5 slice_subtract_fusion.12
  207.6 1.9 fusion.3
  (135 shorter events, 14.1 us)
Async XLA Ops:
  7.2 11.5 %copy-start.44 = (f32[1,320,256]{2,1,0:T(8,128)S(1)}, f32[1,320,256]{2,1,0:T(8,128)}, u32[]{:S(2)}) copy-start(f32[1,320,256]{2,1,0:T(8,128)} %param.32) | copy-start | bytes 983044
  7.2 12.4 %copy-start.45 = (f32[1,320,256]{2,1,0:T(8,128)S(1)}, f32[1,320,256]{2,1,0:T(8,128)}, u32[]{:S(2)}) copy-start(f32[1,320,256]{2,1,0:T(8,128)} %param.33) | copy-start | bytes 983044
  7.2 152.9 %all-reduce.9.cloned.1.call-start = ((), (), s32[]{:S(2)}) async-start(), calls=%async_computation | async-start | bytes 1572864 | tf_op jit(solution)/shard_map/psum | solution.py:219
  19.8 14.1 %copy-start.42 = (f32[1,320,256]{1,2,0:T(8,128)S(1)}, f32[1,320,256]{1,2,0:T(8,128)}, u32[]{:S(2)}) copy-start(f32[1,320,256]{1,2,0:T(8,128)} %copy.82) | copy-start | bytes 983044
  19.8 14.1 %copy-start.41 = (f32[1,320,256]{1,2,0:T(8,128)S(1)}, f32[1,320,256]{1,2,0:T(8,128)}, u32[]{:S(2)}) copy-start(f32[1,320,256]{1,2,0:T(8,128)} %copy.83) | copy-start | bytes 983044
  19.8 14.2 %copy-start.40 = (f32[1,320,256]{1,2,0:T(8,128)S(1)}, f32[1,320,256]{1,2,0:T(8,128)}, u32[]{:S(2)}) copy-start(f32[1,320,256]{1,2,0:T(8,128)} %copy.84) | copy-start | bytes 983044
  34.1 21.4 %copy-start = (f32[8,320,256]{1,2,0:T(8,128)}, f32[8,320,256]{1,2,0:T(8,128)S(1)}, u32[]{:S(2)}) copy-start(f32[8,320,256]{1,2,0:T(8,128)S(1)} %constant_dynamic-update-slice_fusion) | copy-start | bytes 7864324
  34.1 13.2 %copy-start.46 = (f32[1,3,1]{1,2,0:T(1,128)S(1)}, f32[1,3,1]{1,2,0:T(1,128)}, u32[]{:S(2)}) copy-start(f32[1,3,1]{1,2,0:T(1,128)} %param.26) | copy-start | bytes 40
  34.1 13.9 %copy-start.47 = (s32[64]{0:T(128)S(1)}, s32[64]{0:T(128)}, u32[]{:S(2)}) copy-start(s32[64]{0:T(128)} %param.27) | copy-start | bytes 772
  34.1 13.9 %copy-start.48 = (s32[64]{0:T(128)S(1)}, s32[64]{0:T(128)}, u32[]{:S(2)}) copy-start(s32[64]{0:T(128)} %param.28) | copy-start | bytes 772
  34.1 13.9 %copy-start.50 = (s32[3]{0:T(128)S(1)}, s32[3]{0:T(128)}, u32[]{:S(2)}) copy-start(s32[3]{0:T(128)} %constant.129.clone.1) | copy-start | bytes 40
  37.6 16.6 %collective-permute-start.1 = (f32[8,6,256]{2,0,1:T(8,128)S(1)}, f32[8,6,256]{2,0,1:T(8,128)S(1)}, u32[]{:S(2)}, u32[]{:S(2)}) collective-permute-start(f32[8,6,256]{2,0,1:T(8,128)S(1)} %copy.87), channel_id=1, source_target_pairs={{2,0},{4,2},{6,4},{3,1},{5,3},{7,5},{10,8},{12,10},{14,12},{11,9},... | collective-permute-start | bytes 147464 | tf_op jit(solution)/shard_map/ppermute | solution.py:22
  40.4 12.4 %collective-permute-start = (f32[8,6,256]{2,0,1:T(8,128)S(1)}, f32[8,6,256]{2,0,1:T(8,128)S(1)}, u32[]{:S(2)}, u32[]{:S(2)}) collective-permute-start(f32[8,6,256]{2,0,1:T(8,128)S(1)} %copy.86), channel_id=1, source_target_pairs={{0,2},{2,4},{4,6},{1,3},{3,5},{5,7},{8,10},{10,12},{12,14},{9,11},... | collective-permute-start | bytes 147464 | tf_op jit(solution)/shard_map/ppermute | solution.py:20
  55.5 11.5 %copy-start.16 = (f32[8,6,256]{1,2,0:T(8,128)S(1)}, f32[8,6,256]{1,2,0:T(8,128)}, u32[]{:S(2)}) copy-start(f32[8,6,256]{1,2,0:T(8,128)} %copy.88) | copy-start | bytes 147460
  55.5 11.5 %copy-start.17 = (f32[8,6,256]{1,2,0:T(8,128)S(1)}, f32[8,6,256]{1,2,0:T(8,128)}, u32[]{:S(2)}) copy-start(f32[8,6,256]{1,2,0:T(8,128)} %copy.89) | copy-start | bytes 147460
  56.6 6.0 %collective-permute-start.2 = (f32[8,332,6]{1,2,0:T(8,128)S(1)}, f32[8,332,6]{1,2,0:T(8,128)S(1)}, u32[]{:S(2)}, u32[]{:S(2)}) collective-permute-start(f32[8,332,6]{1,2,0:T(8,128)S(1)} %get-tuple-element.81), channel_id=1, source_target_pairs={{0,1},{2,3},{4,5},{6,7},{8,9},{10,11},{12,13},{14,15},{16,17},{18,... | collective-permute-start | bytes 191240 | tf_op jit(solution)/shard_map/ppermute | solution.py:20
  60.4 6.5 %collective-permute-start.3 = (f32[8,332,6]{1,2,0:T(8,128)S(1)}, f32[8,332,6]{1,2,0:T(8,128)S(1)}, u32[]{:S(2)}, u32[]{:S(2)}) collective-permute-start(f32[8,332,6]{1,2,0:T(8,128)S(1)} %get-tuple-element.82), channel_id=1, source_target_pairs={{1,0},{3,2},{5,4},{7,6},{9,8},{11,10},{13,12},{15,14},{17,16},{19,... | collective-permute-start | bytes 191240 | tf_op jit(solution)/shard_map/ppermute | solution.py:22
  70.2 0.8 copy-start.22
  70.2 2.7 %copy-start.31 = (f32[1,332,268]{1,2,0:T(8,128)}, f32[1,332,268]{1,2,0:T(8,128)S(1)}, u32[]{:S(2)}) copy-start(f32[1,332,268]{1,2,0:T(8,128)S(1)} %get-tuple-element.86) | copy-start | bytes 1067716
  72.9 0.8 copy-start.34
  77.6 0.8 copy-start.14
  81.2 0.8 copy-start.35
  90.3 10.2 %copy-start.49 = (f32[1,3,64]{2,0,1:T(1,128)S(1)}, f32[1,3,64]{2,0,1:T(1,128)}, u32[]{:S(2)}) copy-start(f32[1,3,64]{2,0,1:T(1,128)} %param.29) | copy-start | bytes 2308
  93.0 0.8 copy-start.33
  109.5 2.6 %copy-start.2 = (f32[1,332,268]{1,2,0:T(8,128)S(1)}, f32[1,332,268]{1,2,0:T(8,128)}, u32[]{:S(2)}) copy-start(f32[1,332,268]{1,2,0:T(8,128)} %get-tuple-element.68) | copy-start | bytes 1067716
  109.5 2.6 %copy-start.5 = (f32[1,332,268]{1,2,0:T(8,128)S(1)}, f32[1,332,268]{1,2,0:T(8,128)}, u32[]{:S(2)}) copy-start(f32[1,332,268]{1,2,0:T(8,128)} %get-tuple-element.69) | copy-start | bytes 1067716
  109.5 2.6 %copy-start.8 = (f32[1,332,268]{1,2,0:T(8,128)S(1)}, f32[1,332,268]{1,2,0:T(8,128)}, u32[]{:S(2)}) copy-start(f32[1,332,268]{1,2,0:T(8,128)} %get-tuple-element.70) | copy-start | bytes 1067716
  109.5 2.6 %copy-start.11 = (f32[1,332,268]{1,2,0:T(8,128)S(1)}, f32[1,332,268]{1,2,0:T(8,128)}, u32[]{:S(2)}) copy-start(f32[1,332,268]{1,2,0:T(8,128)} %get-tuple-element.71) | copy-start | bytes 1067716
  109.5 2.6 %copy-start.18 = (f32[332,268]{0,1:T(8,128)S(1)}, f32[332,268]{0,1:T(8,128)}, u32[]{:S(2)}) copy-start(f32[332,268]{0,1:T(8,128)} %scatter_fusion) | copy-start | bytes 1067716
  112.1 1.2 copy-start.21
  112.1 1.2 copy-start.27
  122.5 2.4 %copy-start.3 = (f32[1,332,268]{1,2,0:T(8,128)S(1)}, f32[1,332,268]{1,2,0:T(8,128)}, u32[]{:S(2)}) copy-start(f32[1,332,268]{1,2,0:T(8,128)} %get-tuple-element.68) | copy-start | bytes 1067716
  122.5 2.4 %copy-start.6 = (f32[1,332,268]{1,2,0:T(8,128)S(1)}, f32[1,332,268]{1,2,0:T(8,128)}, u32[]{:S(2)}) copy-start(f32[1,332,268]{1,2,0:T(8,128)} %get-tuple-element.69) | copy-start | bytes 1067716
  122.5 2.4 %copy-start.9 = (f32[1,332,268]{1,2,0:T(8,128)S(1)}, f32[1,332,268]{1,2,0:T(8,128)}, u32[]{:S(2)}) copy-start(f32[1,332,268]{1,2,0:T(8,128)} %get-tuple-element.70) | copy-start | bytes 1067716
  122.5 2.4 %copy-start.12 = (f32[1,332,268]{1,2,0:T(8,128)S(1)}, f32[1,332,268]{1,2,0:T(8,128)}, u32[]{:S(2)}) copy-start(f32[1,332,268]{1,2,0:T(8,128)} %get-tuple-element.71) | copy-start | bytes 1067716
  122.5 2.4 %copy-start.19 = (f32[332,268]{0,1:T(8,128)S(1)}, f32[332,268]{0,1:T(8,128)}, u32[]{:S(2)}) copy-start(f32[332,268]{0,1:T(8,128)} %scatter_fusion.1) | copy-start | bytes 1067716
  124.9 1.2 copy-start.26
  124.9 1.2 copy-start.29
  135.1 2.6 %copy-start.1 = (f32[1,332,268]{1,2,0:T(8,128)S(1)}, f32[1,332,268]{1,2,0:T(8,128)}, u32[]{:S(2)}) copy-start(f32[1,332,268]{1,2,0:T(8,128)} %divide_add_fusion) | copy-start | bytes 1067716
  135.1 2.6 %copy-start.15 = (f32[1,332,268]{1,2,0:T(8,128)S(1)}, f32[1,332,268]{1,2,0:T(8,128)}, u32[]{:S(2)}) copy-start(f32[1,332,268]{1,2,0:T(8,128)} %copy-done.14) | copy-start | bytes 1067716
  135.1 2.6 %copy-start.23 = (f32[332,268]{0,1:T(8,128)S(1)}, f32[332,268]{0,1:T(8,128)}, u32[]{:S(2)}) copy-start(f32[332,268]{0,1:T(8,128)} %copy-done.22) | copy-start | bytes 1067716
  135.1 2.7 %copy-start.28 = (f32[1,332,268]{1,2,0:T(8,128)S(1)}, f32[1,332,268]{1,2,0:T(8,128)}, u32[]{:S(2)}) copy-start(f32[1,332,268]{1,2,0:T(8,128)} %copy-done.27) | copy-start | bytes 1067716
  135.2 2.7 %copy-start.30 = (f32[1,332,268]{1,2,0:T(8,128)S(1)}, f32[1,332,268]{1,2,0:T(8,128)}, u32[]{:S(2)}) copy-start(f32[1,332,268]{1,2,0:T(8,128)} %copy-done.29) | copy-start | bytes 1067716
  135.2 2.7 %copy-start.32 = (f32[1,332,268]{1,2,0:T(8,128)S(1)}, f32[1,332,268]{1,2,0:T(8,128)}, u32[]{:S(2)}) copy-start(f32[1,332,268]{1,2,0:T(8,128)} %copy-done.31) | copy-start | bytes 1067716
  137.8 4.3 %copy-start.24 = (f32[1,332,268]{1,2,0:T(8,128)}, f32[1,332,268]{1,2,0:T(8,128)S(1)}, u32[]{:S(2)}) copy-start(f32[1,332,268]{1,2,0:T(8,128)S(1)} %get-tuple-element.61) | copy-start | bytes 1067716
  137.8 3.4 %copy-start.36 = (f32[332,268]{0,1:T(8,128)S(1)}, f32[332,268]{0,1:T(8,128)}, u32[]{:S(2)}) copy-start(f32[332,268]{0,1:T(8,128)} %get-tuple-element.52) | copy-start | bytes 1067716
  137.8 3.4 %copy-start.37 = (f32[332,268]{0,1:T(8,128)S(1)}, f32[332,268]{0,1:T(8,128)}, u32[]{:S(2)}) copy-start(f32[332,268]{0,1:T(8,128)} %get-tuple-element.55) | copy-start | bytes 1067716
  143.0 50.4 %copy-start.25 = (f32[1,332,268]{1,2,0:T(8,128)S(1)}, f32[1,332,268]{1,2,0:T(8,128)}, u32[]{:S(2)}) copy-start(f32[1,332,268]{1,2,0:T(8,128)} %copy-done.24) | copy-start | bytes 1067716
  161.2 9.7 %collective-permute-start.4 = (f32[2,1,256]{1,2,0:T(8,128)S(1)}, f32[2,1,256]{1,2,0:T(8,128)S(1)}, u32[]{:S(2)}, u32[]{:S(2)}) collective-permute-start(f32[2,1,256]{1,2,0:T(8,128)S(1)} %get-tuple-element.97), channel_id=1, source_target_pairs={{0,2},{2,4},{4,6},{1,3},{3,5},{5,7},{8,10},{10,12},{12,14},{9,11},... | collective-permute-start | bytes 6152 | tf_op jit(solution)/shard_map/ppermute | solution.py:20
  165.0 38.5 %copy-start.4 = (f32[1,332,268]{1,2,0:T(8,128)S(1)}, f32[1,332,268]{1,2,0:T(8,128)}, u32[]{:S(2)}) copy-start(f32[1,332,268]{1,2,0:T(8,128)} %get-tuple-element.68) | copy-start | bytes 1067716
  165.0 38.5 %copy-start.7 = (f32[1,332,268]{1,2,0:T(8,128)S(1)}, f32[1,332,268]{1,2,0:T(8,128)}, u32[]{:S(2)}) copy-start(f32[1,332,268]{1,2,0:T(8,128)} %get-tuple-element.69) | copy-start | bytes 1067716
  165.0 38.5 %copy-start.10 = (f32[1,332,268]{1,2,0:T(8,128)S(1)}, f32[1,332,268]{1,2,0:T(8,128)}, u32[]{:S(2)}) copy-start(f32[1,332,268]{1,2,0:T(8,128)} %get-tuple-element.70) | copy-start | bytes 1067716
  165.0 38.5 %copy-start.13 = (f32[1,332,268]{1,2,0:T(8,128)S(1)}, f32[1,332,268]{1,2,0:T(8,128)}, u32[]{:S(2)}) copy-start(f32[1,332,268]{1,2,0:T(8,128)} %get-tuple-element.71) | copy-start | bytes 1067716
  165.0 38.5 %copy-start.20 = (f32[332,268]{0,1:T(8,128)S(1)}, f32[332,268]{0,1:T(8,128)}, u32[]{:S(2)}) copy-start(f32[332,268]{0,1:T(8,128)} %scatter_fusion.2) | copy-start | bytes 1067716
  165.0 38.5 %copy-start.38 = (f32[1,332,268]{1,2,0:T(8,128)S(1)}, f32[1,332,268]{1,2,0:T(8,128)}, u32[]{:S(2)}) copy-start(f32[1,332,268]{1,2,0:T(8,128)} %get-tuple-element.59) | copy-start | bytes 1067716
  165.0 38.5 %copy-start.39 = (f32[1,332,268]{1,2,0:T(8,128)S(1)}, f32[1,332,268]{1,2,0:T(8,128)}, u32[]{:S(2)}) copy-start(f32[1,332,268]{1,2,0:T(8,128)} %get-tuple-element.60) | copy-start | bytes 1067716
  165.0 10.3 %collective-permute-start.5 = (f32[2,1,256]{1,2,0:T(8,128)S(1)}, f32[2,1,256]{1,2,0:T(8,128)S(1)}, u32[]{:S(2)}, u32[]{:S(2)}) collective-permute-start(f32[2,1,256]{1,2,0:T(8,128)S(1)} %get-tuple-element.98), channel_id=1, source_target_pairs={{2,0},{4,2},{6,4},{3,1},{5,3},{7,5},{10,8},{12,10},{14,12},{11,9},... | collective-permute-start | bytes 6152 | tf_op jit(solution)/shard_map/ppermute | solution.py:22
  176.2 4.7 %collective-permute-start.6 = (f32[2,322,1]{1,2,0:T(1,128)S(1)}, f32[2,322,1]{1,2,0:T(1,128)S(1)}, u32[]{:S(2)}, u32[]{:S(2)}) collective-permute-start(f32[2,322,1]{1,2,0:T(1,128)S(1)} %get-tuple-element.91), channel_id=1, source_target_pairs={{0,1},{2,3},{4,5},{6,7},{8,9},{10,11},{12,13},{14,15},{16,17},{18,... | collective-permute-start | bytes 7736 | tf_op jit(solution)/shard_map/ppermute | solution.py:20
  179.6 5.5 %collective-permute-start.7 = (f32[2,322,1]{1,2,0:T(1,128)S(1)}, f32[2,322,1]{1,2,0:T(1,128)S(1)}, u32[]{:S(2)}, u32[]{:S(2)}) collective-permute-start(f32[2,322,1]{1,2,0:T(1,128)S(1)} %get-tuple-element.92), channel_id=1, source_target_pairs={{1,0},{3,2},{5,4},{7,6},{9,8},{11,10},{13,12},{15,14},{17,16},{19,... | collective-permute-start | bytes 7736 | tf_op jit(solution)/shard_map/ppermute | solution.py:22
  188.7 7.3 %collective-permute-start.8 = (f32[2,1,256]{1,2,0:T(8,128)S(1)}, f32[2,1,256]{1,2,0:T(8,128)S(1)}, u32[]{:S(2)}, u32[]{:S(2)}) collective-permute-start(f32[2,1,256]{1,2,0:T(8,128)S(1)} %get-tuple-element.95), channel_id=1, source_target_pairs={{0,2},{2,4},{4,6},{1,3},{3,5},{5,7},{8,10},{10,12},{12,14},{9,11},... | collective-permute-start | bytes 6152 | tf_op jit(solution)/shard_map/ppermute | solution.py:20
  192.1 8.3 %collective-permute-start.9 = (f32[2,1,256]{1,2,0:T(8,128)S(1)}, f32[2,1,256]{1,2,0:T(8,128)S(1)}, u32[]{:S(2)}, u32[]{:S(2)}) collective-permute-start(f32[2,1,256]{1,2,0:T(8,128)S(1)} %get-tuple-element.96), channel_id=1, source_target_pairs={{2,0},{4,2},{6,4},{3,1},{5,3},{7,5},{10,8},{12,10},{14,12},{11,9},... | collective-permute-start | bytes 6152 | tf_op jit(solution)/shard_map/ppermute | solution.py:22
  200.4 3.1 %copy-start.43 = (f32[2,1,256]{1,2,0:T(8,128)}, f32[2,1,256]{1,2,0:T(8,128)S(1)}, u32[]{:S(2)}) copy-start(f32[2,1,256]{1,2,0:T(8,128)S(1)} %collective-permute-done.9) | copy-start | bytes 6148
  200.5 6.3 %collective-permute-start.10 = (f32[2,322,1]{1,2,0:T(1,128)S(1)}, f32[2,322,1]{1,2,0:T(1,128)S(1)}, u32[]{:S(2)}, u32[]{:S(2)}) collective-permute-start(f32[2,322,1]{1,2,0:T(1,128)S(1)} %get-tuple-element.89), channel_id=1, source_target_pairs={{0,1},{2,3},{4,5},{6,7},{8,9},{10,11},{12,13},{14,15},{16,17},{18,... | collective-permute-start | bytes 7736 | tf_op jit(solution)/shard_map/ppermute | solution.py:20
  202.1 5.5 %collective-permute-start.11 = (f32[2,322,1]{1,2,0:T(1,128)S(1)}, f32[2,322,1]{1,2,0:T(1,128)S(1)}, u32[]{:S(2)}, u32[]{:S(2)}) collective-permute-start(f32[2,322,1]{1,2,0:T(1,128)S(1)} %get-tuple-element.90), channel_id=1, source_target_pairs={{1,0},{3,2},{5,4},{7,6},{9,8},{11,10},{13,12},{15,14},{17,16},{19,... | collective-permute-start | bytes 7736 | tf_op jit(solution)/shard_map/ppermute | solution.py:22
Sparse Core Ops, SparseCore 0:
  143.1 16.8 all-reduce.8
where the time goes:
time: 220 us; the launch traced here: 218 us
  other arithmetic  81 us (37%)
  local copies, waits for them, and re-layouts  43.8 us (20%)
  waiting for transfers between devices  43 us (20%)
  starting transfers between devices  29.6 us (13%)
  between operations  20.8 us (9%)
    scatter-add x3, other arithmetic, inject(): return adjoint_field.at[:, obs_lx, obs_ly].add(mismatch)  27.2 us
    ppermute x6, starting transfers between devices, padded_2(): lax.ppermute(tail, axis, [(i, (i + 1) % count) for i in range(ends)])  21.5 us
    unnamed x118, local copies, waits for them, and re-layouts  20.3 us
    ppermute x6, waiting for transfers between devices, padded_2(): lax.ppermute(head, axis, [((i + 1) % count, i) for i in range(ends)])  18.2 us
    psum x1, waiting for transfers between devices, on_device(): summed = lax.psum(stacked, 'test')  17.1 us
    unnamed x2, other arithmetic  11.8 us
    ppermute x6, starting transfers between devices, padded_2(): lax.ppermute(head, axis, [((i + 1) % count, i) for i in range(ends)])  8.02 us
    ppermute x6, waiting for transfers between devices, padded_2(): lax.ppermute(tail, axis, [(i, (i + 1) % count) for i in range(ends)])  7.71 us
  transfers between devices with their start and end apart: 13, of which 9 were waited for; matrix products, arithmetic and copies ran while one was open for 4% of the time, Pallas kernels for 0%

commit v1 on v0

v1 whole, which is shorter than its diff:
```python
import jax
import jax.numpy as jnp
from jax import lax
from jax.experimental import pallas as pl
from jax.experimental.pallas import tpu as pltpu
from jax.sharding import PartitionSpec as P

SMOOTH = 2
EDGE = 8
LANES = 128
BLEND = 0.2
FIELDS = 7


def pairs_of(count, parity):
    found = []
    for low in range(parity, count - 1, 2):
        found += [(low, low + 1), (low + 1, low)]
    return found


def rounds_of(count):
    return [parity for parity in (0, 1) if pairs_of(count, parity)]


def partner(index, parity):
    return index + 1 if index % 2 == parity else index - 1


def corner_pairs(nx, ny, px, py):
    found = []
    for x in range(nx):
        for y in range(ny):
            there = (partner(x, px), partner(y, py))
            if 0 <= there[0] < nx and 0 <= there[1] < ny:
                found.append((x * ny + y, there[0] * ny + there[1]))
    return found


def forward_of(axis, parity):
    return lax.rem(lax.axis_index(axis), 2) == parity


def lane_iota(rows, cols):
    return lax.broadcasted_iota(jnp.int32, (rows, cols), 1)


def pack(fields, xr, yr):
    tile_rows, tile_cols = fields[0].shape
    half = tile_rows // 2
    nxr, nyr = len(xr), len(yr)

    def kernel(*refs):
        ins = refs[:FIELDS]
        row_out = refs[FIELDS : FIELDS + nxr]
        col_out = refs[FIELDS + nxr : FIELDS + nxr + nyr]
        corner_out = refs[FIELDS + nxr + nyr : FIELDS + nxr + nyr + nxr * nyr]
        rest = refs[FIELDS + nxr + nyr + nxr * nyr :]
        zone_rows, cols, zone_cols, row_sem, col_sem = rest
        row_copies = []
        for i, px in enumerate(xr):
            start = jnp.where(forward_of("tx", px), tile_rows - EDGE, 0)
            start = pl.multiple_of(start, EDGE)
            for f in range(FIELDS):
                into = zone_rows.at[i] if f == 2 else row_out[i].at[pl.ds(EDGE * f, EDGE)]
                row_copies.append(
                    pltpu.make_async_copy(
                        ins[f].at[pl.ds(start, EDGE)], into, row_sem.at[i, f]
                    )
                )
        col_copies = []
        for j, py in enumerate(yr):
            start = jnp.where(forward_of("ty", py), tile_cols - LANES, 0)
            start = pl.multiple_of(start, LANES)
            for f in range(FIELDS):
                into = zone_cols.at[j] if f == 2 else cols.at[j, f]
                col_copies.append(
                    pltpu.make_async_copy(
                        ins[f].at[:, pl.ds(start, LANES)], into, col_sem.at[j, f]
                    )
                )
        for copy in row_copies + col_copies:
            copy.start()
        for copy in row_copies:
            copy.wait()
        for i in range(nxr):
            row_out[i][2 * EDGE : 3 * EDGE, :] = zone_rows[i].astype(jnp.float32)
        slot = lane_iota(EDGE, LANES) // EDGE
        for i in range(nxr):
            for j, py in enumerate(yr):
                ahead = forward_of("ty", py)
                shift = jnp.where(ahead, 1, 0)
                total = jnp.zeros((EDGE, LANES), jnp.float32)
                for f in range(FIELDS):
                    rows = row_out[i][EDGE * f : EDGE * (f + 1), :]
                    part = jnp.where(ahead, rows[:, tile_cols - LANES :], rows[:, :LANES])
                    part = pltpu.roll(part, EDGE * f, 1)
                    want = lax.rem(f - shift + 16, 16)
                    total = jnp.where(slot == want, part, total)
                corner_out[i * nyr + j][...] = total
        for copy in col_copies:
            copy.wait()
        for j, py in enumerate(yr):
            shift = jnp.where(forward_of("ty", py), 1, 0)

            def body(k, carry):
                total = jnp.zeros((EDGE, LANES), jnp.float32)
                for h in range(2):
                    at = pl.multiple_of(k * EDGE + h * half, EDGE)
                    for f in range(FIELDS):
                        if f == 2:
                            part = zone_cols[j, pl.ds(at, EDGE), :].astype(jnp.float32)
                        else:
                            part = cols[j, f, pl.ds(at, EDGE), :]
                        amount = EDGE * f + 64 * h
                        part = pltpu.roll(part, amount, 1) if amount else part
                        want = lax.rem(f + 8 * h - shift + 16, 16)
                        total = jnp.where(slot == want, part, total)
                col_out[j][pl.ds(pl.multiple_of(k * EDGE, EDGE), EDGE), :] = total
                return carry

            lax.fori_loop(0, half // EDGE, body, 0, unroll=2)

    outs = [jax.ShapeDtypeStruct((EDGE * FIELDS, tile_cols), jnp.float32)] * nxr
    outs += [jax.ShapeDtypeStruct((half, LANES), jnp.float32)] * nyr
    outs += [jax.ShapeDtypeStruct((EDGE, LANES), jnp.float32)] * (nxr * nyr)
    made = pl.pallas_call(
        kernel,
        out_shape=outs,
        in_specs=[pl.BlockSpec(memory_space=pl.ANY)] * FIELDS,
        scratch_shapes=[
            pltpu.VMEM((nxr, EDGE, tile_cols), jnp.int32),
            pltpu.VMEM((nyr, FIELDS, tile_rows, LANES), jnp.float32),
            pltpu.VMEM((nyr, tile_rows, LANES), jnp.int32),
            pltpu.SemaphoreType.DMA((nxr, FIELDS)),
            pltpu.SemaphoreType.DMA((nyr, FIELDS)),
        ],
        name="pack",
    )(*fields)
    return made[:nxr], made[nxr : nxr + nyr], made[nxr + nyr :]


def window(fields, scalars, row_in, col_in, corner_in, xr, yr, nx, ny):
    tile_rows, tile_cols = fields[0].shape
    storage, pump_x, pump_y, pump_rates, obs_x, obs_y, observed = scalars
    zones = storage.shape[1]
    steps, pumps = pump_rates.shape
    wells = obs_x.shape[0]
    assert 2 * steps + SMOOTH <= EDGE
    half = tile_rows // 2
    nxr, nyr = len(xr), len(yr)
    rows, cols = tile_rows + 2 * EDGE, tile_cols + LANES
    chunks = rows // EDGE
    f32 = jnp.float32

    def kernel(*refs):
        pos = 0

        def take(count):
            nonlocal pos
            pos += count
            return refs[pos - count : pos]

        (st, pxs, pys, prs, oxs, oys, obs) = take(7)
        ins = take(FIELDS)
        rin, cin, kin = take(nxr), take(nyr), take(nxr * nyr)
        smooth_out, frac_out, mat_out = take(3)
        (wide, zone_mid, colbuf, cornerbuf, rowzone) = take(5)
        (rm, cx, cy, count, seen, frac, fluxx, fluxy, moved, px_, py_, gs_, grad, grad2) = take(14)
        (mid_sem, row_sem, col_sem, corner_sem) = take(4)
        res, shp, rs = wide.at[0], wide.at[1], wide.at[2]
        mat, adj, adm = wide.at[4], wide.at[5], wide.at[6]

        tx, ty = lax.axis_index("tx"), lax.axis_index("ty")
        copies = []
        for f in range(FIELDS):
            into = (
                zone_mid
                if f == 2
                else (frac.at[0] if f == 3 else wide.at[f]).at[pl.ds(EDGE, tile_rows), pl.ds(0, tile_cols)]
            )
            copies.append(pltpu.make_async_copy(ins[f], into, mid_sem.at[f]))
        for j in range(nyr):
            copies.append(pltpu.make_async_copy(cin[j], colbuf.at[j], col_sem.at[j]))
        for i in range(nxr * nyr):
            copies.append(pltpu.make_async_copy(kin[i], cornerbuf.at[i], corner_sem.at[i]))
        tops = []
        for i, px in enumerate(xr):
            to = jnp.where(forward_of("tx", px), tile_rows + EDGE, 0)
            to = pl.multiple_of(to, EDGE)
            tops.append(to)
            for f in range(FIELDS):
                target = frac.at[0] if f == 3 else wide.at[f]
                copies.append(
                    pltpu.make_async_copy(
                        rin[i].at[pl.ds(EDGE * f, EDGE)],
                        target.at[pl.ds(to, EDGE), pl.ds(0, tile_cols)],
                        row_sem.at[i, f],
                    )
                )
        if nxr < 2:
            for f in range(FIELDS):
                target = frac.at[0] if f == 3 else wide.at[f]
                target[0:EDGE, :] = jnp.zeros((EDGE, cols), f32)
                target[rows - EDGE : rows, :] = jnp.zeros((EDGE, cols), f32)
        for copy in copies:
            copy.start()

        lane = lane_iota(EDGE, cols)
        col = jnp.where(lane < tile_cols + LANES // 2, lane, lane - cols)
        gcol = col + ty * tile_cols
        total_cols, total_rows = tile_cols * ny, tile_rows * nx
        col_in_grid = (gcol >= 0) & (gcol < total_cols)
        col_face = (gcol >= 0) & (gcol + 1 < total_cols)
        sub = lax.broadcasted_iota(jnp.int32, (EDGE, cols), 0)
        row0 = tx * tile_rows - EDGE

        zero = jnp.zeros((EDGE, cols), f32)

        def clear(k, carry):
            at = pl.ds(pl.multiple_of(k * EDGE, EDGE), EDGE)
            count[at, :] = zero
            for n in range(steps):
                seen[n, at, :] = zero
            return carry

        lax.fori_loop(0, chunks, clear, 0, unroll=2)
        one_lane = lane_iota(1, cols)

        def place(gx, gy):
            lr = gx - row0
            lc = gy - ty * tile_cols
            ok = (lr >= 0) & (lr < rows) & (lc >= -EDGE) & (lc < tile_cols + EDGE)
            return lr, jnp.where(lc < 0, lc + cols, lc), ok

        def well(o, carry):
            lr, ll, ok = place(oxs[o], oys[o])

            @pl.when(ok)
            def _():
                hit = one_lane == ll
                at = pl.ds(lr, 1)
                count[at, :] += jnp.where(hit, 1.0, 0.0)
                for n in range(steps):
                    seen[n, at, :] += jnp.where(hit, obs[n, o], 0.0)

            return carry

        lax.fori_loop(0, wells, well, 0)

        for copy in copies:
            copy.wait()

        def widen(k, carry):
            at = pl.ds(pl.multiple_of((k + 1) * EDGE, EDGE), EDGE)
            wide[2, at, 0:tile_cols] = zone_mid[pl.ds(pl.multiple_of(k * EDGE, EDGE), EDGE), :].astype(f32)
            return carry

        lax.fori_loop(0, tile_rows // EDGE, widen, 0, unroll=4)
        edge_lane = lane_iota(EDGE, LANES)
        side = []
        for py in yr:
            ahead = forward_of("ty", py)
            low = jnp.where(ahead, 0, LANES - EDGE)
            side.append((edge_lane >= low) & (edge_lane < low + EDGE))

        def edge_of(messages, amount):
            out = jnp.zeros((EDGE, LANES), f32)
            for mask, message in zip(side, messages):
                part = pltpu.roll(message, (LANES - amount) % LANES, 1) if amount % LANES else message
                out = jnp.where(mask, part, out)
            return out

        def put_edge(f, at, value):
            target = frac.at[0] if f == 3 else wide.at[f]
            target[at, tile_cols:cols] = value

        for h in range(2):

            def fringe(k, carry):
                src = pl.ds(pl.multiple_of(k * EDGE, EDGE), EDGE)
                at = pl.ds(pl.multiple_of(k * EDGE + EDGE + h * half, EDGE), EDGE)
                messages = [colbuf[j, src, :] for j in range(nyr)]
                for f in range(FIELDS):
                    put_edge(f, at, edge_of(messages, EDGE * f + 64 * h))
                return carry

            lax.fori_loop(0, half // EDGE, fringe, 0, unroll=2)
        for i in range(nxr):
            messages = [cornerbuf[i * nyr + j] for j in range(nyr)]
            for f in range(FIELDS):
                put_edge(f, pl.ds(tops[i], EDGE), edge_of(messages, EDGE * f))

        def at_of(k):
            return pl.ds(pl.multiple_of(k * EDGE, EDGE), EDGE)

        def next_of(k):
            return at_of(jnp.minimum(k + 1, chunks - 1))

        def up1(x):
            return pltpu.roll(x, EDGE - 1, 0)

        def down1(x):
            return pltpu.roll(x, 1, 0)

        def right(x):
            return pltpu.roll(x, cols - 1, 1)

        def left(x):
            return pltpu.roll(x, 1, 1)

        last, first = sub == EDGE - 1, sub == 0
        inv_f = [1.0 / jnp.full((EDGE, cols), st[0, z], f32) for z in range(zones)]
        inv_m = [1.0 / jnp.full((EDGE, cols), st[1, z], f32) for z in range(zones)]

        def prepare(k, carry):
            at = at_of(k)
            res[at, :] = jnp.exp(-res[at, :])
            shp[at, :] = jnp.exp(shp[at, :])
            zone = rs[at, :]
            a, b = inv_f[0], inv_m[0]
            for z in range(1, zones):
                hit = zone == float(z)
                a = jnp.where(hit, inv_f[z], a)
                b = jnp.where(hit, inv_m[z], b)
            rs[at, :] = a
            rm[at, :] = b
            return carry

        lax.fori_loop(0, chunks, prepare, 0)

        def links(k, carry):
            at = at_of(k)
            here = res[at, :]
            below = jnp.where(last, up1(res[next_of(k), :]), up1(here))
            beside = right(here)
            grow = row0 + k * EDGE + sub
            ok = (grow >= 0) & (grow + 1 < total_rows)
            cx[at, :] = jnp.where(ok, 2.0 / (here + below), 0.0)
            cy[at, :] = jnp.where(col_face, 2.0 / (here + beside), 0.0)
            return carry

        lax.fori_loop(0, chunks, links, 0, unroll=2)

        for n in range(steps):
            src, dst = frac.at[n], frac.at[n + 1]

            def step(k, carry, src=src, dst=dst, n=n):
                f, fup, flux_above = carry
                at = at_of(k)
                f_next = src[next_of(k), :]
                fup_next = up1(f_next)
                m = mat[at, :]
                fx = cx[at, :] * (jnp.where(last, fup_next, fup) - f)
                fy = cy[at, :] * (right(f) - f)
                fx_down = down1(fx)
                flow = fx - jnp.where(first, flux_above, fx_down) + fy - left(fy)
                t = shp[at, :] * (f - m)
                dst[at, :] = f + (flow - t) * rs[at, :]
                mat[at, :] = m + t * rm[at, :]
                fluxx[n, at, :] = fx
                fluxy[n, at, :] = fy
                moved[n, at, :] = t
                return f_next, fup_next, fx_down

            f0 = src[0:EDGE, :]
            lax.fori_loop(0, chunks, step, (f0, up1(f0), zero), unroll=2)
            for p in range(pumps):
                lr, ll, ok = place(pxs[0, p], pys[0, p])

                @pl.when(ok)
                def _(lr=lr, ll=ll, p=p, n=n, dst=dst):
                    at = pl.ds(lr, 1)
                    dst[at, :] += jnp.where(one_lane == ll, prs[n, p], 0.0) * rs[at, :]

        for n in reversed(range(steps)):
            opening, closing = n == steps - 1, n == 0

            def load(at, n=n):
                a = adj[at, :] + (count[at, :] * frac[n + 1, at, :] - seen[n, at, :])
                return a, a * rs[at, :]

            def back(k, carry, n=n, opening=opening, closing=closing, load=load):
                a, s, sup, flux_above, prod_above = carry
                at = at_of(k)
                a_next, s_next = load(next_of(k))
                sup_next = up1(s_next)
                sx = cx[at, :] * (jnp.where(last, sup_next, sup) - s)
                sy = cy[at, :] * (right(s) - s)
                sx_down = down1(sx)
                flow = sx - jnp.where(first, flux_above, sx_down) + sy - left(sy)
                am = adm[at, :]
                q = am * rm[at, :] - s
                swap = shp[at, :] * q
                gx = fluxx[n, at, :] * sx
                gy = fluxy[n, at, :] * sy
                gs = moved[n, at, :] * q
                if not opening:
                    gx += px_[at, :]
                    gy += py_[at, :]
                    gs += gs_[at, :]
                a_new = a + flow + swap
                am_new = am - swap
                adj[at, :] = a_new
                adm[at, :] = am_new
                if closing:
                    gx_down = down1(gx)
                    total = gx + jnp.where(first, prod_above, gx_down) + gy + left(gy)
                    grow = row0 + k * EDGE + sub
                    inside = (grow >= 0) & (grow < total_rows) & col_in_grid
                    grad[0, at, :] = jnp.where(inside, -0.5 * res[at, :] * total, 0.0)
                    grad[1, at, :] = jnp.where(inside, gs, 0.0)
                else:
                    gx_down = prod_above
                    px_[at, :] = gx
                    py_[at, :] = gy
                    gs_[at, :] = gs
                return a_next, s_next, sup_next, sx_down, gx_down

            a0, s0 = load(pl.ds(0, EDGE))
            lax.fori_loop(0, chunks, back, (a0, s0, up1(s0), zero, zero))

        out_copies = [
            pltpu.make_async_copy(
                adj.at[pl.ds(EDGE, tile_rows), pl.ds(0, tile_cols)], frac_out, mid_sem.at[0]
            ),
            pltpu.make_async_copy(
                adm.at[pl.ds(EDGE, tile_rows), pl.ds(0, tile_cols)], mat_out, mid_sem.at[1]
            ),
        ]
        for copy in out_copies:
            copy.start()

        def blur(source, q, k, g, gup, above):
            g_next = source[q, next_of(k), :]
            gup_next = up1(g_next)
            g_down = down1(g)
            around = jnp.where(last, gup_next, gup) + jnp.where(first, above, g_down)
            around = around + left(g) + right(g)
            return g + BLEND * (around - 4.0 * g), (g_next, gup_next, g_down)

        for q in range(2):

            def first_pass(k, carry, q=q):
                value, carry = blur(grad, q, k, *carry)
                grow = row0 + k * EDGE + sub
                inside = (grow >= 0) & (grow < total_rows) & col_in_grid
                grad2[q, at_of(k), :] = jnp.where(inside, value, 0.0)
                return carry

            g0 = grad[q, 0:EDGE, :]
            lax.fori_loop(0, chunks, first_pass, (g0, up1(g0), zero), unroll=2)

            def second_pass(k, carry, q=q):
                value, carry = blur(grad2, q, k, *carry)
                at = pl.ds(pl.multiple_of((k - 1) * EDGE, EDGE), EDGE)
                smooth_out[q, at, :] = value[:, 0:tile_cols]
                return carry

            g0 = grad2[q, EDGE : 2 * EDGE, :]
            lax.fori_loop(
                1,
                chunks - 1,
                second_pass,
                (g0, up1(g0), down1(grad2[q, 0:EDGE, :])),
                unroll=2,
            )
        for copy in out_copies:
            copy.wait()

    smem = pl.BlockSpec(memory_space=pltpu.SMEM)
    hbm = pl.BlockSpec(memory_space=pl.ANY)
    big = (rows, cols)
    return pl.pallas_call(
        kernel,
        out_shape=[
            jax.ShapeDtypeStruct((2, tile_rows, tile_cols), f32),
            jax.ShapeDtypeStruct((tile_rows, tile_cols), f32),
            jax.ShapeDtypeStruct((tile_rows, tile_cols), f32),
        ],
        in_specs=[smem] * 7 + [hbm] * (FIELDS + nxr + nyr + nxr * nyr),
        out_specs=[pl.BlockSpec(memory_space=pltpu.VMEM), hbm, hbm],
        scratch_shapes=[
            pltpu.VMEM((FIELDS,) + big, f32),
            pltpu.VMEM((tile_rows, tile_cols), jnp.int32),
            pltpu.VMEM((max(nyr, 1), half, LANES), f32),
            pltpu.VMEM((max(nxr * nyr, 1), EDGE, LANES), f32),
            pltpu.VMEM((EDGE, LANES), f32),
            pltpu.VMEM(big, f32),
            pltpu.VMEM(big, f32),
            pltpu.VMEM(big, f32),
            pltpu.VMEM(big, f32),
            pltpu.VMEM((steps,) + big, f32),
            pltpu.VMEM((steps + 1,) + big, f32),
            pltpu.VMEM((steps,) + big, f32),
            pltpu.VMEM((steps,) + big, f32),
            pltpu.VMEM((steps,) + big, f32),
            pltpu.VMEM(big, f32),
            pltpu.VMEM(big, f32),
            pltpu.VMEM(big, f32),
            pltpu.VMEM((2,) + big, f32),
            pltpu.VMEM((2,) + big, f32),
            pltpu.SemaphoreType.DMA((FIELDS,)),
            pltpu.SemaphoreType.DMA((nxr, FIELDS)),
            pltpu.SemaphoreType.DMA((max(nyr, 1),)),
            pltpu.SemaphoreType.DMA((max(nxr * nyr, 1),)),
        ],
        name="window",
    )(*scalars, *fields, *row_in, *col_in, *corner_in)


def on_device(
    log_cond,
    log_shape,
    zone_ids,
    storage,
    pump_x,
    pump_y,
    pump_rates,
    obs_x,
    obs_y,
    observed,
    frac_start,
    matrix_start,
    frac_end,
    matrix_end,
):
    nx, ny = lax.axis_size("tx"), lax.axis_size("ty")
    xr, yr = rounds_of(nx), rounds_of(ny)
    fields = (
        log_cond,
        log_shape,
        zone_ids,
        frac_start[0],
        matrix_start[0],
        frac_end[0],
        matrix_end[0],
    )
    row_out, col_out, corner_out = pack(fields, xr, yr)
    col_in = [lax.ppermute(m, "ty", pairs_of(ny, py)) for m, py in zip(col_out, yr)]
    row_in = [lax.ppermute(m, "tx", pairs_of(nx, px)) for m, px in zip(row_out, xr)]
    corner_in = [
        lax.ppermute(corner_out[i * len(yr) + j], ("tx", "ty"), corner_pairs(nx, ny, px, py))
        for i, px in enumerate(xr)
        for j, py in enumerate(yr)
    ]
    scalars = (storage, pump_x, pump_y, pump_rates[0], obs_x, obs_y, observed[0])
    smoothed, fracture_adj, matrix_adj = window(
        fields, scalars, row_in, col_in, corner_in, xr, yr, nx, ny
    )
    tests = lax.axis_size("test")
    summed = smoothed
    if tests == 2:
        summed = smoothed + lax.ppermute(smoothed, "test", [(0, 1), (1, 0)])
    else:
        summed = lax.psum(smoothed, "test")
    return (summed[0], summed[1], fracture_adj[None], matrix_adj[None])


def solution(mesh):
    placed = (
        P(("inv", "tx"), "ty"),
        P(("inv", "tx"), "ty"),
        P(("inv", "tx"), "ty"),
        P("inv", None),
        P(("inv", "test"), None),
        P(("inv", "test"), None),
        P(("inv", "test"), None, None),
        P("inv"),
        P("inv"),
        P(("inv", "test"), None, None),
        P(("inv", "test"), "tx", "ty"),
        P(("inv", "test"), "tx", "ty"),
        P(("inv", "test"), "tx", "ty"),
        P(("inv", "test"), "tx", "ty"),
    )
    return jax.shard_map(
        on_device,
        mesh=mesh,
        in_specs=placed,
        out_specs=(
            P(("inv", "tx"), "ty"),
            P(("inv", "tx"), "ty"),
            P(("inv", "test"), "tx", "ty"),
            P(("inv", "test"), "tx", "ty"),
        ),
        check_vma=False,
    )
```

time: 220 us -> 66.4 us (0.30)
  other arithmetic: 81 us -> 1.17 us
  Pallas kernels: 0 us -> 46.7 us
  waiting for transfers between devices: 43 us -> 2.31 us
  local copies, waits for them, and re-layouts: 43.8 us -> 3.44 us
  starting transfers between devices: 29.6 us -> 10.4 us
  between operations: 20.8 us -> 2.07 us
    pallas_call x0 -> x2, Pallas kernels: none -> 46.7 us  [the longest x1 43.4 us: window(): pl.pallas_call(kernel, out_shape=[jax.ShapeDtypeStruct((2, tile_rows, til...]
    scatter-add x5 -> x0, other arithmetic: 28.4 us -> none  [the longest x3 27.2 us: inject(): return adjoint_field.at[:, obs_lx, obs_ly].add(mismatch)]
    ppermute x12 -> x6, waiting for transfers between devices: 25.9 us -> 2.31 us  [the longest x1 2.3 us: on_device(): summed = smoothed + lax.ppermute(smoothed, 'test', [(0, 1), (1, 0)])]
    ppermute x12 -> x6, starting transfers between devices: 29.6 us -> 10.4 us  [the longest x2 5.08 us: on_device(): lax.ppermute(corner_out[i * len(yr) + j], ('tx', 'ty'), corner_pairs(nx,...]
    unnamed x118 -> x19, local copies, waits for them, and re-layouts: 20.3 us -> 1.9 us
    psum x1 -> x0, waiting for transfers between devices: 17.1 us -> none  [on_device(): summed = lax.psum(stacked, 'test')]
    sub x5 -> x0, other arithmetic: 12.3 us -> none  [the longest x3 7.45 us: margin_window(): flow_sum(zero_border(fracture), conductances) - transfer + source]
    add x7 -> x1, other arithmetic: 13.1 us -> 1.17 us  [on_device(): summed = smoothed + lax.ppermute(smoothed, 'test', [(0, 1), (1, 0)])]
  transfers between devices with their start and end apart: 13 -> 6, of which waited for: 9 -> 1; matrix products, arithmetic and copies ran while one was open for 4% -> 2% of each run, Pallas kernels for 0% -> 0%
where the time goes in v1:
time: 66.4 us; the launch traced here: 66.1 us
  Pallas kernels  46.7 us (70%)
  starting transfers between devices  10.4 us (16%)
  local copies, waits for them, and re-layouts  3.44 us (5%)
  waiting for transfers between devices  2.31 us (3%)
  between operations  2.07 us (3%)
  other arithmetic  1.17 us (2%)
    pallas_call x1, Pallas kernels, window(): pl.pallas_call(kernel, out_shape=[jax.ShapeDtypeStruct((2, tile_rows, til...  43.4 us
    ppermute x2, starting transfers between devices, on_device(): lax.ppermute(corner_out[i * len(yr) + j], ('tx', 'ty'), corner_pairs(nx,...  5.08 us
    pallas_call x1, Pallas kernels, pack(): pl.pallas_call(kernel, out_shape=outs, in_specs=[pl.BlockSpec(memory_spac...  3.26 us
    ppermute x1, starting transfers between devices, on_device(): lax.ppermute(m, 'ty', pairs_of(ny, py))  3.03 us
    ppermute x1, waiting for transfers between devices, on_device(): summed = smoothed + lax.ppermute(smoothed, 'test', [(0, 1), (1, 0)])  2.3 us
    ppermute x2, starting transfers between devices, on_device(): lax.ppermute(m, 'tx', pairs_of(nx, px))  2.23 us
    unnamed x19, local copies, waits for them, and re-layouts  1.9 us
  transfers between devices with their start and end apart: 6, of which 1 were waited for; matrix products, arithmetic and copies ran while one was open for 2% of the time, Pallas kernels for 0%

profile of v1, /device:TPU:0, one launch (start us, length us, event | category | flops | bytes accessed | tf_op | source)
XLA Modules:
  0.0 66.1 jit_solution(14639576703601609711)
XLA Ops:
  0.6 3.3 %pack.1 = (f32[56,256]{1,0:T(8,128)}, f32[56,256]{1,0:T(8,128)}, f32[160,128]{1,0:T(8,128)}, f32[8,128]{1,0:T(8,128)}, f32[8,128]{1,0:T(8,128)}) custom-call(f32[320,256]{1,0:T(8,128)} %refs_7_.1, f32[320,256]{1,0:T(8,128)} %refs_8_.1, s32[320,256]{1,0:T(8,128)} %refs_9_.1, f32[320,256]{1,0:T(8,128)} %bitcast.14, f32[320,256]{1,0:T(8,128)} %bitcast.16, ...), custom_call_target="tpu_custom_call" | custom-call | tf_op jit(solution)/shard_map/pack/pallas_call | solution.py:127
  3.9 0.0 copy-start.8
  3.9 0.0 copy-start.7
  3.9 3.0 %collective-permute-start.2 = (f32[160,128]{1,0:T(8,128)}, f32[160,128]{1,0:T(8,128)S(1)}, u32[]{:S(2)}, u32[]{:S(2)}) collective-permute-start(f32[160,128]{1,0:T(8,128)} %get-tuple-element.14), channel_id=1, source_target_pairs={{0,1},{1,0},{2,3},{3,2},{4,5},{5,4},{6,7},{7,6},{8,9},{9,8},{10,11... | collective-permute-start | bytes 245768 | tf_op jit(solution)/shard_map/ppermute | solution.py:540
  6.9 1.6 %collective-permute-start = (f32[56,256]{1,0:T(8,128)}, f32[56,256]{1,0:T(8,128)S(1)}, u32[]{:S(2)}, u32[]{:S(2)}) collective-permute-start(f32[56,256]{1,0:T(8,128)} %get-tuple-element.12), channel_id=1, source_target_pairs={{0,2},{2,0},{4,6},{6,4},{1,3},{3,1},{5,7},{7,5},{8,10},{10,8},{12,... | collective-permute-start | bytes 172040 | tf_op jit(solution)/shard_map/ppermute | solution.py:541
  8.5 0.7 collective-permute-start.1
  9.2 0.0 copy-done.8
  9.2 4.4 %collective-permute-start.3 = (f32[8,128]{1,0:T(8,128)S(1)}, f32[8,128]{1,0:T(8,128)S(1)}, u32[]{:S(2)}, u32[]{:S(2)}) collective-permute-start(f32[8,128]{1,0:T(8,128)S(1)} %copy-done.8), channel_id=1, source_target_pairs={{0,3},{1,2},{2,1},{3,0},{4,7},{5,6},{6,5},{7,4},{8,11},{9,10},{10,... | collective-permute-start | bytes 12296 | tf_op jit(solution)/shard_map/ppermute | solution.py:543
  13.6 0.0 copy-done.7
  13.6 0.7 collective-permute-start.4
  15.6 0.0 copy-start.6
  15.6 0.6 copy-done.6
  16.2 0.0 copy-start.5
  16.2 0.7 %copy.18.refs_3_ = f32[3,1]{1,0:T(4,128)} copy(f32[3,1]{0,1:T(1,128)S(1)} %bitcast.23) | data formatting | bytes 24 | tf_op jit(solution)/shard_map/squeeze | solution.py:547
  16.9 0.0 copy-done.5
  16.9 0.6 copy.21
  17.5 0.0 collective-permute-done.3.refs_17_
  17.5 0.0 copy-start.3
  17.5 0.0 collective-permute-done.4.refs_18_
  17.5 0.0 copy-start.4
  17.5 0.0 collective-permute-done.refs_14_
  17.5 0.0 copy-start.1
  17.6 0.0 collective-permute-done.1.refs_15_
  17.6 0.0 copy-start.2
  17.6 0.0 collective-permute-done.2.refs_16_
  17.6 0.0 copy-start
  17.6 0.5 copy-done.3
  18.1 0.0 copy-done.4
  18.1 0.1 copy-done.1
  18.2 0.0 copy-done.2
  18.2 0.0 copy-done
  18.2 43.4 %window.1 = (f32[2,320,256]{2,1,0:T(8,128)}, f32[320,256]{1,0:T(8,128)}, f32[320,256]{1,0:T(8,128)}) custom-call(f32[2,8]{1,0:T(2,128)} %refs_0_.3, s32[1,1]{1,0:T(1,128)S(6)} %copy.22.refs_1_, s32[1,1]{1,0:T(1,128)S(6)} %copy.23.refs_2_, f32[3,1]{1,0:T(4,128)} %copy.18.refs_3_, s32[64]{0:T(128)} %refs_4_.1, s32[64]{0:T(128)} %refs_5_.1, f32[3,64]{1,0:T(4,128)} %bitcast.22, ...), custom_call_target="tpu_custom_call" | custom-call | tf_op jit(solution)/shard_map/window/pallas_call | solution.py:474
  61.7 0.1 collective-permute-start.5
  61.8 2.3 %collective-permute-done.5 = f32[2,320,256]{2,1,0:T(8,128)S(1)} collective-permute-done((f32[2,320,256]{2,1,0:T(8,128)}, f32[2,320,256]{2,1,0:T(8,128)S(1)}, u32[]{:S(2)}, u32[]{:S(2)}) %collective-permute-start.5) | collective-permute-done | bytes 655392 | tf_op jit(solution)/shard_map/ppermute | solution.py:554
  64.1 1.2 %add.3 = f32[2,320,256]{2,1,0:T(8,128)S(1)} add(f32[2,320,256]{2,1,0:T(8,128)} %get-tuple-element.17, f32[2,320,256]{2,1,0:T(8,128)S(1)} %collective-permute-done.5) | non-fusion elementwise | flops 163840 | bytes 1966080 | tf_op jit(solution)/shard_map/add | solution.py:554
  65.2 0.9 %slice_bitcast_fusion = (f32[320,256]{1,0:T(8,128)}, f32[320,256]{1,0:T(8,128)}) fusion(f32[2,320,256]{2,1,0:T(8,128)S(1)} %add.3), kind=kLoop, calls=%fused_computation | loop fusion | bytes 1310720 | tf_op jit(solution)/shard_map/squeeze | solution.py:557
Async XLA Ops:
  3.9 5.3 %copy-start.8 = (f32[8,128]{1,0:T(8,128)S(1)}, f32[8,128]{1,0:T(8,128)}, u32[]{:S(2)}) copy-start(f32[8,128]{1,0:T(8,128)} %get-tuple-element.15) | copy-start | bytes 12292
  3.9 9.7 %copy-start.7 = (f32[8,128]{1,0:T(8,128)S(1)}, f32[8,128]{1,0:T(8,128)}, u32[]{:S(2)}) copy-start(f32[8,128]{1,0:T(8,128)} %get-tuple-element.16) | copy-start | bytes 12292
  3.9 13.7 %collective-permute-start.2 = (f32[160,128]{1,0:T(8,128)}, f32[160,128]{1,0:T(8,128)S(1)}, u32[]{:S(2)}, u32[]{:S(2)}) collective-permute-start(f32[160,128]{1,0:T(8,128)} %get-tuple-element.14), channel_id=1, source_target_pairs={{0,1},{1,0},{2,3},{3,2},{4,5},{5,4},{6,7},{7,6},{8,9},{9,8},{10,11... | collective-permute-start | bytes 245768 | tf_op jit(solution)/shard_map/ppermute | solution.py:540
  6.9 10.6 %collective-permute-start = (f32[56,256]{1,0:T(8,128)}, f32[56,256]{1,0:T(8,128)S(1)}, u32[]{:S(2)}, u32[]{:S(2)}) collective-permute-start(f32[56,256]{1,0:T(8,128)} %get-tuple-element.12), channel_id=1, source_target_pairs={{0,2},{2,0},{4,6},{6,4},{1,3},{3,1},{5,7},{7,5},{8,10},{10,8},{12,... | collective-permute-start | bytes 172040 | tf_op jit(solution)/shard_map/ppermute | solution.py:541
  8.5 9.0 %collective-permute-start.1 = (f32[56,256]{1,0:T(8,128)}, f32[56,256]{1,0:T(8,128)S(1)}, u32[]{:S(2)}, u32[]{:S(2)}) collective-permute-start(f32[56,256]{1,0:T(8,128)} %get-tuple-element.13), channel_id=1, source_target_pairs={{2,4},{4,2},{3,5},{5,3},{10,12},{12,10},{11,13},{13,11},{18,20},{2... | collective-permute-start | bytes 172040 | tf_op jit(solution)/shard_map/ppermute | solution.py:541
  9.2 8.3 %collective-permute-start.3 = (f32[8,128]{1,0:T(8,128)S(1)}, f32[8,128]{1,0:T(8,128)S(1)}, u32[]{:S(2)}, u32[]{:S(2)}) collective-permute-start(f32[8,128]{1,0:T(8,128)S(1)} %copy-done.8), channel_id=1, source_target_pairs={{0,3},{1,2},{2,1},{3,0},{4,7},{5,6},{6,5},{7,4},{8,11},{9,10},{10,... | collective-permute-start | bytes 12296 | tf_op jit(solution)/shard_map/ppermute | solution.py:543
  13.6 3.9 %collective-permute-start.4 = (f32[8,128]{1,0:T(8,128)S(1)}, f32[8,128]{1,0:T(8,128)S(1)}, u32[]{:S(2)}, u32[]{:S(2)}) collective-permute-start(f32[8,128]{1,0:T(8,128)S(1)} %copy-done.7), channel_id=1, source_target_pairs={{2,5},{3,4},{4,3},{5,2},{10,13},{11,12},{12,11},{13,10},{18,21},{1... | collective-permute-start | bytes 12296 | tf_op jit(solution)/shard_map/ppermute | solution.py:543
  15.6 0.7 copy-start.6
  16.2 0.7 %copy-start.5 = (f32[1,3,64]{2,0,1:T(1,128)S(1)}, f32[1,3,64]{2,0,1:T(1,128)}, u32[]{:S(2)}) copy-start(f32[1,3,64]{2,0,1:T(1,128)} %param.23) | copy-start | bytes 2308
  17.5 0.6 copy-start.3
  17.5 0.6 copy-start.4
  17.5 0.6 copy-start.1
  17.6 0.6 copy-start.2
  17.6 0.6 copy-start
  61.7 2.4 %collective-permute-start.5 = (f32[2,320,256]{2,1,0:T(8,128)}, f32[2,320,256]{2,1,0:T(8,128)S(1)}, u32[]{:S(2)}, u32[]{:S(2)}) collective-permute-start(f32[2,320,256]{2,1,0:T(8,128)} %get-tuple-element.17), channel_id=1, source_target_pairs={{0,8},{8,0},{1,9},{9,1},{2,10},{10,2},{3,11},{11,3},{4,12},{12,4},... | collective-permute-start | bytes 1966088 | tf_op jit(solution)/shard_map/ppermute | solution.py:554

commit v2 on v1

--- a/solution.py
+++ b/solution.py
@@ -119,7 +119,7 @@
                 col_out[j][pl.ds(pl.multiple_of(k * EDGE, EDGE), EDGE), :] = total
                 return carry
 
-            lax.fori_loop(0, half // EDGE, body, 0, unroll=2)
+            lax.fori_loop(0, half // EDGE, body, 0, unroll=half // EDGE)
 
     outs = [jax.ShapeDtypeStruct((EDGE * FIELDS, tile_cols), jnp.float32)] * nxr
     outs += [jax.ShapeDtypeStruct((half, LANES), jnp.float32)] * nyr
@@ -256,7 +256,7 @@
             wide[2, at, 0:tile_cols] = zone_mid[pl.ds(pl.multiple_of(k * EDGE, EDGE), EDGE), :].astype(f32)
             return carry
 
-        lax.fori_loop(0, tile_rows // EDGE, widen, 0, unroll=4)
+        lax.fori_loop(0, tile_rows // EDGE, widen, 0, unroll=tile_rows // EDGE)
         edge_lane = lane_iota(EDGE, LANES)
         side = []
         for py in yr:
@@ -285,7 +285,7 @@
                     put_edge(f, at, edge_of(messages, EDGE * f + 64 * h))
                 return carry
 
-            lax.fori_loop(0, half // EDGE, fringe, 0, unroll=2)
+            lax.fori_loop(0, half // EDGE, fringe, 0, unroll=half // EDGE)
         for i in range(nxr):
             messages = [cornerbuf[i * nyr + j] for j in range(nyr)]
             for f in range(FIELDS):
@@ -327,7 +327,7 @@
             rm[at, :] = b
             return carry
 
-        lax.fori_loop(0, chunks, prepare, 0)
+        lax.fori_loop(0, chunks, prepare, 0, unroll=42)
 
         def links(k, carry):
             at = at_of(k)
@@ -340,7 +340,7 @@
             cy[at, :] = jnp.where(col_face, 2.0 / (here + beside), 0.0)
             return carry
 
-        lax.fori_loop(0, chunks, links, 0, unroll=2)
+        lax.fori_loop(0, chunks, links, 0, unroll=42)
 
         for n in range(steps):
             src, dst = frac.at[n], frac.at[n + 1]
@@ -364,7 +364,7 @@
                 return f_next, fup_next, fx_down
 
             f0 = src[0:EDGE, :]
-            lax.fori_loop(0, chunks, step, (f0, up1(f0), zero), unroll=2)
+            lax.fori_loop(0, chunks, step, (f0, up1(f0), zero), unroll=42)
             for p in range(pumps):
                 lr, ll, ok = place(pxs[0, p], pys[0, p])
 
@@ -418,7 +418,7 @@
                 return a_next, s_next, sup_next, sx_down, gx_down
 
             a0, s0 = load(pl.ds(0, EDGE))
-            lax.fori_loop(0, chunks, back, (a0, s0, up1(s0), zero, zero))
+            lax.fori_loop(0, chunks, back, (a0, s0, up1(s0), zero, zero), unroll=42)
 
         out_copies = [
             pltpu.make_async_copy(
@@ -449,7 +449,7 @@
                 return carry
 
             g0 = grad[q, 0:EDGE, :]
-            lax.fori_loop(0, chunks, first_pass, (g0, up1(g0), zero), unroll=2)
+            lax.fori_loop(0, chunks, first_pass, (g0, up1(g0), zero), unroll=42)
 
             def second_pass(k, carry, q=q):
                 value, carry = blur(grad2, q, k, *carry)
@@ -463,7 +463,7 @@
                 chunks - 1,
                 second_pass,
                 (g0, up1(g0), down1(grad2[q, 0:EDGE, :])),
-                unroll=2,
+                unroll=40,
             )
         for copy in out_copies:
             copy.wait()

time: 66.4 us -> 42.4 us (0.64)
  Pallas kernels: 46.7 us -> 22.7 us
    pallas_call x1, Pallas kernels: 43.4 us -> 20 us  [window(): pl.pallas_call(kernel, out_shape=[jax.ShapeDtypeStruct((2, tile_rows, til...]
  transfers between devices with their start and end apart: 6 -> 6, of which waited for: 1 -> 1; matrix products, arithmetic and copies ran while one was open for 2% -> 3% of each run, Pallas kernels for 0% -> 0%
where the time goes in v2:
time: 42.4 us; the launch traced here: 42.1 us
  Pallas kernels  22.7 us (54%)
  starting transfers between devices  10.4 us (25%)
  local copies, waits for them, and re-layouts  3.44 us (8%)
  waiting for transfers between devices  2.31 us (5%)
  between operations  2.07 us (5%)
  other arithmetic  1.17 us (3%)
    pallas_call x1, Pallas kernels, window(): pl.pallas_call(kernel, out_shape=[jax.ShapeDtypeStruct((2, tile_rows, til...  20 us
    ppermute x2, starting transfers between devices, on_device(): lax.ppermute(corner_out[i * len(yr) + j], ('tx', 'ty'), corner_pairs(nx,...  5.08 us
    ppermute x1, starting transfers between devices, on_device(): lax.ppermute(m, 'ty', pairs_of(ny, py))  3.03 us
    pallas_call x1, Pallas kernels, pack(): pl.pallas_call(kernel, out_shape=outs, in_specs=[pl.BlockSpec(memory_spac...  2.64 us
    ppermute x1, waiting for transfers between devices, on_device(): summed = smoothed + lax.ppermute(smoothed, 'test', [(0, 1), (1, 0)])  2.3 us
    ppermute x2, starting transfers between devices, on_device(): lax.ppermute(m, 'tx', pairs_of(nx, px))  2.23 us
    unnamed x19, local copies, waits for them, and re-layouts  1.9 us
    add x1, other arithmetic, on_device(): summed = smoothed + lax.ppermute(smoothed, 'test', [(0, 1), (1, 0)])  1.17 us
  transfers between devices with their start and end apart: 6, of which 1 were waited for; matrix products, arithmetic and copies ran while one was open for 3% of the time, Pallas kernels for 0%

profile of v2, /device:TPU:0, one launch (start us, length us, event | category | flops | bytes accessed | tf_op | source)
XLA Modules:
  0.0 42.1 jit_solution(16571938452206887573)
XLA Ops:
  0.6 2.6 %pack.1 = (f32[56,256]{1,0:T(8,128)}, f32[56,256]{1,0:T(8,128)}, f32[160,128]{1,0:T(8,128)}, f32[8,128]{1,0:T(8,128)}, f32[8,128]{1,0:T(8,128)}) custom-call(f32[320,256]{1,0:T(8,128)} %refs_7_.1, f32[320,256]{1,0:T(8,128)} %refs_8_.1, s32[320,256]{1,0:T(8,128)} %refs_9_.1, f32[320,256]{1,0:T(8,128)} %bitcast.14, f32[320,256]{1,0:T(8,128)} %bitcast.16, ...), custom_call_target="tpu_custom_call" | custom-call | tf_op jit(solution)/shard_map/pack/pallas_call | solution.py:127
  3.3 0.0 copy-start.8
  3.3 0.0 copy-start.7
  3.3 3.0 %collective-permute-start.2 = (f32[160,128]{1,0:T(8,128)}, f32[160,128]{1,0:T(8,128)S(1)}, u32[]{:S(2)}, u32[]{:S(2)}) collective-permute-start(f32[160,128]{1,0:T(8,128)} %get-tuple-element.14), channel_id=1, source_target_pairs={{0,1},{1,0},{2,3},{3,2},{4,5},{5,4},{6,7},{7,6},{8,9},{9,8},{10,11... | collective-permute-start | bytes 245768 | tf_op jit(solution)/shard_map/ppermute | solution.py:540
  6.3 1.6 %collective-permute-start = (f32[56,256]{1,0:T(8,128)}, f32[56,256]{1,0:T(8,128)S(1)}, u32[]{:S(2)}, u32[]{:S(2)}) collective-permute-start(f32[56,256]{1,0:T(8,128)} %get-tuple-element.12), channel_id=1, source_target_pairs={{0,2},{2,0},{4,6},{6,4},{1,3},{3,1},{5,7},{7,5},{8,10},{10,8},{12,... | collective-permute-start | bytes 172040 | tf_op jit(solution)/shard_map/ppermute | solution.py:541
  7.9 0.7 %collective-permute-start.1 = (f32[56,256]{1,0:T(8,128)}, f32[56,256]{1,0:T(8,128)S(1)}, u32[]{:S(2)}, u32[]{:S(2)}) collective-permute-start(f32[56,256]{1,0:T(8,128)} %get-tuple-element.13), channel_id=1, source_target_pairs={{2,4},{4,2},{3,5},{5,3},{10,12},{12,10},{11,13},{13,11},{18,20},{2... | collective-permute-start | bytes 172040 | tf_op jit(solution)/shard_map/ppermute | solution.py:541
  8.6 0.0 copy-done.8
  8.6 4.4 %collective-permute-start.3 = (f32[8,128]{1,0:T(8,128)S(1)}, f32[8,128]{1,0:T(8,128)S(1)}, u32[]{:S(2)}, u32[]{:S(2)}) collective-permute-start(f32[8,128]{1,0:T(8,128)S(1)} %copy-done.8), channel_id=1, source_target_pairs={{0,3},{1,2},{2,1},{3,0},{4,7},{5,6},{6,5},{7,4},{8,11},{9,10},{10,... | collective-permute-start | bytes 12296 | tf_op jit(solution)/shard_map/ppermute | solution.py:543
  13.0 0.0 copy-done.7
  13.0 0.7 %collective-permute-start.4 = (f32[8,128]{1,0:T(8,128)S(1)}, f32[8,128]{1,0:T(8,128)S(1)}, u32[]{:S(2)}, u32[]{:S(2)}) collective-permute-start(f32[8,128]{1,0:T(8,128)S(1)} %copy-done.7), channel_id=1, source_target_pairs={{2,5},{3,4},{4,3},{5,2},{10,13},{11,12},{12,11},{13,10},{18,21},{1... | collective-permute-start | bytes 12296 | tf_op jit(solution)/shard_map/ppermute | solution.py:543
  15.0 0.0 copy-start.6
  15.0 0.6 %copy-done.6 = f32[1,3,1]{1,2,0:T(1,128)S(1)} copy-done((f32[1,3,1]{1,2,0:T(1,128)S(1)}, f32[1,3,1]{1,2,0:T(1,128)}, u32[]{:S(2)}) %copy-start.6) | copy-done | bytes 36
  15.6 0.0 copy-start.5
  15.6 0.7 %copy.18.refs_3_ = f32[3,1]{1,0:T(4,128)} copy(f32[3,1]{0,1:T(1,128)S(1)} %bitcast.23) | data formatting | bytes 24 | tf_op jit(solution)/shard_map/squeeze | solution.py:547
  16.3 0.0 copy-done.5
  16.3 0.6 %copy.21 = f32[1,3,64]{2,1,0:T(4,128)} copy(f32[1,3,64]{2,0,1:T(1,128)S(1)} %copy-done.5) | data formatting | bytes 1536
  16.9 0.0 collective-permute-done.3.refs_17_
  16.9 0.0 copy-start.3
  16.9 0.0 collective-permute-done.4.refs_18_
  16.9 0.0 copy-start.4
  16.9 0.0 collective-permute-done.refs_14_
  16.9 0.0 copy-start.1
  16.9 0.0 collective-permute-done.1.refs_15_
  17.0 0.0 copy-start.2
  17.0 0.0 collective-permute-done.2.refs_16_
  17.0 0.0 copy-start
  17.0 0.5 %copy-done.3 = f32[8,128]{1,0:T(8,128)} copy-done((f32[8,128]{1,0:T(8,128)}, f32[8,128]{1,0:T(8,128)S(1)}, u32[]{:S(2)}) %copy-start.3) | copy-done | bytes 4120
  17.5 0.0 copy-done.4
  17.5 0.1 copy-done.1
  17.6 0.0 copy-done.2
  17.6 0.0 copy-done
  17.6 20.0 %window.1 = (f32[2,320,256]{2,1,0:T(8,128)}, f32[320,256]{1,0:T(8,128)}, f32[320,256]{1,0:T(8,128)}) custom-call(f32[2,8]{1,0:T(2,128)} %refs_0_.3, s32[1,1]{1,0:T(1,128)S(6)} %copy.22.refs_1_, s32[1,1]{1,0:T(1,128)S(6)} %copy.23.refs_2_, f32[3,1]{1,0:T(4,128)} %copy.18.refs_3_, s32[64]{0:T(128)} %refs_4_.1, s32[64]{0:T(128)} %refs_5_.1, f32[3,64]{1,0:T(4,128)} %bitcast.22, ...), custom_call_target="tpu_custom_call" | custom-call | tf_op jit(solution)/shard_map/window/pallas_call | solution.py:474
  37.6 0.1 collective-permute-start.5
  37.7 2.3 %collective-permute-done.5 = f32[2,320,256]{2,1,0:T(8,128)S(1)} collective-permute-done((f32[2,320,256]{2,1,0:T(8,128)}, f32[2,320,256]{2,1,0:T(8,128)S(1)}, u32[]{:S(2)}, u32[]{:S(2)}) %collective-permute-start.5) | collective-permute-done | bytes 655392 | tf_op jit(solution)/shard_map/ppermute | solution.py:554
  40.0 1.2 %add.3 = f32[2,320,256]{2,1,0:T(8,128)S(1)} add(f32[2,320,256]{2,1,0:T(8,128)} %get-tuple-element.17, f32[2,320,256]{2,1,0:T(8,128)S(1)} %collective-permute-done.5) | non-fusion elementwise | flops 163840 | bytes 1966080 | tf_op jit(solution)/shard_map/add | solution.py:554
  41.2 0.9 %slice_bitcast_fusion = (f32[320,256]{1,0:T(8,128)}, f32[320,256]{1,0:T(8,128)}) fusion(f32[2,320,256]{2,1,0:T(8,128)S(1)} %add.3), kind=kLoop, calls=%fused_computation | loop fusion | bytes 1310720 | tf_op jit(solution)/shard_map/squeeze | solution.py:557
Async XLA Ops:
  3.3 5.3 %copy-start.8 = (f32[8,128]{1,0:T(8,128)S(1)}, f32[8,128]{1,0:T(8,128)}, u32[]{:S(2)}) copy-start(f32[8,128]{1,0:T(8,128)} %get-tuple-element.15) | copy-start | bytes 12292
  3.3 9.7 %copy-start.7 = (f32[8,128]{1,0:T(8,128)S(1)}, f32[8,128]{1,0:T(8,128)}, u32[]{:S(2)}) copy-start(f32[8,128]{1,0:T(8,128)} %get-tuple-element.16) | copy-start | bytes 12292
  3.3 13.7 %collective-permute-start.2 = (f32[160,128]{1,0:T(8,128)}, f32[160,128]{1,0:T(8,128)S(1)}, u32[]{:S(2)}, u32[]{:S(2)}) collective-permute-start(f32[160,128]{1,0:T(8,128)} %get-tuple-element.14), channel_id=1, source_target_pairs={{0,1},{1,0},{2,3},{3,2},{4,5},{5,4},{6,7},{7,6},{8,9},{9,8},{10,11... | collective-permute-start | bytes 245768 | tf_op jit(solution)/shard_map/ppermute | solution.py:540
  6.3 10.6 %collective-permute-start = (f32[56,256]{1,0:T(8,128)}, f32[56,256]{1,0:T(8,128)S(1)}, u32[]{:S(2)}, u32[]{:S(2)}) collective-permute-start(f32[56,256]{1,0:T(8,128)} %get-tuple-element.12), channel_id=1, source_target_pairs={{0,2},{2,0},{4,6},{6,4},{1,3},{3,1},{5,7},{7,5},{8,10},{10,8},{12,... | collective-permute-start | bytes 172040 | tf_op jit(solution)/shard_map/ppermute | solution.py:541
  7.9 9.0 %collective-permute-start.1 = (f32[56,256]{1,0:T(8,128)}, f32[56,256]{1,0:T(8,128)S(1)}, u32[]{:S(2)}, u32[]{:S(2)}) collective-permute-start(f32[56,256]{1,0:T(8,128)} %get-tuple-element.13), channel_id=1, source_target_pairs={{2,4},{4,2},{3,5},{5,3},{10,12},{12,10},{11,13},{13,11},{18,20},{2... | collective-permute-start | bytes 172040 | tf_op jit(solution)/shard_map/ppermute | solution.py:541
  8.6 8.3 %collective-permute-start.3 = (f32[8,128]{1,0:T(8,128)S(1)}, f32[8,128]{1,0:T(8,128)S(1)}, u32[]{:S(2)}, u32[]{:S(2)}) collective-permute-start(f32[8,128]{1,0:T(8,128)S(1)} %copy-done.8), channel_id=1, source_target_pairs={{0,3},{1,2},{2,1},{3,0},{4,7},{5,6},{6,5},{7,4},{8,11},{9,10},{10,... | collective-permute-start | bytes 12296 | tf_op jit(solution)/shard_map/ppermute | solution.py:543
  13.0 3.9 %collective-permute-start.4 = (f32[8,128]{1,0:T(8,128)S(1)}, f32[8,128]{1,0:T(8,128)S(1)}, u32[]{:S(2)}, u32[]{:S(2)}) collective-permute-start(f32[8,128]{1,0:T(8,128)S(1)} %copy-done.7), channel_id=1, source_target_pairs={{2,5},{3,4},{4,3},{5,2},{10,13},{11,12},{12,11},{13,10},{18,21},{1... | collective-permute-start | bytes 12296 | tf_op jit(solution)/shard_map/ppermute | solution.py:543
  15.0 0.7 %copy-start.6 = (f32[1,3,1]{1,2,0:T(1,128)S(1)}, f32[1,3,1]{1,2,0:T(1,128)}, u32[]{:S(2)}) copy-start(f32[1,3,1]{1,2,0:T(1,128)} %param.20) | copy-start | bytes 40
  15.6 0.7 %copy-start.5 = (f32[1,3,64]{2,0,1:T(1,128)S(1)}, f32[1,3,64]{2,0,1:T(1,128)}, u32[]{:S(2)}) copy-start(f32[1,3,64]{2,0,1:T(1,128)} %param.23) | copy-start | bytes 2308
  16.9 0.6 %copy-start.3 = (f32[8,128]{1,0:T(8,128)}, f32[8,128]{1,0:T(8,128)S(1)}, u32[]{:S(2)}) copy-start(f32[8,128]{1,0:T(8,128)S(1)} %collective-permute-done.3.refs_17_) | copy-start | bytes 12292
  16.9 0.6 %copy-start.4 = (f32[8,128]{1,0:T(8,128)}, f32[8,128]{1,0:T(8,128)S(1)}, u32[]{:S(2)}) copy-start(f32[8,128]{1,0:T(8,128)S(1)} %collective-permute-done.4.refs_18_) | copy-start | bytes 12292
  16.9 0.6 %copy-start.1 = (f32[56,256]{1,0:T(8,128)}, f32[56,256]{1,0:T(8,128)S(1)}, u32[]{:S(2)}) copy-start(f32[56,256]{1,0:T(8,128)S(1)} %collective-permute-done.refs_14_) | copy-start | bytes 172036
  17.0 0.6 %copy-start.2 = (f32[56,256]{1,0:T(8,128)}, f32[56,256]{1,0:T(8,128)S(1)}, u32[]{:S(2)}) copy-start(f32[56,256]{1,0:T(8,128)S(1)} %collective-permute-done.1.refs_15_) | copy-start | bytes 172036
  17.0 0.6 %copy-start = (f32[160,128]{1,0:T(8,128)}, f32[160,128]{1,0:T(8,128)S(1)}, u32[]{:S(2)}) copy-start(f32[160,128]{1,0:T(8,128)S(1)} %collective-permute-done.2.refs_16_) | copy-start | bytes 245764
  37.6 2.4 %collective-permute-start.5 = (f32[2,320,256]{2,1,0:T(8,128)}, f32[2,320,256]{2,1,0:T(8,128)S(1)}, u32[]{:S(2)}, u32[]{:S(2)}) collective-permute-start(f32[2,320,256]{2,1,0:T(8,128)} %get-tuple-element.17), channel_id=1, source_target_pairs={{0,8},{8,0},{1,9},{9,1},{2,10},{10,2},{3,11},{11,3},{4,12},{12,4},... | collective-permute-start | bytes 1966088 | tf_op jit(solution)/shard_map/ppermute | solution.py:554

commit v3 on v2

v3 whole, which is shorter than its diff:
```python
import jax
import jax.numpy as jnp
from jax import lax
from jax.experimental import pallas as pl
from jax.experimental.pallas import tpu as pltpu
from jax.sharding import PartitionSpec as P

SMOOTH = 2
EDGE = 8
LANES = 128
BLEND = 0.2
LEAD = 6
LAG = 6
FIELDS = 7


def in_vmem(x):
    return pltpu.with_memory_space_constraint(x, pltpu.VMEM)


def pairs_of(count, parity):
    found = []
    for low in range(parity, count - 1, 2):
        found += [(low, low + 1), (low + 1, low)]
    return found


def rounds_of(count):
    return [parity for parity in (0, 1) if pairs_of(count, parity)]


def partner(index, parity):
    return index + 1 if index % 2 == parity else index - 1


def corner_pairs(nx, ny, px, py):
    found = []
    for x in range(nx):
        for y in range(ny):
            there = (partner(x, px), partner(y, py))
            if 0 <= there[0] < nx and 0 <= there[1] < ny:
                found.append((x * ny + y, there[0] * ny + there[1]))
    return found


def forward_of(axis, parity):
    return lax.rem(lax.axis_index(axis), 2) == parity


def lane_iota(rows, cols):
    return lax.broadcasted_iota(jnp.int32, (rows, cols), 1)


def pack(fields, xr, yr):
    tile_rows, tile_cols = fields[0].shape
    half = tile_rows // 2
    nxr, nyr = len(xr), len(yr)

    def kernel(*refs):
        ins = refs[:FIELDS]
        row_out = refs[FIELDS : FIELDS + nxr]
        col_out = refs[FIELDS + nxr : FIELDS + nxr + nyr]
        corner_out = refs[FIELDS + nxr + nyr : FIELDS + nxr + nyr + nxr * nyr]
        rest = refs[FIELDS + nxr + nyr + nxr * nyr :]
        zone_rows, cols, zone_cols, row_sem, col_sem = rest
        row_copies = []
        for i, px in enumerate(xr):
            start = jnp.where(forward_of("tx", px), tile_rows - EDGE, 0)
            start = pl.multiple_of(start, EDGE)
            for f in range(FIELDS):
                into = zone_rows.at[i] if f == 2 else row_out[i].at[pl.ds(EDGE * f, EDGE)]
                row_copies.append(
                    pltpu.make_async_copy(
                        ins[f].at[pl.ds(start, EDGE)], into, row_sem.at[i, f]
                    )
                )
        col_copies = []
        for j, py in enumerate(yr):
            start = jnp.where(forward_of("ty", py), tile_cols - LANES, 0)
            start = pl.multiple_of(start, LANES)
            for f in range(FIELDS):
                into = zone_cols.at[j] if f == 2 else cols.at[j, f]
                col_copies.append(
                    pltpu.make_async_copy(
                        ins[f].at[:, pl.ds(start, LANES)], into, col_sem.at[j, f]
                    )
                )
        for copy in row_copies + col_copies:
            copy.start()
        for copy in row_copies:
            copy.wait()
        for i in range(nxr):
            row_out[i][2 * EDGE : 3 * EDGE, :] = zone_rows[i].astype(jnp.float32)
        slot = lane_iota(EDGE, LANES) // EDGE
        for i in range(nxr):
            for j, py in enumerate(yr):
                ahead = forward_of("ty", py)
                shift = jnp.where(ahead, 1, 0)
                total = jnp.zeros((EDGE, LANES), jnp.float32)
                for f in range(FIELDS):
                    rows = row_out[i][EDGE * f : EDGE * (f + 1), :]
                    part = jnp.where(ahead, rows[:, tile_cols - LANES :], rows[:, :LANES])
                    part = pltpu.roll(part, EDGE * f, 1)
                    want = lax.rem(f - shift + 16, 16)
                    total = jnp.where(slot == want, part, total)
                corner_out[i * nyr + j][...] = total
        for copy in col_copies:
            copy.wait()
        for j, py in enumerate(yr):
            shift = jnp.where(forward_of("ty", py), 1, 0)

            def body(k, carry):
                total = jnp.zeros((EDGE, LANES), jnp.float32)
                for h in range(2):
                    at = pl.multiple_of(k * EDGE + h * half, EDGE)
                    for f in range(FIELDS):
                        if f == 2:
                            part = zone_cols[j, pl.ds(at, EDGE), :].astype(jnp.float32)
                        else:
                            part = cols[j, f, pl.ds(at, EDGE), :]
                        amount = EDGE * f + 64 * h
                        part = pltpu.roll(part, amount, 1) if amount else part
                        want = lax.rem(f + 8 * h - shift + 16, 16)
                        total = jnp.where(slot == want, part, total)
                col_out[j][pl.ds(pl.multiple_of(k * EDGE, EDGE), EDGE), :] = total
                return carry

            lax.fori_loop(0, half // EDGE, body, 0, unroll=half // EDGE)

    outs = [pltpu.VMEM((EDGE * FIELDS, tile_cols), jnp.float32)] * nxr
    outs += [pltpu.VMEM((half, LANES), jnp.float32)] * nyr
    outs += [pltpu.VMEM((EDGE, LANES), jnp.float32)] * (nxr * nyr)
    made = pl.pallas_call(
        kernel,
        out_shape=outs,
        in_specs=[pl.BlockSpec(memory_space=pltpu.HBM)] * FIELDS,
        out_specs=[pl.BlockSpec(memory_space=pltpu.VMEM)] * len(outs),
        scratch_shapes=[
            pltpu.VMEM((nxr, EDGE, tile_cols), jnp.int32),
            pltpu.VMEM((nyr, FIELDS, tile_rows, LANES), jnp.float32),
            pltpu.VMEM((nyr, tile_rows, LANES), jnp.int32),
            pltpu.SemaphoreType.DMA((nxr, FIELDS)),
            pltpu.SemaphoreType.DMA((nyr, FIELDS)),
        ],
        name="pack",
    )(*fields)
    return made[:nxr], made[nxr : nxr + nyr], made[nxr + nyr :]


def window(fields, scalars, row_in, col_in, corner_in, xr, yr, nx, ny):
    tile_rows, tile_cols = fields[0].shape
    storage, pump_rates, spots, observed = scalars
    zones = storage.shape[1]
    pumps, steps = pump_rates.shape
    wells = observed.shape[2]
    assert 2 * steps + SMOOTH <= EDGE
    half = tile_rows // 2
    nxr, nyr = len(xr), len(yr)
    rows = tile_rows + 2 * EDGE
    chunks = rows // EDGE
    own = tile_cols // LANES
    tiles = own + 1
    f32 = jnp.float32

    def kernel(*refs):
        pos = 0

        def take(count):
            nonlocal pos
            pos += count
            return refs[pos - count : pos]

        small_in = take(4)
        ins = take(FIELDS)
        rin, cin, kin = take(nxr), take(nyr), take(nxr * nyr)
        smooth_out, frac_out, mat_out = take(3)
        (wide, zone_mid) = take(2)
        (rm, cx, cy, count, seen, frac, fluxx, fluxy, moved, scaled, flux, prod) = take(12)
        (px_, py_, gs_, grad, grad2) = take(5)
        (st, prs, spot, obs) = take(4)
        (mid_sem, small_sem) = take(2)
        res, shp, rs = wide.at[0], wide.at[1], wide.at[2]
        mat, adj, adm = wide.at[4], wide.at[5], wide.at[6]
        tx, ty = lax.axis_index("tx"), lax.axis_index("ty")

        def field(f):
            return frac.at[0] if f == 3 else wide.at[f]

        def at_of(k, shift=0):
            return slice(EDGE * (k + 1) + shift, EDGE * (k + 2) + shift)

        def get(ref, k, shift=0):
            return ref[:, at_of(k, shift), :]

        def put(ref, k, value):
            ref[:, at_of(k), :] = value

        small = [
            pltpu.make_async_copy(a, b, small_sem.at[i])
            for i, (a, b) in enumerate(zip(small_in, (st, prs, spot, obs)))
        ]
        copies = []
        for f in range(FIELDS):
            for t in range(own):
                into = zone_mid.at[t] if f == 2 else field(f).at[t, pl.ds(2 * EDGE, tile_rows)]
                copies.append(
                    pltpu.make_async_copy(
                        ins[f].at[:, pl.ds(LANES * t, LANES)], into, mid_sem.at[f, t]
                    )
                )
        tops = []
        for i, px in enumerate(xr):
            to = jnp.where(forward_of("tx", px), tile_rows + 2 * EDGE, EDGE)
            to = pl.multiple_of(to, EDGE)
            tops.append(to)
        block = (tiles, EDGE, LANES)
        zero = jnp.zeros(block, f32)
        if nxr < 2:
            for f in range(FIELDS):
                put(field(f), 0, zero)
                put(field(f), chunks - 1, zero)
        for copy in small + copies:
            copy.start()
        for ref in (
            [res, grad.at[0], grad.at[1], grad2.at[0], grad2.at[1], flux, prod]
            + [frac.at[n] for n in range(steps + 1)]
            + [fluxx.at[n] for n in range(steps)]
            + [scaled.at[n] for n in range(2)]
        ):
            put(ref, -1, zero)
            put(ref, chunks, zero)

        def iota(axis):
            return lax.broadcasted_iota(jnp.int32, block, axis)

        lane = iota(2)
        where_col = iota(0) * LANES + lane
        col = jnp.where(where_col < tile_cols + LANES // 2, where_col, where_col - tiles * LANES)
        gcol = col + ty * tile_cols
        total_cols, total_rows = tile_cols * ny, tile_rows * nx
        col_in_grid = (gcol >= 0) & (gcol < total_cols)
        col_face = (gcol >= 0) & (gcol + 1 < total_cols)
        row0 = tx * tile_rows - EDGE
        sub = iota(1)
        last_lane, first_lane = lane == LANES - 1, lane == 0

        def right(x):
            turned = pltpu.roll(x, LANES - 1, 2)
            beside = jnp.concatenate([turned[1:], turned[:1]], 0)
            return jnp.where(last_lane, beside, turned)

        def left(x):
            turned = pltpu.roll(x, 1, 2)
            beside = jnp.concatenate([turned[-1:], turned[:-1]], 0)
            return jnp.where(first_lane, beside, turned)

        for k in range(chunks):
            put(count, k, zero)
            for n in range(steps):
                put(seen.at[n], k, zero)
        one_lane = lane_iota(1, LANES)
        for copy in small:
            copy.wait()

        def place(gx, gy):
            lr = gx - row0
            lc = gy - ty * tile_cols
            ok = (lr >= 0) & (lr < rows) & (lc >= -EDGE) & (lc < tile_cols + EDGE)
            at = jnp.where(lc < 0, lc + tiles * LANES, lc)
            return lr + EDGE, at // LANES, lax.rem(at, LANES), ok

        def well(o, carry):
            lr, lt, ll, ok = place(spot[2 * pumps + o], spot[2 * pumps + wells + o])

            @pl.when(ok)
            def _():
                hit = one_lane == ll
                at = pl.ds(lr, 1)
                count[lt, at, :] += jnp.where(hit, 1.0, 0.0)
                for n in range(steps):
                    seen[n, lt, at, :] += jnp.where(hit, obs[n, 0, o], 0.0)

            return carry

        lax.fori_loop(0, wells, well, 0)

        by_lane = lane_iota(EDGE, LANES)
        stores = []
        for kind in range(2):
            table = jnp.full((EDGE, LANES), st[kind, 0], f32)
            for z in range(1, zones):
                table = jnp.where(by_lane == z, st[kind, z], table)
            stores.append(1.0 / table)

        for copy in copies:
            copy.wait()
        for i in range(nxr):
            for f in range(FIELDS):
                for t in range(own):
                    field(f)[t, pl.ds(tops[i], EDGE), :] = rin[i][
                        EDGE * f : EDGE * (f + 1), LANES * t : LANES * (t + 1)
                    ]

        edge_lane = lane_iota(EDGE, LANES)
        side = []
        for py in yr:
            low = jnp.where(forward_of("ty", py), 0, LANES - EDGE)
            side.append((edge_lane >= low) & (edge_lane < low + EDGE))

        def edge_of(messages, amount):
            out = jnp.zeros((EDGE, LANES), f32)
            for mask, message in zip(side, messages):
                part = pltpu.roll(message, (LANES - amount) % LANES, 1) if amount % LANES else message
                out = jnp.where(mask, part, out)
            return out

        for h in range(2):
            for k in range(half // EDGE):
                messages = [cin[j][EDGE * k : EDGE * (k + 1), :] for j in range(nyr)]
                for f in range(FIELDS):
                    value = edge_of(messages, EDGE * f + 64 * h)
                    field(f)[own, at_of(k + 1 + h * (half // EDGE)), :] = value
        for i in range(nxr):
            messages = [kin[i * nyr + j][...] for j in range(nyr)]
            for f in range(FIELDS):
                field(f)[own, pl.ds(tops[i], EDGE), :] = edge_of(messages, EDGE * f)

        def inject(k, n):
            return get(count, k) * get(frac.at[n], k) - get(seen.at[n - 1], k)

        def look_up(table, index):
            return jnp.take_along_axis(table, index, axis=1, mode="promise_in_bounds")

        for k in range(chunks):
            put(res, k, jnp.exp(-get(res, k)))
            put(shp, k, jnp.exp(get(shp, k)))
            for t in range(tiles):
                if t < own and 0 < k < chunks - 1:
                    zone = zone_mid[t, EDGE * (k - 1) : EDGE * k, :]
                else:
                    zone = rs[t, at_of(k), :].astype(jnp.int32)
                rs[t, at_of(k), :] = look_up(stores[0], zone)
                rm[t, at_of(k), :] = look_up(stores[1], zone)

        def row_of(k):
            return row0 + k * EDGE + sub

        for k in range(chunks):
            here = get(res, k)
            down = 2.0 / (here + get(res, k, 1))
            if k in (0, chunks - 2, chunks - 1):
                down = jnp.where((row_of(k) >= 0) & (row_of(k) + 1 < total_rows), down, 0.0)
            put(cx, k, down)
            put(cy, k, jnp.where(col_face, 2.0 / (here + right(here)), 0.0))

        def in_grid(k, value):
            if k in (0, chunks - 1):
                keep = col_in_grid & (row_of(k) >= 0) & (row_of(k) < total_rows)
                return jnp.where(keep, value, 0.0)
            edge = jnp.where(col_in_grid[own:], value[own:], 0.0)
            return jnp.concatenate([value[:own], edge], 0)

        for n in range(steps):
            src, dst = frac.at[n], frac.at[n + 1]
            ahead, behind = {}, {}

            def update(k, src=src, dst=dst, n=n, behind=behind):
                fx, fy, fy_left, t = behind.pop(k)
                flow = fx - get(fluxx.at[n], k, -1) + (fy - fy_left)
                put(dst, k, get(src, k) + (flow - t) * get(rs, k))

            for k in range(chunks + LEAD):
                if k < chunks:
                    ahead[k] = right(get(src, k))
                if k >= LEAD:
                    j = k - LEAD
                    f, m = get(src, j), get(mat, j)
                    fx = get(cx, j) * (get(src, j, 1) - f)
                    put(fluxx.at[n], j, fx)
                    fy = get(cy, j) * (ahead.pop(j) - f)
                    put(fluxy.at[n], j, fy)
                    t = get(shp, j) * (f - m)
                    put(moved.at[n], j, t)
                    put(mat, j, m + t * get(rm, j))
                    behind[j] = (fx, fy, left(fy), t)
                    if j >= LAG:
                        update(j - LAG)
            for j in range(chunks - LAG, chunks):
                update(j)
            for p in range(pumps):
                lr, lt, ll, ok = place(spot[p], spot[pumps + p])

                @pl.when(ok)
                def _(lr=lr, lt=lt, ll=ll, p=p, n=n, dst=dst):
                    at = pl.ds(lr, 1)
                    dst[lt, at, :] += jnp.where(one_lane == ll, prs[p, n], 0.0) * rs[lt, at, :]

        for k in range(chunks):
            a = get(adj, k) + inject(k, steps)
            put(adj, k, a)
            put(scaled.at[steps % 2], k, a * get(rs, k))
        for n in reversed(range(steps)):
            old, new = scaled.at[(n + 1) % 2], scaled.at[n % 2]
            ahead, behind, ends = {}, {}, {}

            def update(k, n=n, new=new, behind=behind):
                sx, sy, sy_left, swap = behind.pop(k)
                a = get(adj, k) + (sx - get(flux, k, -1) + (sy - sy_left)) + swap
                if n > 0:
                    a = a + inject(k, n)
                    put(new, k, a * get(rs, k))
                put(adj, k, a)

            def close(k, ends=ends):
                gx, gy, gy_left = ends.pop(k)
                total = gx + get(prod, k, -1) + (gy + gy_left)
                gc = -0.5 * get(res, k) * total
                put(grad.at[0], k, in_grid(k, gc))

            for k in range(chunks + LEAD):
                if k < chunks:
                    ahead[k] = right(get(old, k))
                if k < LEAD:
                    continue
                j = k - LEAD
                s = get(old, j)
                sx = get(cx, j) * (get(old, j, 1) - s)
                put(flux, j, sx)
                sy = get(cy, j) * (ahead.pop(j) - s)
                am = get(adm, j)
                q = am * get(rm, j) - s
                swap = get(shp, j) * q
                put(adm, j, am - swap)
                gx = get(fluxx.at[n], j) * sx
                gy = get(fluxy.at[n], j) * sy
                gs = get(moved.at[n], j) * q
                if n < steps - 1:
                    gx += get(px_, j)
                    gy += get(py_, j)
                    gs += get(gs_, j)
                behind[j] = (sx, sy, left(sy), swap)
                if n > 0:
                    put(px_, j, gx)
                    put(py_, j, gy)
                    put(gs_, j, gs)
                else:
                    put(prod, j, gx)
                    ends[j] = (gx, gy, left(gy))
                    put(grad.at[1], j, in_grid(j, gs))
                if j >= LAG:
                    update(j - LAG)
                    if n == 0:
                        close(j - LAG)
            for j in range(chunks - LAG, chunks):
                update(j)
                if n == 0:
                    close(j)

        out_copies = []
        for q, (source, out) in enumerate(((adj, frac_out), (adm, mat_out))):
            for t in range(own):
                out_copies.append(
                    pltpu.make_async_copy(
                        source.at[t, pl.ds(2 * EDGE, tile_rows)],
                        out.at[:, pl.ds(LANES * t, LANES)],
                        mid_sem.at[q, t],
                    )
                )
        for copy in out_copies:
            copy.start()

        def blur(source, ks, emit):
            turned = {}
            for i in range(len(ks) + LEAD):
                if i < len(ks):
                    g = get(source, ks[i])
                    turned[i] = left(g) + right(g)
                if i >= LEAD:
                    k = ks[i - LEAD]
                    around = get(source, k, -1) + get(source, k, 1) + turned.pop(i - LEAD)
                    emit(k, (1.0 - 4.0 * BLEND) * get(source, k) + BLEND * around)

        for q in range(2):

            def first(k, value, q=q):
                put(grad2.at[q], k, in_grid(k, value))

            blur(grad.at[q], list(range(chunks)), first)
        for q in range(2):

            def second(k, value, q=q):
                for t in range(own):
                    smooth_out[q, EDGE * (k - 1) : EDGE * k, LANES * t : LANES * (t + 1)] = value[t]

            blur(grad2.at[q], list(range(1, chunks - 1)), second)
        for copy in out_copies:
            copy.wait()

    hbm = pl.BlockSpec(memory_space=pltpu.HBM)
    vmem = pl.BlockSpec(memory_space=pltpu.VMEM)
    big = (tiles, rows + 2 * EDGE, LANES)
    flat = jax.ShapeDtypeStruct((tile_rows, tile_cols), f32)
    return pl.pallas_call(
        kernel,
        out_shape=[pltpu.VMEM((2, tile_rows, tile_cols), f32), flat, flat],
        in_specs=[hbm] * (4 + FIELDS) + [vmem] * (nxr + nyr + nxr * nyr),
        out_specs=[vmem, hbm, hbm],
        scratch_shapes=[
            pltpu.VMEM((FIELDS,) + big, f32),
            pltpu.VMEM((own, tile_rows, LANES), jnp.int32),
            pltpu.VMEM(big, f32),
            pltpu.VMEM(big, f32),
            pltpu.VMEM(big, f32),
            pltpu.VMEM(big, f32),
            pltpu.VMEM((steps,) + big, f32),
            pltpu.VMEM((steps + 1,) + big, f32),
            pltpu.VMEM((steps,) + big, f32),
            pltpu.VMEM((steps,) + big, f32),
            pltpu.VMEM((steps,) + big, f32),
            pltpu.VMEM((2,) + big, f32),
            pltpu.VMEM(big, f32),
            pltpu.VMEM(big, f32),
            pltpu.VMEM(big, f32),
            pltpu.VMEM(big, f32),
            pltpu.VMEM(big, f32),
            pltpu.VMEM((2,) + big, f32),
            pltpu.VMEM((2,) + big, f32),
        ]
        + [pltpu.SMEM(x.shape, x.dtype) for x in scalars]
        + [
            pltpu.SemaphoreType.DMA((FIELDS, own)),
            pltpu.SemaphoreType.DMA((4,)),
        ],
        name="window",
    )(*scalars, *fields, *(in_vmem(x) for x in row_in + col_in + corner_in))


def add_parts(mine, theirs):
    def kernel(a_ref, b_ref, cond_ref, shape_ref):
        cond_ref[...] = a_ref[0] + b_ref[0]
        shape_ref[...] = a_ref[1] + b_ref[1]

    vmem = pl.BlockSpec(memory_space=pltpu.VMEM)
    flat = jax.ShapeDtypeStruct(mine.shape[1:], mine.dtype)
    return pl.pallas_call(
        kernel, out_shape=[flat] * 2, in_specs=[vmem] * 2, out_specs=[vmem] * 2, name="add_parts"
    )(in_vmem(mine), in_vmem(theirs))


def on_device(
    log_cond,
    log_shape,
    zone_ids,
    storage,
    pump_x,
    pump_y,
    pump_rates,
    obs_x,
    obs_y,
    observed,
    frac_start,
    matrix_start,
    frac_end,
    matrix_end,
):
    nx, ny = lax.axis_size("tx"), lax.axis_size("ty")
    xr, yr = rounds_of(nx), rounds_of(ny)
    fields = (
        log_cond,
        log_shape,
        zone_ids,
        frac_start[0],
        matrix_start[0],
        frac_end[0],
        matrix_end[0],
    )
    row_out, col_out, corner_out = pack(fields, xr, yr)
    col_in = [lax.ppermute(m, "ty", pairs_of(ny, py)) for m, py in zip(col_out, yr)]
    row_in = [lax.ppermute(m, "tx", pairs_of(nx, px)) for m, px in zip(row_out, xr)]
    corner_in = [
        lax.ppermute(corner_out[i * len(yr) + j], ("tx", "ty"), corner_pairs(nx, ny, px, py))
        for i, px in enumerate(xr)
        for j, py in enumerate(yr)
    ]
    rates = jnp.transpose(pump_rates, (0, 2, 1))[0]
    spots = jnp.concatenate([pump_x[0], pump_y[0], obs_x, obs_y])
    scalars = (storage, rates, spots, jnp.transpose(observed, (1, 0, 2)))
    part, fracture_adj, matrix_adj = window(
        fields, scalars, row_in, col_in, corner_in, xr, yr, nx, ny
    )
    tests = lax.axis_size("test")
    if tests == 2:
        cond_sum, shape_sum = add_parts(part, lax.ppermute(part, "test", [(0, 1), (1, 0)]))
    else:
        cond_sum, shape_sum = lax.psum(part, "test")
    return (cond_sum, shape_sum, fracture_adj[None], matrix_adj[None])


def solution(mesh):
    placed = (
        P(("inv", "tx"), "ty"),
        P(("inv", "tx"), "ty"),
        P(("inv", "tx"), "ty"),
        P("inv", None),
        P(("inv", "test"), None),
        P(("inv", "test"), None),
        P(("inv", "test"), None, None),
        P("inv"),
        P("inv"),
        P(("inv", "test"), None, None),
        P(("inv", "test"), "tx", "ty"),
        P(("inv", "test"), "tx", "ty"),
        P(("inv", "test"), "tx", "ty"),
        P(("inv", "test"), "tx", "ty"),
    )
    return jax.shard_map(
        on_device,
        mesh=mesh,
        in_specs=placed,
        out_specs=(
            P(("inv", "tx"), "ty"),
            P(("inv", "tx"), "ty"),
            P(("inv", "test"), "tx", "ty"),
            P(("inv", "test"), "tx", "ty"),
        ),
        check_vma=False,
    )
```

time: 42.4 us -> 29.7 us (0.70)
  Pallas kernels: 22.7 us -> 12.3 us
  local copies, waits for them, and re-layouts: 3.44 us -> 0.66 us
  starting transfers between devices: 10.4 us -> 11.4 us
  other arithmetic: 1.17 us -> 0.64 us
    pallas_call x1 -> x2, Pallas kernels: 20 us -> 10.3 us  [the longest x1 9.41 us: window(): pl.pallas_call(kernel, out_shape=[pltpu.VMEM((2, tile_rows, tile_cols), f...]
    ppermute x2, starting transfers between devices: 2.23 us -> 5.09 us  [on_device(): lax.ppermute(m, 'tx', pairs_of(nx, px))]
    squeeze x2 -> x0, local copies, waits for them, and re-layouts: 1.55 us -> none  [the longest x1 0.88 us: on_device(): return (summed[0], summed[1], fracture_adj[None], matrix_adj[None])]
    ppermute x1, starting transfers between devices: 3.03 us -> 1.56 us  [on_device(): lax.ppermute(m, 'ty', pairs_of(ny, py))]
    unnamed x19 -> x4, local copies, waits for them, and re-layouts: 1.9 us -> 0.66 us
    add x1 -> x0, other arithmetic: 1.17 us -> none  [on_device(): summed = smoothed + lax.ppermute(smoothed, 'test', [(0, 1), (1, 0)])]
    concatenate x0 -> x1, other arithmetic: none -> 0.64 us  [on_device(): spots = jnp.concatenate([pump_x[0], pump_y[0], obs_x, obs_y])]
    pallas_call x1, Pallas kernels: 2.64 us -> 2 us  [pack(): pl.pallas_call(kernel, out_shape=outs, in_specs=[pl.BlockSpec(memory_spac...]
  transfers between devices with their start and end apart: 6 -> 6, of which waited for: 1 -> 2; matrix products, arithmetic and copies ran while one was open for 3% -> 2% of each run, Pallas kernels for 0% -> 0%
where the time goes in v3:
time: 29.7 us; the launch traced here: 29.4 us
  Pallas kernels  12.3 us (41%)
  starting transfers between devices  11.4 us (38%)
  waiting for transfers between devices  2.41 us (8%)
  between operations  2 us (7%)
  local copies, waits for them, and re-layouts  0.66 us (2%)
  other arithmetic  0.64 us (2%)
    pallas_call x1, Pallas kernels, window(): pl.pallas_call(kernel, out_shape=[pltpu.VMEM((2, tile_rows, tile_cols), f...  9.41 us
    ppermute x2, starting transfers between devices, on_device(): lax.ppermute(m, 'tx', pairs_of(nx, px))  5.09 us
    ppermute x2, starting transfers between devices, on_device(): lax.ppermute(corner_out[i * len(yr) + j], ('tx', 'ty'), corner_pairs(nx,...  4.69 us
    ppermute x1, waiting for transfers between devices, on_device(): lax.ppermute(part, 'test', [(0, 1), (1, 0)])  2.08 us
    pallas_call x1, Pallas kernels, pack(): pl.pallas_call(kernel, out_shape=outs, in_specs=[pl.BlockSpec(memory_spac...  2 us
    ppermute x1, starting transfers between devices, on_device(): lax.ppermute(m, 'ty', pairs_of(ny, py))  1.56 us
    pallas_call x1, Pallas kernels, add_parts(): pl.pallas_call(kernel, out_shape=[flat] * 2, in_specs=[vmem] * 2, out_spe...  0.9 us
    unnamed x4, local copies, waits for them, and re-layouts  0.66 us
  transfers between devices with their start and end apart: 6, of which 2 were waited for; matrix products, arithmetic and copies ran while one was open for 2% of the time, Pallas kernels for 0%

profile of v3, /device:TPU:0, one launch (start us, length us, event | category | flops | bytes accessed | tf_op | source)
XLA Modules:
  0.0 29.4 jit_solution(26369275251333790)
XLA Ops:
  0.6 2.0 %pack.1 = (f32[56,256]{1,0:T(8,128)S(1)}, f32[56,256]{1,0:T(8,128)S(1)}, f32[160,128]{1,0:T(8,128)S(1)}, f32[8,128]{1,0:T(8,128)S(1)}, f32[8,128]{1,0:T(8,128)S(1)}) custom-call(f32[320,256]{1,0:T(8,128)} %refs_4_.1, f32[320,256]{1,0:T(8,128)} %refs_5_.1, s32[320,256]{1,0:T(8,128)} %refs_6_.1, f32[320,256]{1,0:T(8,128)} %bitcast.12, f32[320,256]{1,0:T(8,128)} %bitcast.14, ...), custom_call_target="tpu_custom_call" | custom-call | tf_op jit(solution)/shard_map/pack/pallas_call | solution.py:133
  2.6 4.0 %collective-permute-start.3 = (f32[8,128]{1,0:T(8,128)S(1)}, f32[8,128]{1,0:T(8,128)S(1)}, u32[]{:S(2)}, u32[]{:S(2)}) collective-permute-start(f32[8,128]{1,0:T(8,128)S(1)} %get-tuple-element.17), channel_id=1, source_target_pairs={{0,3},{1,2},{2,1},{3,0},{4,7},{5,6},{6,5},{7,4},{8,11},{9,10},{10,... | collective-permute-start | bytes 12296 | tf_op jit(solution)/shard_map/ppermute | solution.py:581
  6.7 0.6 %collective-permute-start.4 = (f32[8,128]{1,0:T(8,128)S(1)}, f32[8,128]{1,0:T(8,128)S(1)}, u32[]{:S(2)}, u32[]{:S(2)}) collective-permute-start(f32[8,128]{1,0:T(8,128)S(1)} %get-tuple-element.18), channel_id=1, source_target_pairs={{2,5},{3,4},{4,3},{5,2},{10,13},{11,12},{12,11},{13,10},{18,21},{1... | collective-permute-start | bytes 12296 | tf_op jit(solution)/shard_map/ppermute | solution.py:581
  7.3 4.4 %collective-permute-start = (f32[56,256]{1,0:T(8,128)S(1)}, f32[56,256]{1,0:T(8,128)S(1)}, u32[]{:S(2)}, u32[]{:S(2)}) collective-permute-start(f32[56,256]{1,0:T(8,128)S(1)} %get-tuple-element.14), channel_id=1, source_target_pairs={{0,2},{2,0},{4,6},{6,4},{1,3},{3,1},{5,7},{7,5},{8,10},{10,8},{12,... | collective-permute-start | bytes 172040 | tf_op jit(solution)/shard_map/ppermute | solution.py:579
  11.8 0.7 %collective-permute-start.1 = (f32[56,256]{1,0:T(8,128)S(1)}, f32[56,256]{1,0:T(8,128)S(1)}, u32[]{:S(2)}, u32[]{:S(2)}) collective-permute-start(f32[56,256]{1,0:T(8,128)S(1)} %get-tuple-element.15), channel_id=1, source_target_pairs={{2,4},{4,2},{3,5},{5,3},{10,12},{12,10},{11,13},{13,11},{18,20},{2... | collective-permute-start | bytes 172040 | tf_op jit(solution)/shard_map/ppermute | solution.py:579
  12.4 1.6 %collective-permute-start.2 = (f32[160,128]{1,0:T(8,128)S(1)}, f32[160,128]{1,0:T(8,128)S(1)}, u32[]{:S(2)}, u32[]{:S(2)}) collective-permute-start(f32[160,128]{1,0:T(8,128)S(1)} %get-tuple-element.16), channel_id=1, source_target_pairs={{0,1},{1,0},{2,3},{3,2},{4,5},{5,4},{6,7},{7,6},{8,9},{9,8},{10,11... | collective-permute-start | bytes 245768 | tf_op jit(solution)/shard_map/ppermute | solution.py:578
  15.3 0.0 copy-start
  15.3 0.0 copy-start.1
  15.3 0.6 %copy-done = s32[64]{0:T(128)S(1)} copy-done((s32[64]{0:T(128)S(1)}, s32[64]{0:T(128)}, u32[]{:S(2)}) %copy-start) | copy-done | bytes 280
  16.0 0.0 copy-done.1
  16.0 0.6 %pad_add_fusion.refs_2_ = s32[130]{0:T(256)} fusion(s32[64]{0:T(128)S(1)} %copy-done, s32[64]{0:T(128)S(1)} %copy-done.1, s32[1]{0:T(128)} %bitcast.11, s32[1]{0:T(128)} %bitcast.10), kind=kLoop, calls=%fused_computation | loop fusion | flops 390 | bytes 1040 | tf_op jit(solution)/shard_map/concatenate | solution.py:586
  16.6 0.0 collective-permute-done.3.refs_14_
  16.6 0.0 collective-permute-done.4.refs_15_
  16.6 0.0 collective-permute-done.refs_11_
  16.6 0.0 collective-permute-done.1.refs_12_
  16.6 0.3 %collective-permute-done.2.refs_13_ = f32[160,128]{1,0:T(8,128)S(1)} collective-permute-done((f32[160,128]{1,0:T(8,128)S(1)}, f32[160,128]{1,0:T(8,128)S(1)}, u32[]{:S(2)}, u32[]{:S(2)}) %collective-permute-start.2) | collective-permute-done | bytes 81952 | tf_op jit(solution)/shard_map/ppermute | solution.py:578
  16.9 9.4 %window.1 = (f32[2,320,256]{2,1,0:T(8,128)S(1)}, f32[320,256]{1,0:T(8,128)}, f32[320,256]{1,0:T(8,128)}) custom-call(f32[2,8]{1,0:T(2,128)} %refs_0_.3, f32[1,3]{1,0:T(1,128)} %bitcast.21, s32[130]{0:T(256)} %pad_add_fusion.refs_2_, f32[3,1,64]{2,1,0:T(1,128)} %bitcast.20, f32[320,256]{1,0:T(8,128)} %refs_4_.1, f32[320,256]{1,0:T(8,128)} %refs_5_.1, ...), custom_call_target="tpu_custom_call" | custom-call | tf_op jit(solution)/shard_map/window/pallas_call | solution.py:503
  26.4 0.1 collective-permute-start.5
  26.4 2.1 %collective-permute-done.5.b_ref = f32[2,320,256]{2,1,0:T(8,128)S(1)} collective-permute-done((f32[2,320,256]{2,1,0:T(8,128)S(1)}, f32[2,320,256]{2,1,0:T(8,128)S(1)}, u32[]{:S(2)}, u32[]{:S(2)}) %collective-permute-start.5) | collective-permute-done | bytes 655392 | tf_op jit(solution)/shard_map/ppermute | solution.py:593
  28.5 0.9 %add_parts.1 = (f32[320,256]{1,0:T(8,128)}, f32[320,256]{1,0:T(8,128)}) custom-call(f32[2,320,256]{2,1,0:T(8,128)S(1)} %get-tuple-element.19.a_ref, f32[2,320,256]{2,1,0:T(8,128)S(1)} %collective-permute-done.5.b_ref), custom_call_target="tpu_custom_call" | custom-call | tf_op jit(solution)/shard_map/add_parts/pallas_call | solution.py:545
Async XLA Ops:
  2.6 14.0 %collective-permute-start.3 = (f32[8,128]{1,0:T(8,128)S(1)}, f32[8,128]{1,0:T(8,128)S(1)}, u32[]{:S(2)}, u32[]{:S(2)}) collective-permute-start(f32[8,128]{1,0:T(8,128)S(1)} %get-tuple-element.17), channel_id=1, source_target_pairs={{0,3},{1,2},{2,1},{3,0},{4,7},{5,6},{6,5},{7,4},{8,11},{9,10},{10,... | collective-permute-start | bytes 12296 | tf_op jit(solution)/shard_map/ppermute | solution.py:581
  6.7 9.9 %collective-permute-start.4 = (f32[8,128]{1,0:T(8,128)S(1)}, f32[8,128]{1,0:T(8,128)S(1)}, u32[]{:S(2)}, u32[]{:S(2)}) collective-permute-start(f32[8,128]{1,0:T(8,128)S(1)} %get-tuple-element.18), channel_id=1, source_target_pairs={{2,5},{3,4},{4,3},{5,2},{10,13},{11,12},{12,11},{13,10},{18,21},{1... | collective-permute-start | bytes 12296 | tf_op jit(solution)/shard_map/ppermute | solution.py:581
  7.3 9.3 %collective-permute-start = (f32[56,256]{1,0:T(8,128)S(1)}, f32[56,256]{1,0:T(8,128)S(1)}, u32[]{:S(2)}, u32[]{:S(2)}) collective-permute-start(f32[56,256]{1,0:T(8,128)S(1)} %get-tuple-element.14), channel_id=1, source_target_pairs={{0,2},{2,0},{4,6},{6,4},{1,3},{3,1},{5,7},{7,5},{8,10},{10,8},{12,... | collective-permute-start | bytes 172040 | tf_op jit(solution)/shard_map/ppermute | solution.py:579
  11.8 4.8 %collective-permute-start.1 = (f32[56,256]{1,0:T(8,128)S(1)}, f32[56,256]{1,0:T(8,128)S(1)}, u32[]{:S(2)}, u32[]{:S(2)}) collective-permute-start(f32[56,256]{1,0:T(8,128)S(1)} %get-tuple-element.15), channel_id=1, source_target_pairs={{2,4},{4,2},{3,5},{5,3},{10,12},{12,10},{11,13},{13,11},{18,20},{2... | collective-permute-start | bytes 172040 | tf_op jit(solution)/shard_map/ppermute | solution.py:579
  12.4 4.5 %collective-permute-start.2 = (f32[160,128]{1,0:T(8,128)S(1)}, f32[160,128]{1,0:T(8,128)S(1)}, u32[]{:S(2)}, u32[]{:S(2)}) collective-permute-start(f32[160,128]{1,0:T(8,128)S(1)} %get-tuple-element.16), channel_id=1, source_target_pairs={{0,1},{1,0},{2,3},{3,2},{4,5},{5,4},{6,7},{7,6},{8,9},{9,8},{10,11... | collective-permute-start | bytes 245768 | tf_op jit(solution)/shard_map/ppermute | solution.py:578
  15.3 0.7 %copy-start = (s32[64]{0:T(128)S(1)}, s32[64]{0:T(128)}, u32[]{:S(2)}) copy-start(s32[64]{0:T(128)} %param.22) | copy-start | bytes 772
  15.3 0.7 %copy-start.1 = (s32[64]{0:T(128)S(1)}, s32[64]{0:T(128)}, u32[]{:S(2)}) copy-start(s32[64]{0:T(128)} %param.21) | copy-start | bytes 772
  26.4 2.2 %collective-permute-start.5 = (f32[2,320,256]{2,1,0:T(8,128)S(1)}, f32[2,320,256]{2,1,0:T(8,128)S(1)}, u32[]{:S(2)}, u32[]{:S(2)}) collective-permute-start(f32[2,320,256]{2,1,0:T(8,128)S(1)} %get-tuple-element.19.a_ref), channel_id=1, source_target_pairs={{0,8},{8,0},{1,9},{9,1},{2,10},{10,2},{3,11},{11,3},{4,12},{12,4},... | collective-permute-start | bytes 1966088 | tf_op jit(solution)/shard_map/ppermute | solution.py:593

commit v4 on v3

v4 whole, which is shorter than its diff:
```python
import jax
import jax.numpy as jnp
from jax import lax
from jax.experimental import pallas as pl
from jax.experimental.pallas import tpu as pltpu
from jax.sharding import PartitionSpec as P


SMOOTH = 2
EDGE = 8
LANES = 128
BLEND = 0.2
LEAD = 6
LAG = 6
FIELDS = 7


def in_vmem(x):
    return pltpu.with_memory_space_constraint(x, pltpu.VMEM)


def in_hbm(x):
    return pltpu.with_memory_space_constraint(x, pltpu.HBM)


def pairs_of(count, parity):
    found = []
    for low in range(parity, count - 1, 2):
        found += [(low, low + 1), (low + 1, low)]
    return found


def rounds_of(count):
    return [parity for parity in (0, 1) if pairs_of(count, parity)]


def forward_of(axis, parity):
    return lax.rem(lax.axis_index(axis), 2) == parity


def lane_iota(rows, cols):
    return lax.broadcasted_iota(jnp.int32, (rows, cols), 1)


def tile_shape(fields):
    tile_rows, tile_cols = fields[0].shape
    return tile_rows, tile_cols, tile_cols // LANES


def vmem_like(shape, kind=jnp.float32):
    return pltpu.VMEM(shape, kind)


HBM = pl.BlockSpec(memory_space=pltpu.HBM)
VMEM = pl.BlockSpec(memory_space=pltpu.VMEM)


def pack_columns(fields, yr):
    tile_rows, tile_cols, _ = tile_shape(fields)
    half = tile_rows // 2
    nyr = len(yr)

    def kernel(*refs):
        ins, outs = refs[:FIELDS], refs[FIELDS : FIELDS + nyr]
        cols, zone_cols, sem = refs[FIELDS + nyr :]
        copies = []
        for j, py in enumerate(yr):
            start = jnp.where(forward_of("ty", py), tile_cols - LANES, 0)
            start = pl.multiple_of(start, LANES)
            for f in range(FIELDS):
                into = zone_cols.at[j] if f == 2 else cols.at[j, f]
                copies.append(
                    pltpu.make_async_copy(ins[f].at[:, pl.ds(start, LANES)], into, sem.at[j, f])
                )
        for copy in copies:
            copy.start()
        for copy in copies:
            copy.wait()
        slot = lane_iota(EDGE, LANES) // EDGE
        for j, py in enumerate(yr):
            shift = jnp.where(forward_of("ty", py), 1, 0)
            masks = {}
            for h in range(2):
                for f in range(FIELDS):
                    masks[h, f] = slot == lax.rem(f + 8 * h - shift + 16, 16)
            for k in range(half // EDGE):
                total = jnp.zeros((EDGE, LANES), jnp.float32)
                for h in range(2):
                    at = k * EDGE + h * half
                    for f in range(FIELDS):
                        part = (zone_cols if f == 2 else cols.at[:, f])[j, at : at + EDGE, :]
                        amount = EDGE * f + 64 * h
                        part = part.astype(jnp.float32)
                        part = pltpu.roll(part, amount, 1) if amount else part
                        total = jnp.where(masks[h, f], part, total)
                outs[j][EDGE * k : EDGE * (k + 1), :] = total

    return pl.pallas_call(
        kernel,
        out_shape=[vmem_like((half, LANES))] * nyr,
        in_specs=[HBM] * FIELDS,
        out_specs=[VMEM] * nyr,
        scratch_shapes=[
            pltpu.VMEM((nyr, FIELDS, tile_rows, LANES), jnp.float32),
            pltpu.VMEM((nyr, tile_rows, LANES), jnp.int32),
            pltpu.SemaphoreType.DMA((nyr, FIELDS)),
        ],
        compiler_params=grant(8),
        name="pack_columns",
    )(*(in_hbm(x) for x in fields))


def load_tile(fields, xr):
    tile_rows, tile_cols, own = tile_shape(fields)
    nxr = len(xr)

    def kernel(*refs):
        ins = refs[:FIELDS]
        wide, zone_mid = refs[FIELDS : FIELDS + 2]
        outs = refs[FIELDS + 2 : FIELDS + 2 + nxr]
        sem = refs[FIELDS + 2 + nxr]
        copies = []
        for f in range(FIELDS):
            for t in range(own):
                into = zone_mid.at[t] if f == 2 else wide.at[f, t, pl.ds(2 * EDGE, tile_rows)]
                copies.append(
                    pltpu.make_async_copy(ins[f].at[:, pl.ds(LANES * t, LANES)], into, sem.at[f, t])
                )
        for copy in copies:
            copy.start()
        for copy in copies:
            copy.wait()
        for i, px in enumerate(xr):
            start = pl.multiple_of(jnp.where(forward_of("tx", px), tile_rows - EDGE, 0), EDGE)
            for f in range(FIELDS):
                for t in range(own):
                    if f == 2:
                        part = zone_mid[t, pl.ds(start, EDGE), :].astype(jnp.float32)
                    else:
                        part = wide[f, t, pl.ds(start + 2 * EDGE, EDGE), :]
                    outs[i][EDGE * f : EDGE * (f + 1), LANES * t : LANES * (t + 1)] = part

    big = (own + 1, tile_rows + 4 * EDGE, LANES)
    made = pl.pallas_call(
        kernel,
        out_shape=[
            vmem_like((FIELDS,) + big),
            vmem_like((own, tile_rows, LANES), jnp.int32),
        ]
        + [vmem_like((EDGE * (FIELDS + 1), tile_cols))] * nxr,
        in_specs=[HBM] * FIELDS,
        out_specs=[VMEM] * (2 + nxr),
        scratch_shapes=[pltpu.SemaphoreType.DMA((FIELDS, own))],
        compiler_params=grant(4),
        name="load_tile",
    )(*(in_hbm(x) for x in fields))
    return made[0], made[1], made[2:]


def add_corners(row_out, col_in, xr):
    nxr, nyr = len(xr), len(col_in)
    assert nyr * LANES <= row_out[0].shape[1]

    def kernel(*refs):
        cols, outs = refs[:nyr], refs[nyr + nxr :]
        for i, px in enumerate(xr):
            outs[i][EDGE * FIELDS :, :] = jnp.zeros((EDGE, row_out[0].shape[1]), jnp.float32)
            ahead = forward_of("tx", px)
            for j in range(nyr):
                top = cols[j][0:EDGE, :]
                low = pltpu.roll(cols[j][cols[j].shape[0] - EDGE :, :], LANES // 2, 1)
                outs[i][EDGE * FIELDS :, LANES * j : LANES * (j + 1)] = jnp.where(ahead, low, top)

    return pl.pallas_call(
        kernel,
        out_shape=[vmem_like(x.shape) for x in row_out],
        in_specs=[VMEM] * (nyr + nxr),
        out_specs=[VMEM] * nxr,
        input_output_aliases={nyr + i: i for i in range(nxr)},
        compiler_params=grant(2),
        name="add_corners",
    )(*(in_vmem(x) for x in list(col_in) + list(row_out)))


def grant(mib):
    return pltpu.CompilerParams(vmem_limit_bytes=mib * 2**20)


class Chunks:
    def __init__(self, tile_rows):
        self.count = tile_rows // EDGE + 2

    @staticmethod
    def at(k, shift=0):
        return slice(EDGE * (k + 1) + shift, EDGE * (k + 2) + shift)


def get(ref, k, shift=0):
    return ref[:, Chunks.at(k, shift), :]


def put(ref, k, value):
    ref[:, Chunks.at(k), :] = value


def turn_right(x, last_lane):
    turned = pltpu.roll(x, LANES - 1, 2)
    return jnp.where(last_lane, jnp.concatenate([turned[1:], turned[:1]], 0), turned)


def turn_left(x, first_lane):
    turned = pltpu.roll(x, 1, 2)
    return jnp.where(first_lane, jnp.concatenate([turned[-1:], turned[:-1]], 0), turned)


def store_tables(storage_ref, zones):
    by_lane = lane_iota(EDGE, LANES)
    tables = []
    for kind in range(2):
        table = jnp.full((EDGE, LANES), storage_ref[kind, 0], jnp.float32)
        for z in range(1, zones):
            table = jnp.where(by_lane == z, storage_ref[kind, z], table)
        tables.append(1.0 / table)
    return tables


def look_up(table, index):
    return jnp.take_along_axis(table, index, axis=1, mode="promise_in_bounds")


def place_of(gx, gy, tile_rows, tile_cols):
    lr = gx - lax.axis_index("tx") * tile_rows + EDGE
    lc = gy - lax.axis_index("ty") * tile_cols
    ok = (lr >= 0) & (lr < tile_rows + 2 * EDGE) & (lc >= -EDGE) & (lc < tile_cols + EDGE)
    at = jnp.where(lc < 0, lc + tile_cols + LANES, lc)
    return lr + EDGE, at // LANES, lax.rem(at, LANES), ok


def prepare_tile(wide, zone_mid, scalars):
    storage, _, _, observed = scalars
    tile_rows = zone_mid.shape[1]
    own = zone_mid.shape[0]
    tile_cols = own * LANES
    big = wide.shape[1:]
    zones = storage.shape[1]
    steps, wells = observed.shape[0], observed.shape[2]
    chunks = Chunks(tile_rows).count
    f32 = jnp.float32

    def kernel(*refs):
        small_in, zone_in = refs[:4], refs[5]
        wide, rm, cx, cy, count, seen = refs[6:12]
        st, oxs, oys, obs = refs[12:16]
        sem = refs[16]
        copies = [
            pltpu.make_async_copy(a, b, sem.at[i])
            for i, (a, b) in enumerate(zip(small_in, (st, oxs, oys, obs)))
        ]
        for copy in copies:
            copy.start()
        res, shp, rs = wide.at[0], wide.at[1], wide.at[2]
        zero = jnp.zeros((own + 1, EDGE, LANES), f32)
        for k in range(chunks):
            put(count, k, zero)
            for n in range(steps):
                put(seen.at[n], k, zero)
        for k in range(1, chunks - 1):
            res[0:own, Chunks.at(k), :] = jnp.exp(-res[0:own, Chunks.at(k), :])
            shp[0:own, Chunks.at(k), :] = jnp.exp(shp[0:own, Chunks.at(k), :])
        last_lane = lax.broadcasted_iota(jnp.int32, (1, EDGE, LANES), 2) == LANES - 1
        ahead = {}
        for k in range(1, chunks - 1 + LEAD):
            if k < chunks - 1:
                turned = pltpu.roll(res[0:own, Chunks.at(k), :], LANES - 1, 2)
                ahead[k] = jnp.where(last_lane, turned[1:], turned[:-1])
            j = k - LEAD
            if j >= 1:
                here = res[0:own, Chunks.at(j), :]
                if j < chunks - 2:
                    below = res[0:own, Chunks.at(j, 1), :]
                    cx[0:own, Chunks.at(j), :] = 2.0 / (here + below)
                cy[0 : own - 1, Chunks.at(j), :] = 2.0 / (here[: own - 1] + ahead.pop(j))
        for copy in copies:
            copy.wait()
        tables = store_tables(st, zones)
        for k in range(1, chunks - 1):
            for t in range(own):
                zone = zone_in[t, EDGE * (k - 1) : EDGE * k, :]
                rs[t, Chunks.at(k), :] = look_up(tables[0], zone)
                rm[t, Chunks.at(k), :] = look_up(tables[1], zone)
        one_lane = lane_iota(1, LANES)

        def well(o, carry):
            lr, lt, ll, ok = place_of(oxs[o], oys[o], tile_rows, tile_cols)

            @pl.when(ok)
            def _():
                hit = one_lane == ll
                at = pl.ds(lr, 1)
                count[lt, at, :] += jnp.where(hit, 1.0, 0.0)
                for n in range(steps):
                    seen[n, lt, at, :] += jnp.where(hit, obs[n, 0, o], 0.0)

            return carry

        lax.fori_loop(0, wells, well, 0)

    return pl.pallas_call(
        kernel,
        out_shape=[vmem_like(wide.shape)] + [vmem_like(big)] * 4 + [vmem_like((steps,) + big)],
        in_specs=[HBM] * 4 + [VMEM] * 2,
        out_specs=[VMEM] * 6,
        input_output_aliases={4: 0},
        scratch_shapes=[pltpu.SMEM(x.shape, x.dtype) for x in scalars]
        + [pltpu.SemaphoreType.DMA((4,))],
        compiler_params=grant(4),
        name="prepare_tile",
    )(*(in_hbm(x) for x in scalars), in_vmem(wide), in_vmem(zone_mid))


def window(prepared, scalars, row_in, col_in, xr, yr, nx, ny):
    storage, pump_rates, _, _ = scalars
    zones = storage.shape[1]
    pumps, steps = pump_rates.shape
    tiles, _, _ = big = prepared[1].shape
    own = tiles - 1
    tile_rows, tile_cols = 2 * col_in[0].shape[0], own * LANES
    assert 2 * steps + SMOOTH <= EDGE
    half = tile_rows // 2
    nxr, nyr = len(xr), len(yr)
    chunks = Chunks(tile_rows).count
    f32 = jnp.float32
    kept = len(prepared)

    def kernel(*refs):
        pos = 0

        def take(count):
            nonlocal pos
            pos += count
            return refs[pos - count : pos]

        small_in = take(2)
        pump_at = take(2)
        take(kept)
        rin, cin = take(nxr), take(nyr)
        (wide, rm, cx, cy, count, seen) = take(kept)
        smooth_out, frac_out, mat_out = take(3)
        (later, fluxx, fluxy, moved, scaled, flux, prod) = take(7)
        (px_, py_, gs_, grad, grad2) = take(5)
        (st, prs) = take(2)
        (mid_sem, small_sem) = take(2)
        res, shp, rs = wide.at[0], wide.at[1], wide.at[2]
        mat, adj, adm = wide.at[4], wide.at[5], wide.at[6]
        tx, ty = lax.axis_index("tx"), lax.axis_index("ty")
        frac = [wide.at[3]] + [later.at[n] for n in range(steps)]

        small = [
            pltpu.make_async_copy(a, b, small_sem.at[i])
            for i, (a, b) in enumerate(zip(small_in, (st, prs)))
        ]
        for copy in small:
            copy.start()
        block = (tiles, EDGE, LANES)
        zero = jnp.zeros(block, f32)
        if nxr < 2:
            for f in range(FIELDS):
                put(wide.at[f], 0, zero)
                put(wide.at[f], chunks - 1, zero)
        for ref in (
            [res, grad.at[0], grad.at[1], grad2.at[0], grad2.at[1], flux, prod]
            + frac
            + [fluxx.at[n] for n in range(steps)]
            + [scaled.at[n] for n in range(2)]
        ):
            put(ref, -1, zero)
            put(ref, chunks, zero)

        def iota(axis):
            return lax.broadcasted_iota(jnp.int32, block, axis)

        lane = iota(2)
        where_col = iota(0) * LANES + lane
        col = jnp.where(where_col < tile_cols + LANES // 2, where_col, where_col - tiles * LANES)
        gcol = col + ty * tile_cols
        total_cols, total_rows = tile_cols * ny, tile_rows * nx
        col_in_grid = (gcol >= 0) & (gcol < total_cols)
        col_face = (gcol >= 0) & (gcol + 1 < total_cols)
        row0 = tx * tile_rows - EDGE
        sub = iota(1)
        last_lane, first_lane = lane == LANES - 1, lane == 0

        def right(x):
            return turn_right(x, last_lane)

        def left(x):
            return turn_left(x, first_lane)

        one_lane = lane_iota(1, LANES)

        def number(ref, p):
            there = lax.broadcasted_iota(jnp.int32, (1, pumps), 1) == p
            return jnp.sum(jnp.where(there, ref[...], 0))

        pump_spots = [
            place_of(number(pump_at[0], p), number(pump_at[1], p), tile_rows, tile_cols)
            for p in range(pumps)
        ]

        tops = []
        for i, px in enumerate(xr):
            to = jnp.where(forward_of("tx", px), tile_rows + 2 * EDGE, EDGE)
            tops.append(pl.ds(pl.multiple_of(to, EDGE), EDGE))
            for f in range(FIELDS):
                for t in range(own):
                    wide[f, t, tops[i], :] = rin[i][
                        EDGE * f : EDGE * (f + 1), LANES * t : LANES * (t + 1)
                    ]
        edge_lane = lane_iota(EDGE, LANES)
        side = []
        for py in yr:
            low = jnp.where(forward_of("ty", py), 0, LANES - EDGE)
            side.append((edge_lane >= low) & (edge_lane < low + EDGE))

        def edge_of(messages, amount):
            out = jnp.zeros((EDGE, LANES), f32)
            for mask, message in zip(side, messages):
                part = pltpu.roll(message, (LANES - amount) % LANES, 1) if amount % LANES else message
                out = jnp.where(mask, part, out)
            return out

        for i in range(nxr):
            messages = [
                rin[i][EDGE * FIELDS :, LANES * j : LANES * (j + 1)] for j in range(nyr)
            ]
            for f in range(FIELDS):
                wide[f, own, tops[i], :] = edge_of(messages, EDGE * f)
        for h in range(2):
            for k in range(half // EDGE):
                messages = [cin[j][EDGE * k : EDGE * (k + 1), :] for j in range(nyr)]
                for f in range(FIELDS):
                    value = edge_of(messages, EDGE * f + 64 * h)
                    wide[f, own, Chunks.at(k + 1 + h * (half // EDGE)), :] = value

        def inject(k, n):
            return get(count, k) * get(frac[n], k) - get(seen.at[n - 1], k)

        for copy in small:
            copy.wait()
        tables = store_tables(st, zones)
        for k in range(chunks):
            at = Chunks.at(k)
            for t in range(0 if k in (0, chunks - 1) else own, tiles):
                res[t, at, :] = jnp.exp(-res[t, at, :])
                shp[t, at, :] = jnp.exp(shp[t, at, :])
                zone = rs[t, at, :].astype(jnp.int32)
                rs[t, at, :] = look_up(tables[0], zone)
                rm[t, at, :] = look_up(tables[1], zone)

        def row_of(k):
            return row0 + k * EDGE + sub

        ahead = {}
        for k in range(chunks + LEAD):
            if k < chunks:
                ahead[k] = right(get(res, k))
            if k < LEAD:
                continue
            j = k - LEAD
            here, at = get(res, j), Chunks.at(j)
            t = own if 0 < j < chunks - 2 else 0
            down = 2.0 / (here + get(res, j, 1))[t:]
            if t == 0:
                down = jnp.where((row_of(j) >= 0) & (row_of(j) + 1 < total_rows), down, 0.0)
            cx[t:, at, :] = down
            t = own - 1 if 0 < j < chunks - 1 else 0
            beside = 2.0 / (here + ahead.pop(j))[t:]
            cy[t:, at, :] = jnp.where(col_face[t:], beside, 0.0)

        def in_grid(k, value):
            if k in (0, chunks - 1):
                keep = col_in_grid & (row_of(k) >= 0) & (row_of(k) < total_rows)
                return jnp.where(keep, value, 0.0)
            edge = jnp.where(col_in_grid[own:], value[own:], 0.0)
            return jnp.concatenate([value[:own], edge], 0)

        for n in range(steps):
            src, dst = frac[n], frac[n + 1]
            ahead, behind = {}, {}

            def update(k, src=src, dst=dst, n=n, behind=behind):
                fx, fy, fy_left, t = behind.pop(k)
                flow = fx - get(fluxx.at[n], k, -1) + (fy - fy_left)
                put(dst, k, get(src, k) + (flow - t) * get(rs, k))

            for k in range(chunks + LEAD):
                if k < chunks:
                    ahead[k] = right(get(src, k))
                if k >= LEAD:
                    j = k - LEAD
                    f, m = get(src, j), get(mat, j)
                    fx = get(cx, j) * (get(src, j, 1) - f)
                    put(fluxx.at[n], j, fx)
                    fy = get(cy, j) * (ahead.pop(j) - f)
                    put(fluxy.at[n], j, fy)
                    t = get(shp, j) * (f - m)
                    put(moved.at[n], j, t)
                    put(mat, j, m + t * get(rm, j))
                    behind[j] = (fx, fy, left(fy), t)
                    if j >= LAG:
                        update(j - LAG)
            for j in range(chunks - LAG, chunks):
                update(j)
            for p in range(pumps):
                lr, lt, ll, ok = pump_spots[p]

                @pl.when(ok)
                def _(lr=lr, lt=lt, ll=ll, p=p, n=n, dst=dst):
                    at = pl.ds(lr, 1)
                    dst[lt, at, :] += jnp.where(one_lane == ll, prs[p, n], 0.0) * rs[lt, at, :]

        for k in range(chunks):
            a = get(adj, k) + inject(k, steps)
            put(adj, k, a)
            put(scaled.at[steps % 2], k, a * get(rs, k))
        for n in reversed(range(steps)):
            old, new = scaled.at[(n + 1) % 2], scaled.at[n % 2]
            ahead, behind, ends = {}, {}, {}

            def update(k, n=n, new=new, behind=behind):
                sx, sy, sy_left, swap = behind.pop(k)
                a = get(adj, k) + (sx - get(flux, k, -1) + (sy - sy_left)) + swap
                if n > 0:
                    a = a + inject(k, n)
                    put(new, k, a * get(rs, k))
                put(adj, k, a)

            def close(k, ends=ends):
                gx, gy, gy_left = ends.pop(k)
                total = gx + get(prod, k, -1) + (gy + gy_left)
                gc = -0.5 * get(res, k) * total
                put(grad.at[0], k, in_grid(k, gc))

            for k in range(chunks + LEAD):
                if k < chunks:
                    ahead[k] = right(get(old, k))
                if k < LEAD:
                    continue
                j = k - LEAD
                s = get(old, j)
                sx = get(cx, j) * (get(old, j, 1) - s)
                put(flux, j, sx)
                sy = get(cy, j) * (ahead.pop(j) - s)
                am = get(adm, j)
                q = am * get(rm, j) - s
                swap = get(shp, j) * q
                put(adm, j, am - swap)
                gx = get(fluxx.at[n], j) * sx
                gy = get(fluxy.at[n], j) * sy
                gs = get(moved.at[n], j) * q
                if n < steps - 1:
                    gx += get(px_, j)
                    gy += get(py_, j)
                    gs += get(gs_, j)
                behind[j] = (sx, sy, left(sy), swap)
                if n > 0:
                    put(px_, j, gx)
                    put(py_, j, gy)
                    put(gs_, j, gs)
                else:
                    put(prod, j, gx)
                    ends[j] = (gx, gy, left(gy))
                    put(grad.at[1], j, in_grid(j, gs))
                if j >= LAG:
                    update(j - LAG)
                    if n == 0:
                        close(j - LAG)
            for j in range(chunks - LAG, chunks):
                update(j)
                if n == 0:
                    close(j)

        out_copies = []
        for q, (source, out) in enumerate(((adj, frac_out), (adm, mat_out))):
            for t in range(own):
                out_copies.append(
                    pltpu.make_async_copy(
                        source.at[t, pl.ds(2 * EDGE, tile_rows)],
                        out.at[:, pl.ds(LANES * t, LANES)],
                        mid_sem.at[q, t],
                    )
                )
        for copy in out_copies:
            copy.start()

        def blur(source, ks, emit):
            turned = {}
            for i in range(len(ks) + LEAD):
                if i < len(ks):
                    g = get(source, ks[i])
                    turned[i] = left(g) + right(g)
                if i >= LEAD:
                    k = ks[i - LEAD]
                    around = get(source, k, -1) + get(source, k, 1) + turned.pop(i - LEAD)
                    emit(k, (1.0 - 4.0 * BLEND) * get(source, k) + BLEND * around)

        for q in range(2):

            def first(k, value, q=q):
                put(grad2.at[q], k, in_grid(k, value))

            blur(grad.at[q], list(range(chunks)), first)
        for q in range(2):

            def second(k, value, q=q):
                for t in range(own):
                    smooth_out[q, EDGE * (k - 1) : EDGE * k, LANES * t : LANES * (t + 1)] = value[t]

            blur(grad2.at[q], list(range(1, chunks - 1)), second)
        for copy in out_copies:
            copy.wait()

    flat = jax.ShapeDtypeStruct((tile_rows, tile_cols), f32)
    made = pl.pallas_call(
        kernel,
        out_shape=[vmem_like(x.shape) for x in prepared]
        + [vmem_like((2, tile_rows, tile_cols)), flat, flat],
        in_specs=[HBM] * 2 + [VMEM] * (2 + kept + nxr + nyr),
        out_specs=[VMEM] * (kept + 1) + [HBM] * 2,
        input_output_aliases={4 + i: i for i in range(kept)},
        scratch_shapes=[
            pltpu.VMEM((steps,) + big, f32),
            pltpu.VMEM((steps,) + big, f32),
            pltpu.VMEM((steps,) + big, f32),
            pltpu.VMEM((steps,) + big, f32),
            pltpu.VMEM((2,) + big, f32),
            pltpu.VMEM(big, f32),
            pltpu.VMEM(big, f32),
            pltpu.VMEM(big, f32),
            pltpu.VMEM(big, f32),
            pltpu.VMEM(big, f32),
            pltpu.VMEM((2,) + big, f32),
            pltpu.VMEM((2,) + big, f32),
            pltpu.SMEM(storage.shape, f32),
            pltpu.SMEM(pump_rates.shape, f32),
            pltpu.SemaphoreType.DMA((FIELDS, own)),
            pltpu.SemaphoreType.DMA((2,)),
        ],
        compiler_params=grant(24),
        name="window",
    )(
        *(in_hbm(x) for x in scalars[:2]),
        *scalars[2:],
        *(in_vmem(x) for x in list(prepared) + list(row_in) + list(col_in)),
    )
    return made[kept:]


def add_parts(mine, theirs):
    def kernel(a_ref, b_ref, cond_ref, shape_ref):
        cond_ref[...] = a_ref[0] + b_ref[0]
        shape_ref[...] = a_ref[1] + b_ref[1]

    vmem = pl.BlockSpec(memory_space=pltpu.VMEM)
    flat = jax.ShapeDtypeStruct(mine.shape[1:], mine.dtype)
    return pl.pallas_call(
        kernel, out_shape=[flat] * 2, in_specs=[vmem] * 2, out_specs=[vmem] * 2, compiler_params=grant(4), name="add_parts"
    )(in_vmem(mine), in_vmem(theirs))


def on_device(
    log_cond,
    log_shape,
    zone_ids,
    storage,
    pump_x,
    pump_y,
    pump_rates,
    obs_x,
    obs_y,
    observed,
    frac_start,
    matrix_start,
    frac_end,
    matrix_end,
):
    nx, ny = lax.axis_size("tx"), lax.axis_size("ty")
    xr, yr = rounds_of(nx), rounds_of(ny)
    fields = (
        log_cond,
        log_shape,
        zone_ids,
        frac_start[0],
        matrix_start[0],
        frac_end[0],
        matrix_end[0],
    )
    rates = jnp.transpose(pump_rates, (0, 2, 1))[0]
    seen = jnp.transpose(observed, (1, 0, 2))
    col_in, row_in = [], []
    col_out = pack_columns(fields, yr)
    for m, py in zip(col_out, yr):
        col_in.append(lax.ppermute(m, "ty", pairs_of(ny, py)))
    wide, zone_mid, row_out = load_tile(fields, xr)
    row_out = add_corners(row_out, col_in, xr)
    for m, px in zip(row_out, xr):
        row_in.append(lax.ppermute(m, "tx", pairs_of(nx, px)))
    prepared = prepare_tile(wide, zone_mid, (storage, obs_x, obs_y, seen))
    part, fracture_adj, matrix_adj = window(
        prepared, (storage, rates, pump_x, pump_y), row_in, col_in, xr, yr, nx, ny
    )
    tests = lax.axis_size("test")
    if tests == 2:
        cond_sum, shape_sum = add_parts(part, lax.ppermute(part, "test", [(0, 1), (1, 0)]))
    else:
        cond_sum, shape_sum = lax.psum(part, "test")
    return (cond_sum, shape_sum, fracture_adj[None], matrix_adj[None])


def solution(mesh):
    placed = (
        P(("inv", "tx"), "ty"),
        P(("inv", "tx"), "ty"),
        P(("inv", "tx"), "ty"),
        P("inv", None),
        P(("inv", "test"), None),
        P(("inv", "test"), None),
        P(("inv", "test"), None, None),
        P("inv"),
        P("inv"),
        P(("inv", "test"), None, None),
        P(("inv", "test"), "tx", "ty"),
        P(("inv", "test"), "tx", "ty"),
        P(("inv", "test"), "tx", "ty"),
        P(("inv", "test"), "tx", "ty"),
    )
    return jax.shard_map(
        on_device,
        mesh=mesh,
        in_specs=placed,
        out_specs=(
            P(("inv", "tx"), "ty"),
            P(("inv", "tx"), "ty"),
            P(("inv", "test"), "tx", "ty"),
            P(("inv", "test"), "tx", "ty"),
        ),
        check_vma=False,
    )
```

time: 29.7 us -> 27.1 us (0.912)
  the two profiles are of different devices: /device:TPU:0 before, /device:TPU:13 now
where the time goes in v4:
time: 27.1 us; the launch traced here: 26.9 us
  Pallas kernels  14.7 us (54%)
  starting transfers between devices  8.22 us (30%)
  waiting for transfers between devices  1.99 us (7%)
  between operations  1.98 us (7%)
    pallas_call x1, Pallas kernels, window(): pl.pallas_call(kernel, out_shape=[vmem_like(x.shape) for x in prepared] +...  7.16 us
    ppermute x2, starting transfers between devices, on_device(): row_in.append(lax.ppermute(m, 'tx', pairs_of(nx, px)))  4.49 us
    pallas_call x1, Pallas kernels, prepare_tile(): pl.pallas_call(kernel, out_shape=[vmem_like(wide.shape)] + [vmem_like(big...  2.97 us
    ppermute x1, starting transfers between devices, on_device(): lax.ppermute(part, 'test', [(0, 1), (1, 0)])  2.45 us
    pallas_call x1, Pallas kernels, load_tile(): pl.pallas_call(kernel, out_shape=[vmem_like((FIELDS,) + big), vmem_like((...  1.81 us
    pallas_call x1, Pallas kernels, pack_columns(): pl.pallas_call(kernel, out_shape=[vmem_like((half, LANES))] * nyr, in_spe...  1.75 us
    ppermute x1, waiting for transfers between devices, on_device(): lax.ppermute(part, 'test', [(0, 1), (1, 0)])  1.72 us
    ppermute x1, starting transfers between devices, on_device(): col_in.append(lax.ppermute(m, 'ty', pairs_of(ny, py)))  1.28 us
  transfers between devices with their start and end apart: 4, of which 2 were waited for; matrix products, arithmetic and copies ran while one was open for 0% of the time, Pallas kernels for 18%

profile of v4, /device:TPU:13, one launch (start us, length us, event | category | flops | bytes accessed | tf_op | source)
XLA Modules:
  0.0 26.9 jit_solution(16644450806507803091)
XLA Ops:
  0.6 1.8 %pack_columns.1 = f32[160,128]{1,0:T(8,128)S(1)} custom-call(f32[320,256]{1,0:T(8,128)} %refs_0_.6, f32[320,256]{1,0:T(8,128)} %refs_1_.5, s32[320,256]{1,0:T(8,128)} %refs_2_.6, f32[320,256]{1,0:T(8,128)} %bitcast.8, f32[320,256]{1,0:T(8,128)} %bitcast.10, f32[320,256]{1,0:T(8,128)} %bitcast.12, f32[320,256]{1,0:T(8,128)} %bitcast.14), custom_call_target="tpu_custom_call" | custom-call | tf_op jit(solution)/shard_map/pack_columns/pallas_call | solution.py:98
  2.4 1.3 %collective-permute-start = (f32[160,128]{1,0:T(8,128)S(1)}, f32[160,128]{1,0:T(8,128)S(1)}, u32[]{:S(2)}, u32[]{:S(2)}) collective-permute-start(f32[160,128]{1,0:T(8,128)S(1)} %pack_columns.1), channel_id=1, source_target_pairs={{0,1},{1,0},{2,3},{3,2},{4,5},{5,4},{6,7},{7,6},{8,9},{9,8},{10,11... | collective-permute-start | bytes 245768 | tf_op jit(solution)/shard_map/ppermute | solution.py:703
  3.7 1.8 %load_tile.1 = (f32[7,3,352,128]{3,2,1,0:T(8,128)S(1)}, s32[2,320,128]{2,1,0:T(8,128)S(1)}, f32[64,256]{1,0:T(8,128)S(1)}, f32[64,256]{1,0:T(8,128)S(1)}) custom-call(f32[320,256]{1,0:T(8,128)} %refs_0_.6, f32[320,256]{1,0:T(8,128)} %refs_1_.5, s32[320,256]{1,0:T(8,128)} %refs_2_.6, f32[320,256]{1,0:T(8,128)} %bitcast.9, f32[320,256]{1,0:T(8,128)} %bitcast.11, ...), custom_call_target="tpu_custom_call" | custom-call | tf_op jit(solution)/shard_map/load_tile/pallas_call | solution.py:144
  5.5 0.3 collective-permute-done.refs_0_.refs_12_
  5.7 0.1 add_corners.1
  5.8 0.2 collective-permute-start.1
  6.0 4.3 %collective-permute-start.2 = (f32[64,256]{1,0:T(8,128)S(1)}, f32[64,256]{1,0:T(8,128)S(1)}, u32[]{:S(2)}, u32[]{:S(2)}) collective-permute-start(f32[64,256]{1,0:T(8,128)S(1)} %get-tuple-element.32), channel_id=1, source_target_pairs={{2,4},{4,2},{3,5},{5,3},{10,12},{12,10},{11,13},{13,11},{18,20},{2... | collective-permute-start | bytes 196616 | tf_op jit(solution)/shard_map/ppermute | solution.py:707
  11.6 3.0 %prepare_tile.1 = (f32[7,3,352,128]{3,2,1,0:T(8,128)S(1)}, f32[3,352,128]{2,1,0:T(8,128)S(1)}, f32[3,352,128]{2,1,0:T(8,128)S(1)}, f32[3,352,128]{2,1,0:T(8,128)...) custom-call(f32[2,8]{1,0:T(2,128)} %refs_0_.7, s32[64]{0:T(128)} %refs_1_.4, ...), custom_call_target="tpu_custom_call", output_to_operand_aliasing={{0}: (4, {})} | custom-call | tf_op jit(solution)/shard_map/prepare_tile/pallas_call | solution.py:308
  14.6 0.0 collective-permute-done.1.refs_10_
  14.6 0.0 collective-permute-done.2.refs_11_
  14.6 7.2 %window.1 = (f32[7,3,352,128]{3,2,1,0:T(8,128)S(1)}, f32[3,352,128]{2,1,0:T(8,128)S(1)}, f32[3,352,128]{2,1,0:T(8,128)S(1)}, f32[3,352,128]{2,1,0:T(8,128)S(1)},...) custom-call(f32[2,8]{1,0:T(2,128)} %refs_0_.7, ...), custom_call_target="tpu_custom_call", output_to_operand_aliasing={{0}: (4, {}), {1}: (5, {}), {2}: (6, {}), {3}: (7, {}), {4}... | custom-call | tf_op jit(solution)/shard_map/window/pallas_call | solution.py:624
  21.8 2.5 %collective-permute-start.3 = (f32[2,320,256]{2,1,0:T(8,128)S(1)}, f32[2,320,256]{2,1,0:T(8,128)S(1)}, u32[]{:S(2)}, u32[]{:S(2)}) collective-permute-start(f32[2,320,256]{2,1,0:T(8,128)S(1)} %get-tuple-element.33.a_ref), channel_id=1, source_target_pairs={{0,8},{8,0},{1,9},{9,1},{2,10},{10,2},{3,11},{11,3},{4,12},{12,4},... | collective-permute-start | bytes 1966088 | tf_op jit(solution)/shard_map/ppermute | solution.py:714
  24.2 1.7 %collective-permute-done.3.b_ref = f32[2,320,256]{2,1,0:T(8,128)S(1)} collective-permute-done((f32[2,320,256]{2,1,0:T(8,128)S(1)}, f32[2,320,256]{2,1,0:T(8,128)S(1)}, u32[]{:S(2)}, u32[]{:S(2)}) %collective-permute-start.3) | collective-permute-done | bytes 655392 | tf_op jit(solution)/shard_map/ppermute | solution.py:714
  26.0 0.9 %add_parts.1 = (f32[320,256]{1,0:T(8,128)}, f32[320,256]{1,0:T(8,128)}) custom-call(f32[2,320,256]{2,1,0:T(8,128)S(1)} %get-tuple-element.33.a_ref, f32[2,320,256]{2,1,0:T(8,128)S(1)} %collective-permute-done.3.b_ref), custom_call_target="tpu_custom_call" | custom-call | tf_op jit(solution)/shard_map/add_parts/pallas_call | solution.py:666
Async XLA Ops:
  2.4 3.4 %collective-permute-start = (f32[160,128]{1,0:T(8,128)S(1)}, f32[160,128]{1,0:T(8,128)S(1)}, u32[]{:S(2)}, u32[]{:S(2)}) collective-permute-start(f32[160,128]{1,0:T(8,128)S(1)} %pack_columns.1), channel_id=1, source_target_pairs={{0,1},{1,0},{2,3},{3,2},{4,5},{5,4},{6,7},{7,6},{8,9},{9,8},{10,11... | collective-permute-start | bytes 245768 | tf_op jit(solution)/shard_map/ppermute | solution.py:703
  5.8 8.8 %collective-permute-start.1 = (f32[64,256]{1,0:T(8,128)S(1)}, f32[64,256]{1,0:T(8,128)S(1)}, u32[]{:S(2)}, u32[]{:S(2)}) collective-permute-start(f32[64,256]{1,0:T(8,128)S(1)} %get-tuple-element.31), channel_id=1, source_target_pairs={{0,2},{2,0},{4,6},{6,4},{1,3},{3,1},{5,7},{7,5},{8,10},{10,8},{12,... | collective-permute-start | bytes 196616 | tf_op jit(solution)/shard_map/ppermute | solution.py:707
  6.0 8.6 %collective-permute-start.2 = (f32[64,256]{1,0:T(8,128)S(1)}, f32[64,256]{1,0:T(8,128)S(1)}, u32[]{:S(2)}, u32[]{:S(2)}) collective-permute-start(f32[64,256]{1,0:T(8,128)S(1)} %get-tuple-element.32), channel_id=1, source_target_pairs={{2,4},{4,2},{3,5},{5,3},{10,12},{12,10},{11,13},{13,11},{18,20},{2... | collective-permute-start | bytes 196616 | tf_op jit(solution)/shard_map/ppermute | solution.py:707
  21.8 4.2 %collective-permute-start.3 = (f32[2,320,256]{2,1,0:T(8,128)S(1)}, f32[2,320,256]{2,1,0:T(8,128)S(1)}, u32[]{:S(2)}, u32[]{:S(2)}) collective-permute-start(f32[2,320,256]{2,1,0:T(8,128)S(1)} %get-tuple-element.33.a_ref), channel_id=1, source_target_pairs={{0,8},{8,0},{1,9},{9,1},{2,10},{10,2},{3,11},{11,3},{4,12},{12,4},... | collective-permute-start | bytes 1966088 | tf_op jit(solution)/shard_map/ppermute | solution.py:714

commit v5 on v4

--- a/solution.py
+++ b/solution.py
@@ -74,26 +74,23 @@
                 )
         for copy in copies:
             copy.start()
-        for copy in copies:
-            copy.wait()
         slot = lane_iota(EDGE, LANES) // EDGE
         for j, py in enumerate(yr):
             shift = jnp.where(forward_of("ty", py), 1, 0)
-            masks = {}
-            for h in range(2):
-                for f in range(FIELDS):
-                    masks[h, f] = slot == lax.rem(f + 8 * h - shift + 16, 16)
-            for k in range(half // EDGE):
-                total = jnp.zeros((EDGE, LANES), jnp.float32)
+            totals = [jnp.zeros((EDGE, LANES), jnp.float32)] * (half // EDGE)
+            for f in range(FIELDS):
+                copies[j * FIELDS + f].wait()
                 for h in range(2):
-                    at = k * EDGE + h * half
-                    for f in range(FIELDS):
+                    mask = slot == lax.rem(f + 8 * h - shift + 16, 16)
+                    amount = EDGE * f + 64 * h
+                    for k in range(half // EDGE):
+                        at = k * EDGE + h * half
                         part = (zone_cols if f == 2 else cols.at[:, f])[j, at : at + EDGE, :]
-                        amount = EDGE * f + 64 * h
                         part = part.astype(jnp.float32)
                         part = pltpu.roll(part, amount, 1) if amount else part
-                        total = jnp.where(masks[h, f], part, total)
-                outs[j][EDGE * k : EDGE * (k + 1), :] = total
+                        totals[k] = jnp.where(mask, part, totals[k])
+            for k in range(half // EDGE):
+                outs[j][EDGE * k : EDGE * (k + 1), :] = totals[k]
 
     return pl.pallas_call(
         kernel,
@@ -116,9 +113,9 @@
 
     def kernel(*refs):
         ins = refs[:FIELDS]
-        wide, zone_mid = refs[FIELDS : FIELDS + 2]
-        outs = refs[FIELDS + 2 : FIELDS + 2 + nxr]
-        sem = refs[FIELDS + 2 + nxr]
+        wide, zone_mid, cx, cy = refs[FIELDS : FIELDS + 4]
+        outs = refs[FIELDS + 4 : FIELDS + 4 + nxr]
+        sem = refs[FIELDS + 4 + nxr]
         copies = []
         for f in range(FIELDS):
             for t in range(own):
@@ -139,131 +136,8 @@
                     else:
                         part = wide[f, t, pl.ds(start + 2 * EDGE, EDGE), :]
                     outs[i][EDGE * f : EDGE * (f + 1), LANES * t : LANES * (t + 1)] = part
-
-    big = (own + 1, tile_rows + 4 * EDGE, LANES)
-    made = pl.pallas_call(
-        kernel,
-        out_shape=[
-            vmem_like((FIELDS,) + big),
-            vmem_like((own, tile_rows, LANES), jnp.int32),
-        ]
-        + [vmem_like((EDGE * (FIELDS + 1), tile_cols))] * nxr,
-        in_specs=[HBM] * FIELDS,
-        out_specs=[VMEM] * (2 + nxr),
-        scratch_shapes=[pltpu.SemaphoreType.DMA((FIELDS, own))],
-        compiler_params=grant(4),
-        name="load_tile",
-    )(*(in_hbm(x) for x in fields))
-    return made[0], made[1], made[2:]
-
-
-def add_corners(row_out, col_in, xr):
-    nxr, nyr = len(xr), len(col_in)
-    assert nyr * LANES <= row_out[0].shape[1]
-
-    def kernel(*refs):
-        cols, outs = refs[:nyr], refs[nyr + nxr :]
-        for i, px in enumerate(xr):
-            outs[i][EDGE * FIELDS :, :] = jnp.zeros((EDGE, row_out[0].shape[1]), jnp.float32)
-            ahead = forward_of("tx", px)
-            for j in range(nyr):
-                top = cols[j][0:EDGE, :]
-                low = pltpu.roll(cols[j][cols[j].shape[0] - EDGE :, :], LANES // 2, 1)
-                outs[i][EDGE * FIELDS :, LANES * j : LANES * (j + 1)] = jnp.where(ahead, low, top)
-
-    return pl.pallas_call(
-        kernel,
-        out_shape=[vmem_like(x.shape) for x in row_out],
-        in_specs=[VMEM] * (nyr + nxr),
-        out_specs=[VMEM] * nxr,
-        input_output_aliases={nyr + i: i for i in range(nxr)},
-        compiler_params=grant(2),
-        name="add_corners",
-    )(*(in_vmem(x) for x in list(col_in) + list(row_out)))
-
-
-def grant(mib):
-    return pltpu.CompilerParams(vmem_limit_bytes=mib * 2**20)
-
-
-class Chunks:
-    def __init__(self, tile_rows):
-        self.count = tile_rows // EDGE + 2
-
-    @staticmethod
-    def at(k, shift=0):
-        return slice(EDGE * (k + 1) + shift, EDGE * (k + 2) + shift)
-
-
-def get(ref, k, shift=0):
-    return ref[:, Chunks.at(k, shift), :]
-
-
-def put(ref, k, value):
-    ref[:, Chunks.at(k), :] = value
-
-
-def turn_right(x, last_lane):
-    turned = pltpu.roll(x, LANES - 1, 2)
-    return jnp.where(last_lane, jnp.concatenate([turned[1:], turned[:1]], 0), turned)
-
-
-def turn_left(x, first_lane):
-    turned = pltpu.roll(x, 1, 2)
-    return jnp.where(first_lane, jnp.concatenate([turned[-1:], turned[:-1]], 0), turned)
-
-
-def store_tables(storage_ref, zones):
-    by_lane = lane_iota(EDGE, LANES)
-    tables = []
-    for kind in range(2):
-        table = jnp.full((EDGE, LANES), storage_ref[kind, 0], jnp.float32)
-        for z in range(1, zones):
-            table = jnp.where(by_lane == z, storage_ref[kind, z], table)
-        tables.append(1.0 / table)
-    return tables
-
-
-def look_up(table, index):
-    return jnp.take_along_axis(table, index, axis=1, mode="promise_in_bounds")
-
-
-def place_of(gx, gy, tile_rows, tile_cols):
-    lr = gx - lax.axis_index("tx") * tile_rows + EDGE
-    lc = gy - lax.axis_index("ty") * tile_cols
-    ok = (lr >= 0) & (lr < tile_rows + 2 * EDGE) & (lc >= -EDGE) & (lc < tile_cols + EDGE)
-    at = jnp.where(lc < 0, lc + tile_cols + LANES, lc)
-    return lr + EDGE, at // LANES, lax.rem(at, LANES), ok
-
-
-def prepare_tile(wide, zone_mid, scalars):
-    storage, _, _, observed = scalars
-    tile_rows = zone_mid.shape[1]
-    own = zone_mid.shape[0]
-    tile_cols = own * LANES
-    big = wide.shape[1:]
-    zones = storage.shape[1]
-    steps, wells = observed.shape[0], observed.shape[2]
-    chunks = Chunks(tile_rows).count
-    f32 = jnp.float32
-
-    def kernel(*refs):
-        small_in, zone_in = refs[:4], refs[5]
-        wide, rm, cx, cy, count, seen = refs[6:12]
-        st, oxs, oys, obs = refs[12:16]
-        sem = refs[16]
-        copies = [
-            pltpu.make_async_copy(a, b, sem.at[i])
-            for i, (a, b) in enumerate(zip(small_in, (st, oxs, oys, obs)))
-        ]
-        for copy in copies:
-            copy.start()
-        res, shp, rs = wide.at[0], wide.at[1], wide.at[2]
-        zero = jnp.zeros((own + 1, EDGE, LANES), f32)
-        for k in range(chunks):
-            put(count, k, zero)
-            for n in range(steps):
-                put(seen.at[n], k, zero)
+        chunks = Chunks(tile_rows).count
+        res, shp = wide.at[0], wide.at[1]
         for k in range(1, chunks - 1):
             res[0:own, Chunks.at(k), :] = jnp.exp(-res[0:own, Chunks.at(k), :])
             shp[0:own, Chunks.at(k), :] = jnp.exp(shp[0:own, Chunks.at(k), :])
@@ -280,6 +154,133 @@
                     below = res[0:own, Chunks.at(j, 1), :]
                     cx[0:own, Chunks.at(j), :] = 2.0 / (here + below)
                 cy[0 : own - 1, Chunks.at(j), :] = 2.0 / (here[: own - 1] + ahead.pop(j))
+
+    big = (own + 1, tile_rows + 4 * EDGE, LANES)
+    made = pl.pallas_call(
+        kernel,
+        out_shape=[
+            vmem_like((FIELDS,) + big),
+            vmem_like((own, tile_rows, LANES), jnp.int32),
+            vmem_like(big),
+            vmem_like(big),
+        ]
+        + [vmem_like((EDGE * (FIELDS + 1), tile_cols))] * nxr,
+        in_specs=[HBM] * FIELDS,
+        out_specs=[VMEM] * (4 + nxr),
+        scratch_shapes=[pltpu.SemaphoreType.DMA((FIELDS, own))],
+        compiler_params=grant(4),
+        name="load_tile",
+    )(*(in_hbm(x) for x in fields))
+    return made[:2], made[2:4], made[4:]
+
+
+def add_corners(row_out, col_in, xr):
+    nxr, nyr = len(xr), len(col_in)
+    assert nyr * LANES <= row_out[0].shape[1]
+
+    def kernel(*refs):
+        cols, outs = refs[:nyr], refs[nyr + nxr :]
+        for i, px in enumerate(xr):
+            outs[i][EDGE * FIELDS :, :] = jnp.zeros((EDGE, row_out[0].shape[1]), jnp.float32)
+            ahead = forward_of("tx", px)
+            for j in range(nyr):
+                top = cols[j][0:EDGE, :]
+                low = pltpu.roll(cols[j][cols[j].shape[0] - EDGE :, :], LANES // 2, 1)
+                outs[i][EDGE * FIELDS :, LANES * j : LANES * (j + 1)] = jnp.where(ahead, low, top)
+
+    return pl.pallas_call(
+        kernel,
+        out_shape=[vmem_like(x.shape) for x in row_out],
+        in_specs=[VMEM] * (nyr + nxr),
+        out_specs=[VMEM] * nxr,
+        input_output_aliases={nyr + i: i for i in range(nxr)},
+        compiler_params=grant(2),
+        name="add_corners",
+    )(*(in_vmem(x) for x in list(col_in) + list(row_out)))
+
+
+def grant(mib):
+    return pltpu.CompilerParams(vmem_limit_bytes=mib * 2**20)
+
+
+class Chunks:
+    def __init__(self, tile_rows):
+        self.count = tile_rows // EDGE + 2
+
+    @staticmethod
+    def at(k, shift=0):
+        return slice(EDGE * (k + 1) + shift, EDGE * (k + 2) + shift)
+
+
+def get(ref, k, shift=0):
+    return ref[:, Chunks.at(k, shift), :]
+
+
+def put(ref, k, value):
+    ref[:, Chunks.at(k), :] = value
+
+
+def turn_right(x, last_lane):
+    turned = pltpu.roll(x, LANES - 1, 2)
+    return jnp.where(last_lane, jnp.concatenate([turned[1:], turned[:1]], 0), turned)
+
+
+def turn_left(x, first_lane):
+    turned = pltpu.roll(x, 1, 2)
+    return jnp.where(first_lane, jnp.concatenate([turned[-1:], turned[:-1]], 0), turned)
+
+
+def store_tables(storage_ref, zones):
+    by_lane = lane_iota(EDGE, LANES)
+    tables = []
+    for kind in range(2):
+        table = jnp.full((EDGE, LANES), storage_ref[kind, 0], jnp.float32)
+        for z in range(1, zones):
+            table = jnp.where(by_lane == z, storage_ref[kind, z], table)
+        tables.append(1.0 / table)
+    return tables
+
+
+def look_up(table, index):
+    return jnp.take_along_axis(table, index, axis=1, mode="promise_in_bounds")
+
+
+def place_of(gx, gy, tile_rows, tile_cols):
+    lr = gx - lax.axis_index("tx") * tile_rows + EDGE
+    lc = gy - lax.axis_index("ty") * tile_cols
+    ok = (lr >= 0) & (lr < tile_rows + 2 * EDGE) & (lc >= -EDGE) & (lc < tile_cols + EDGE)
+    at = jnp.where(lc < 0, lc + tile_cols + LANES, lc)
+    return lr + EDGE, at // LANES, lax.rem(at, LANES), ok
+
+
+def prepare_tile(wide, zone_mid, scalars):
+    storage, _, _, observed = scalars
+    tile_rows = zone_mid.shape[1]
+    own = zone_mid.shape[0]
+    tile_cols = own * LANES
+    big = wide.shape[1:]
+    zones = storage.shape[1]
+    steps, wells = observed.shape[0], observed.shape[2]
+    chunks = Chunks(tile_rows).count
+    f32 = jnp.float32
+
+    def kernel(*refs):
+        small_in, zone_in = refs[:4], refs[5]
+        wide, rm, count, seen = refs[6:10]
+        st, oxs, oys, obs = refs[10:14]
+        sem = refs[14]
+        copies = [
+            pltpu.make_async_copy(a, b, sem.at[i])
+            for i, (a, b) in enumerate(zip(small_in, (st, oxs, oys, obs)))
+        ]
+        for copy in copies:
+            copy.start()
+        rs = wide.at[2]
+        zero = jnp.zeros((own + 1, EDGE, LANES), f32)
+        for k in range(-1, chunks):
+            put(count, k, zero)
+            for n in range(steps):
+                put(seen.at[n], k, zero)
         for copy in copies:
             copy.wait()
         tables = store_tables(st, zones)
@@ -292,24 +293,21 @@
 
         def well(o, carry):
             lr, lt, ll, ok = place_of(oxs[o], oys[o], tile_rows, tile_cols)
-
-            @pl.when(ok)
-            def _():
-                hit = one_lane == ll
-                at = pl.ds(lr, 1)
-                count[lt, at, :] += jnp.where(hit, 1.0, 0.0)
-                for n in range(steps):
-                    seen[n, lt, at, :] += jnp.where(hit, obs[n, 0, o], 0.0)
-
+            at = pl.ds(jnp.where(ok, lr, 0), 1)
+            lt = jnp.where(ok, lt, 0)
+            hit = one_lane == jnp.where(ok, ll, -1)
+            count[lt, at, :] += jnp.where(hit, 1.0, 0.0)
+            for n in range(steps):
+                seen[n, lt, at, :] += jnp.where(hit, obs[n, 0, o], 0.0)
             return carry
 
-        lax.fori_loop(0, wells, well, 0)
+        lax.fori_loop(0, wells, well, 0, unroll=8 if wells % 8 == 0 else 1)
 
     return pl.pallas_call(
         kernel,
-        out_shape=[vmem_like(wide.shape)] + [vmem_like(big)] * 4 + [vmem_like((steps,) + big)],
+        out_shape=[vmem_like(wide.shape)] + [vmem_like(big)] * 2 + [vmem_like((steps,) + big)],
         in_specs=[HBM] * 4 + [VMEM] * 2,
-        out_specs=[VMEM] * 6,
+        out_specs=[VMEM] * 4,
         input_output_aliases={4: 0},
         scratch_shapes=[pltpu.SMEM(x.shape, x.dtype) for x in scalars]
         + [pltpu.SemaphoreType.DMA((4,))],
@@ -318,8 +316,65 @@
     )(*(in_hbm(x) for x in scalars), in_vmem(wide), in_vmem(zone_mid))
 
 
+def masked(k, value, tile_rows, nx, ny):
+    block = (1, EDGE, LANES)
+    lane = lax.broadcasted_iota(jnp.int32, block, 2)
+    after = jnp.where(lax.axis_index("ty") < ny - 1, 1, 0)
+    before = jnp.where(lax.axis_index("ty") > 0, 1, 0)
+    keep = jnp.where(lane < LANES // 2, after, before) > 0
+    value = jnp.concatenate([value[:-1], jnp.where(keep, value[-1:], 0.0)], 0)
+    if k in (0, tile_rows // EDGE + 1):
+        tx = lax.axis_index("tx")
+        value = jnp.where(tx > 0 if k == 0 else tx < nx - 1, value, 0.0)
+    return value
+
+
+def smooth(grad, middle, out, nx, ny):
+    tile_rows = out.shape[0]
+    chunks = Chunks(tile_rows).count
+    lane = lax.broadcasted_iota(jnp.int32, (grad.shape[0], EDGE, LANES), 2)
+    last_lane, first_lane = lane == LANES - 1, lane == 0
+
+    def blur(source, ks, emit):
+        turned = {}
+        for i in range(len(ks) + LEAD):
+            if i < len(ks):
+                g = get(source, ks[i])
+                turned[i] = turn_left(g, first_lane) + turn_right(g, last_lane)
+            if i >= LEAD:
+                k = ks[i - LEAD]
+                around = get(source, k, -1) + get(source, k, 1) + turned.pop(i - LEAD)
+                emit(k, (1.0 - 4.0 * BLEND) * get(source, k) + BLEND * around)
+
+    def first(k, value):
+        put(middle, k, masked(k, value, tile_rows, nx, ny))
+
+    def second(k, value):
+        for t in range(grad.shape[0] - 1):
+            out[EDGE * (k - 1) : EDGE * k, LANES * t : LANES * (t + 1)] = value[t]
+
+    blur(grad, list(range(chunks)), first)
+    blur(middle, list(range(1, chunks - 1)), second)
+
+
+def smooth_alone(grad, tile_rows, nx, ny):
+    def kernel(grad_ref, out_ref, middle):
+        smooth(grad_ref, middle, out_ref, nx, ny)
+
+    tile_cols = (grad.shape[0] - 1) * LANES
+    return pl.pallas_call(
+        kernel,
+        out_shape=vmem_like((tile_rows, tile_cols)),
+        in_specs=[VMEM],
+        out_specs=VMEM,
+        scratch_shapes=[pltpu.VMEM(grad.shape, jnp.float32)],
+        compiler_params=grant(4),
+        name="smooth_alone",
+    )(in_vmem(grad))
+
+
 def window(prepared, scalars, row_in, col_in, xr, yr, nx, ny):
-    storage, pump_rates, _, _ = scalars
+    storage, pump_rates, pump_at = scalars
     zones = storage.shape[1]
     pumps, steps = pump_rates.shape
     tiles, _, _ = big = prepared[1].shape
@@ -340,15 +395,14 @@
             pos += count
             return refs[pos - count : pos]
 
-        small_in = take(2)
-        pump_at = take(2)
+        small_in = take(3)
         take(kept)
         rin, cin = take(nxr), take(nyr)
         (wide, rm, cx, cy, count, seen) = take(kept)
-        smooth_out, frac_out, mat_out = take(3)
+        grad0, smooth_out, frac_out, mat_out = take(4)
         (later, fluxx, fluxy, moved, scaled, flux, prod) = take(7)
-        (px_, py_, gs_, grad, grad2) = take(5)
-        (st, prs) = take(2)
+        (px_, py_, gs_, grad1, grad2) = take(5)
+        (st, prs, spot) = take(3)
         (mid_sem, small_sem) = take(2)
         res, shp, rs = wide.at[0], wide.at[1], wide.at[2]
         mat, adj, adm = wide.at[4], wide.at[5], wide.at[6]
@@ -357,7 +411,7 @@
 
         small = [
             pltpu.make_async_copy(a, b, small_sem.at[i])
-            for i, (a, b) in enumerate(zip(small_in, (st, prs)))
+            for i, (a, b) in enumerate(zip(small_in, (st, prs, spot)))
         ]
         for copy in small:
             copy.start()
@@ -368,7 +422,7 @@
                 put(wide.at[f], 0, zero)
                 put(wide.at[f], chunks - 1, zero)
         for ref in (
-            [res, grad.at[0], grad.at[1], grad2.at[0], grad2.at[1], flux, prod]
+            [res, grad0, grad1, grad2, flux, prod]
             + frac
             + [fluxx.at[n] for n in range(steps)]
             + [scaled.at[n] for n in range(2)]
@@ -398,13 +452,10 @@
 
         one_lane = lane_iota(1, LANES)
 
-        def number(ref, p):
-            there = lax.broadcasted_iota(jnp.int32, (1, pumps), 1) == p
-            return jnp.sum(jnp.where(there, ref[...], 0))
-
+        for copy in small:
+            copy.wait()
         pump_spots = [
-            place_of(number(pump_at[0], p), number(pump_at[1], p), tile_rows, tile_cols)
-            for p in range(pumps)
+            place_of(spot[0, p], spot[0, pumps + p], tile_rows, tile_cols) for p in range(pumps)
         ]
 
         tops = []
@@ -445,8 +496,6 @@
         def inject(k, n):
             return get(count, k) * get(frac[n], k) - get(seen.at[n - 1], k)
 
-        for copy in small:
-            copy.wait()
         tables = store_tables(st, zones)
         for k in range(chunks):
             at = Chunks.at(k)
@@ -478,11 +527,7 @@
             cy[t:, at, :] = jnp.where(col_face[t:], beside, 0.0)
 
         def in_grid(k, value):
-            if k in (0, chunks - 1):
-                keep = col_in_grid & (row_of(k) >= 0) & (row_of(k) < total_rows)
-                return jnp.where(keep, value, 0.0)
-            edge = jnp.where(col_in_grid[own:], value[own:], 0.0)
-            return jnp.concatenate([value[:own], edge], 0)
+            return masked(k, value, tile_rows, nx, ny)
 
         for n in range(steps):
             src, dst = frac[n], frac[n + 1]
@@ -539,7 +584,7 @@
                 gx, gy, gy_left = ends.pop(k)
                 total = gx + get(prod, k, -1) + (gy + gy_left)
                 gc = -0.5 * get(res, k) * total
-                put(grad.at[0], k, in_grid(k, gc))
+                put(grad0, k, in_grid(k, gc))
 
             for k in range(chunks + LEAD):
                 if k < chunks:
@@ -570,7 +615,7 @@
                 else:
                     put(prod, j, gx)
                     ends[j] = (gx, gy, left(gy))
-                    put(grad.at[1], j, in_grid(j, gs))
+                    put(grad1, j, in_grid(j, gs))
                 if j >= LAG:
                     update(j - LAG)
                     if n == 0:
@@ -593,30 +638,7 @@
         for copy in out_copies:
             copy.start()
 
-        def blur(source, ks, emit):
-            turned = {}
-            for i in range(len(ks) + LEAD):
-                if i < len(ks):
-                    g = get(source, ks[i])
-                    turned[i] = left(g) + right(g)
-                if i >= LEAD:
-                    k = ks[i - LEAD]
-                    around = get(source, k, -1) + get(source, k, 1) + turned.pop(i - LEAD)
-                    emit(k, (1.0 - 4.0 * BLEND) * get(source, k) + BLEND * around)
-
-        for q in range(2):
-
-            def first(k, value, q=q):
-                put(grad2.at[q], k, in_grid(k, value))
-
-            blur(grad.at[q], list(range(chunks)), first)
-        for q in range(2):
-
-            def second(k, value, q=q):
-                for t in range(own):
-                    smooth_out[q, EDGE * (k - 1) : EDGE * k, LANES * t : LANES * (t + 1)] = value[t]
-
-            blur(grad2.at[q], list(range(1, chunks - 1)), second)
+        smooth(grad1, grad2, smooth_out, nx, ny)
         for copy in out_copies:
             copy.wait()
 
@@ -624,10 +646,10 @@
     made = pl.pallas_call(
         kernel,
         out_shape=[vmem_like(x.shape) for x in prepared]
-        + [vmem_like((2, tile_rows, tile_cols)), flat, flat],
-        in_specs=[HBM] * 2 + [VMEM] * (2 + kept + nxr + nyr),
-        out_specs=[VMEM] * (kept + 1) + [HBM] * 2,
-        input_output_aliases={4 + i: i for i in range(kept)},
+        + [vmem_like(big), vmem_like((tile_rows, tile_cols)), flat, flat],
+        in_specs=[HBM] * 3 + [VMEM] * (kept + nxr + nyr),
+        out_specs=[VMEM] * (kept + 2) + [HBM] * 2,
+        input_output_aliases={3 + i: i for i in range(kept)},
         scratch_shapes=[
             pltpu.VMEM((steps,) + big, f32),
             pltpu.VMEM((steps,) + big, f32),
@@ -639,32 +661,35 @@
             pltpu.VMEM(big, f32),
             pltpu.VMEM(big, f32),
             pltpu.VMEM(big, f32),
-            pltpu.VMEM((2,) + big, f32),
-            pltpu.VMEM((2,) + big, f32),
+            pltpu.VMEM(big, f32),
+            pltpu.VMEM(big, f32),
             pltpu.SMEM(storage.shape, f32),
             pltpu.SMEM(pump_rates.shape, f32),
+            pltpu.SMEM(pump_at.shape, jnp.int32),
             pltpu.SemaphoreType.DMA((FIELDS, own)),
-            pltpu.SemaphoreType.DMA((2,)),
+            pltpu.SemaphoreType.DMA((3,)),
         ],
         compiler_params=grant(24),
         name="window",
     )(
-        *(in_hbm(x) for x in scalars[:2]),
-        *scalars[2:],
+        *(in_hbm(x) for x in scalars),
         *(in_vmem(x) for x in list(prepared) + list(row_in) + list(col_in)),
     )
     return made[kept:]
 
 
 def add_parts(mine, theirs):
-    def kernel(a_ref, b_ref, cond_ref, shape_ref):
-        cond_ref[...] = a_ref[0] + b_ref[0]
-        shape_ref[...] = a_ref[1] + b_ref[1]
-
-    vmem = pl.BlockSpec(memory_space=pltpu.VMEM)
-    flat = jax.ShapeDtypeStruct(mine.shape[1:], mine.dtype)
+    def kernel(a_ref, b_ref, out_ref):
+        out_ref[...] = a_ref[...] + b_ref[...]
+
+    flat = jax.ShapeDtypeStruct(mine.shape, mine.dtype)
     return pl.pallas_call(
-        kernel, out_shape=[flat] * 2, in_specs=[vmem] * 2, out_specs=[vmem] * 2, compiler_params=grant(4), name="add_parts"
+        kernel,
+        out_shape=flat,
+        in_specs=[VMEM] * 2,
+        out_specs=VMEM,
+        compiler_params=grant(4),
+        name="add_parts",
     )(in_vmem(mine), in_vmem(theirs))
 
 
@@ -701,19 +726,25 @@
     col_out = pack_columns(fields, yr)
     for m, py in zip(col_out, yr):
         col_in.append(lax.ppermute(m, "ty", pairs_of(ny, py)))
-    wide, zone_mid, row_out = load_tile(fields, xr)
+    (wide, zone_mid), links, row_out = load_tile(fields, xr)
     row_out = add_corners(row_out, col_in, xr)
     for m, px in zip(row_out, xr):
         row_in.append(lax.ppermute(m, "tx", pairs_of(nx, px)))
-    prepared = prepare_tile(wide, zone_mid, (storage, obs_x, obs_y, seen))
-    part, fracture_adj, matrix_adj = window(
-        prepared, (storage, rates, pump_x, pump_y), row_in, col_in, xr, yr, nx, ny
+    made = prepare_tile(wide, zone_mid, (storage, obs_x, obs_y, seen))
+    prepared = list(made[:2]) + list(links) + list(made[2:])
+    cond_grad, shape_part, fracture_adj, matrix_adj = window(
+        prepared, (storage, rates, jnp.concatenate([pump_x, pump_y], 1)), row_in, col_in, xr, yr, nx, ny
     )
-    tests = lax.axis_size("test")
-    if tests == 2:
-        cond_sum, shape_sum = add_parts(part, lax.ppermute(part, "test", [(0, 1), (1, 0)]))
+    if lax.axis_size("test") == 2:
+        other = [(0, 1), (1, 0)]
+        shape_other = lax.ppermute(shape_part, "test", other)
+        cond_part = smooth_alone(cond_grad, log_cond.shape[0], nx, ny)
+        cond_other = lax.ppermute(cond_part, "test", other)
+        shape_sum = add_parts(shape_part, shape_other)
+        cond_sum = add_parts(cond_part, cond_other)
     else:
-        cond_sum, shape_sum = lax.psum(part, "test")
+        cond_part = smooth_alone(cond_grad, log_cond.shape[0], nx, ny)
+        cond_sum, shape_sum = lax.psum((cond_part, shape_part), "test")
     return (cond_sum, shape_sum, fracture_adj[None], matrix_adj[None])
 
 

time: 27.1 us -> 28 us (1.033)
  the two profiles are of different devices: /device:TPU:13 before, /device:TPU:17 now
where the time goes in v5:
time: 28 us; the launch traced here: 27.7 us
  Pallas kernels  14.4 us (51%)
  starting transfers between devices  7.03 us (25%)
  waiting for transfers between devices  3.68 us (13%)
  between operations  1.98 us (7%)
  other arithmetic  0.59 us (2%)
    pallas_call x1, Pallas kernels, window(): pl.pallas_call(kernel, out_shape=[vmem_like(x.shape) for x in prepared] +...  6.3 us
    ppermute x2, starting transfers between devices, on_device(): row_in.append(lax.ppermute(m, 'tx', pairs_of(nx, px)))  3.22 us
    ppermute x2, waiting for transfers between devices, on_device(): row_in.append(lax.ppermute(m, 'tx', pairs_of(nx, px)))  2.49 us
    ppermute x1, starting transfers between devices, on_device(): cond_other = lax.ppermute(cond_part, 'test', other)  2.45 us
    pallas_call x1, Pallas kernels, prepare_tile(): pl.pallas_call(kernel, out_shape=[vmem_like(wide.shape)] + [vmem_like(big...  2.17 us
    pallas_call x1, Pallas kernels, load_tile(): pl.pallas_call(kernel, out_shape=[vmem_like((FIELDS,) + big), vmem_like((...  2.06 us
    pallas_call x1, Pallas kernels, pack_columns(): pl.pallas_call(kernel, out_shape=[vmem_like((half, LANES))] * nyr, in_spe...  1.74 us
    pallas_call x2, Pallas kernels, add_parts(): pl.pallas_call(kernel, out_shape=flat, in_specs=[VMEM] * 2, out_specs=VME...  1.52 us
  transfers between devices with their start and end apart: 5, of which 2 were waited for; matrix products, arithmetic and copies ran while one was open for 2% of the time, Pallas kernels for 18%

profile of v5, /device:TPU:17, one launch (start us, length us, event | category | flops | bytes accessed | tf_op | source)
XLA Modules:
  0.0 27.7 jit_solution(10497285821350973747)
XLA Ops:
  0.6 1.7 %pack_columns.1 = f32[160,128]{1,0:T(8,128)S(1)} custom-call(f32[320,256]{1,0:T(8,128)} %refs_0_.6, f32[320,256]{1,0:T(8,128)} %refs_1_.5, s32[320,256]{1,0:T(8,128)} %refs_2_.5, f32[320,256]{1,0:T(8,128)} %bitcast.8, f32[320,256]{1,0:T(8,128)} %bitcast.10, f32[320,256]{1,0:T(8,128)} %bitcast.12, f32[320,256]{1,0:T(8,128)} %bitcast.14), custom_call_target="tpu_custom_call" | custom-call | tf_op jit(solution)/shard_map/pack_columns/pallas_call | solution.py:95
  2.4 1.3 %collective-permute-start = (f32[160,128]{1,0:T(8,128)S(1)}, f32[160,128]{1,0:T(8,128)S(1)}, u32[]{:S(2)}, u32[]{:S(2)}) collective-permute-start(f32[160,128]{1,0:T(8,128)S(1)} %pack_columns.1), channel_id=1, source_target_pairs={{0,1},{1,0},{2,3},{3,2},{4,5},{5,4},{6,7},{7,6},{8,9},{9,8},{10,11... | collective-permute-start | bytes 245768 | tf_op jit(solution)/shard_map/ppermute | solution.py:728
  3.7 2.1 %load_tile.1 = (f32[7,3,352,128]{3,2,1,0:T(8,128)S(1)}, s32[2,320,128]{2,1,0:T(8,128)S(1)}, f32[3,352,128]{2,1,0:T(8,128)S(1)}, f32[3,352,128]{2,1,0:T(8,128)S(1...) custom-call(f32[320,256]{1,0:T(8,128)} %refs_0_.6, f32[320,256]{1,0:T(8,128)} %refs_1_.5, s32[320,256]{1,0:T(8,128)} %refs_2_.5, ...), custom_call_target="tpu_custom_call" | custom-call | tf_op jit(solution)/shard_map/load_tile/pallas_call | solution.py:159
  7.0 2.2 %prepare_tile.1 = (f32[7,3,352,128]{3,2,1,0:T(8,128)S(1)}, f32[3,352,128]{2,1,0:T(8,128)S(1)}, f32[3,352,128]{2,1,0:T(8,128)S(1)}, f32[3,3,352,128]{3,2,1,0:T(8,128)S(1)}) custom-call(f32[2,8]{1,0:T(2,128)} %refs_0_.7, s32[64]{0:T(128)} %refs_1_.4, s32[64]{0:T(128)} %refs_2_.4, f32[3,1,64]{2,1,0:T(1,128)} %bitcast.16, ...), custom_call_target="tpu_custom_call", output_to_operand_aliasing={{0}: (4, {})} | custom-call | tf_op jit(solution)/shard_map/prepare_tile/pallas_call | solution.py:306
  9.2 0.0 collective-permute-done.refs_0_.refs_11_
  9.2 0.1 add_corners.1
  9.3 1.3 %collective-permute-start.1 = (f32[64,256]{1,0:T(8,128)S(1)}, f32[64,256]{1,0:T(8,128)S(1)}, u32[]{:S(2)}, u32[]{:S(2)}) collective-permute-start(f32[64,256]{1,0:T(8,128)S(1)} %get-tuple-element.30), channel_id=1, source_target_pairs={{0,2},{2,0},{4,6},{6,4},{1,3},{3,1},{5,7},{7,5},{8,10},{10,8},{12,... | collective-permute-start | bytes 196616 | tf_op jit(solution)/shard_map/ppermute | solution.py:732
  10.6 1.9 %collective-permute-start.2 = (f32[64,256]{1,0:T(8,128)S(1)}, f32[64,256]{1,0:T(8,128)S(1)}, u32[]{:S(2)}, u32[]{:S(2)}) collective-permute-start(f32[64,256]{1,0:T(8,128)S(1)} %get-tuple-element.31), channel_id=1, source_target_pairs={{2,4},{4,2},{3,5},{5,3},{10,12},{12,10},{11,13},{13,11},{18,20},{2... | collective-permute-start | bytes 196616 | tf_op jit(solution)/shard_map/ppermute | solution.py:732
  12.5 0.6 %pad_add_fusion.refs_2_ = s32[1,2]{1,0:T(1,128)} fusion(s32[1,1]{1,0:T(1,128)S(6)} %copy.37, s32[1,1]{1,0:T(1,128)S(6)} %copy.36), kind=kLoop, calls=%fused_computation | loop fusion | flops 2 | bytes 16 | tf_op jit(solution)/shard_map/concatenate | solution.py:736
  13.1 0.0 collective-permute-done.1.refs_9_
  13.1 2.5 %collective-permute-done.2.refs_10_ = f32[64,256]{1,0:T(8,128)S(1)} collective-permute-done((f32[64,256]{1,0:T(8,128)S(1)}, f32[64,256]{1,0:T(8,128)S(1)}, u32[]{:S(2)}, u32[]{:S(2)}) %collective-permute-start.2) | collective-permute-done | bytes 65568 | tf_op jit(solution)/shard_map/ppermute | solution.py:732
  15.6 6.3 %window.1 = (f32[7,3,352,128]{3,2,1,0:T(8,128)S(1)}, f32[3,352,128]{2,1,0:T(8,128)S(1)}, f32[3,352,128]{2,1,0:T(8,128)S(1)}, f32[3,352,128]{2,1,0:T(8,128)S(1)},...) custom-call(f32[2,8]{1,0:T(2,128)} %refs_0_.7, ...), custom_call_target="tpu_custom_call", output_to_operand_aliasing={{0}: (3, {}), {1}: (4, {}), {2}: (5, {}), {3}: (6, {}), {4}... | custom-call | tf_op jit(solution)/shard_map/window/pallas_call | solution.py:646
  21.9 0.6 %smooth_alone.1.a_ref = f32[320,256]{1,0:T(8,128)S(1)} custom-call(f32[3,352,128]{2,1,0:T(8,128)S(1)} %get-tuple-element.32.grad_ref), custom_call_target="tpu_custom_call" | custom-call | tf_op jit(solution)/shard_map/smooth_alone/pallas_call | solution.py:365
  22.5 2.5 %collective-permute-start.3 = (f32[320,256]{1,0:T(8,128)S(1)}, f32[320,256]{1,0:T(8,128)S(1)}, u32[]{:S(2)}, u32[]{:S(2)}) collective-permute-start(f32[320,256]{1,0:T(8,128)S(1)} %smooth_alone.1.a_ref), channel_id=1, source_target_pairs={{0,8},{8,0},{1,9},{9,1},{2,10},{10,2},{3,11},{11,3},{4,12},{12,4},... | collective-permute-start | bytes 983048 | tf_op jit(solution)/shard_map/ppermute | solution.py:742
  24.9 0.1 collective-permute-start.4
  25.0 1.2 %collective-permute-done.3.b_ref = f32[320,256]{1,0:T(8,128)S(1)} collective-permute-done((f32[320,256]{1,0:T(8,128)S(1)}, f32[320,256]{1,0:T(8,128)S(1)}, u32[]{:S(2)}, u32[]{:S(2)}) %collective-permute-start.3) | collective-permute-done | bytes 327712 | tf_op jit(solution)/shard_map/ppermute | solution.py:742
  26.2 0.8 %add_parts.2 = f32[320,256]{1,0:T(8,128)} custom-call(f32[320,256]{1,0:T(8,128)S(1)} %smooth_alone.1.a_ref, f32[320,256]{1,0:T(8,128)S(1)} %collective-permute-done.3.b_ref), custom_call_target="tpu_custom_call" | custom-call | tf_op jit(solution)/shard_map/add_parts/pallas_call | solution.py:686
  27.0 0.0 collective-permute-done.4.b_ref
  27.0 0.8 %add_parts.3 = f32[320,256]{1,0:T(8,128)} custom-call(f32[320,256]{1,0:T(8,128)S(1)} %get-tuple-element.33.a_ref, f32[320,256]{1,0:T(8,128)S(1)} %collective-permute-done.4.b_ref), custom_call_target="tpu_custom_call" | custom-call | tf_op jit(solution)/shard_map/add_parts/pallas_call | solution.py:686
Async XLA Ops:
  2.4 6.8 %collective-permute-start = (f32[160,128]{1,0:T(8,128)S(1)}, f32[160,128]{1,0:T(8,128)S(1)}, u32[]{:S(2)}, u32[]{:S(2)}) collective-permute-start(f32[160,128]{1,0:T(8,128)S(1)} %pack_columns.1), channel_id=1, source_target_pairs={{0,1},{1,0},{2,3},{3,2},{4,5},{5,4},{6,7},{7,6},{8,9},{9,8},{10,11... | collective-permute-start | bytes 245768 | tf_op jit(solution)/shard_map/ppermute | solution.py:728
  9.3 3.8 %collective-permute-start.1 = (f32[64,256]{1,0:T(8,128)S(1)}, f32[64,256]{1,0:T(8,128)S(1)}, u32[]{:S(2)}, u32[]{:S(2)}) collective-permute-start(f32[64,256]{1,0:T(8,128)S(1)} %get-tuple-element.30), channel_id=1, source_target_pairs={{0,2},{2,0},{4,6},{6,4},{1,3},{3,1},{5,7},{7,5},{8,10},{10,8},{12,... | collective-permute-start | bytes 196616 | tf_op jit(solution)/shard_map/ppermute | solution.py:732
  10.6 5.0 %collective-permute-start.2 = (f32[64,256]{1,0:T(8,128)S(1)}, f32[64,256]{1,0:T(8,128)S(1)}, u32[]{:S(2)}, u32[]{:S(2)}) collective-permute-start(f32[64,256]{1,0:T(8,128)S(1)} %get-tuple-element.31), channel_id=1, source_target_pairs={{2,4},{4,2},{3,5},{5,3},{10,12},{12,10},{11,13},{13,11},{18,20},{2... | collective-permute-start | bytes 196616 | tf_op jit(solution)/shard_map/ppermute | solution.py:732
  22.5 3.7 %collective-permute-start.3 = (f32[320,256]{1,0:T(8,128)S(1)}, f32[320,256]{1,0:T(8,128)S(1)}, u32[]{:S(2)}, u32[]{:S(2)}) collective-permute-start(f32[320,256]{1,0:T(8,128)S(1)} %smooth_alone.1.a_ref), channel_id=1, source_target_pairs={{0,8},{8,0},{1,9},{9,1},{2,10},{10,2},{3,11},{11,3},{4,12},{12,4},... | collective-permute-start | bytes 983048 | tf_op jit(solution)/shard_map/ppermute | solution.py:742
  24.9 2.0 %collective-permute-start.4 = (f32[320,256]{1,0:T(8,128)S(1)}, f32[320,256]{1,0:T(8,128)S(1)}, u32[]{:S(2)}, u32[]{:S(2)}) collective-permute-start(f32[320,256]{1,0:T(8,128)S(1)} %get-tuple-element.33.a_ref), channel_id=1, source_target_pairs={{0,8},{8,0},{1,9},{9,1},{2,10},{10,2},{3,11},{11,3},{4,12},{12,4},... | collective-permute-start | bytes 983048 | tf_op jit(solution)/shard_map/ppermute | solution.py:740
